TPU v7x, 256 devices: a whole 4x4x8 slice. The times are simulated.
256 devices in a mesh: section: 4 (over x), seq: 64 (over z, y, core).
Axes of the slice: x: 4, y: 4, z: 8, core: 2. Of those that a mesh axis runs over, the one named last changes fastest.
Arguments:
- queries: bfloat16 [4, 16384, 2048], P('section', 'seq'), may hold values from -24 to 24
- keys: bfloat16 [4, 16384, 1024], P('section', 'seq'), may hold values from -24 to 24
- values: bfloat16 [4, 16384, 1024], P('section', 'seq'), may hold values from -6 to 6
- segment_ids: int32 [16384], P('seq'), may hold values from 0 to 7, as said below
- positions: int32 [16384], P('seq'), may hold values from 0 to 8191, as said below
- residual_in: bfloat16 [16384, 2048], P('seq'), may hold values from -6 to 6
- post_gain: float32 [4, 2048], P('section'), may hold values from 0.1 to 1.9
Outputs:
- layer_out: bfloat16 [4, 16384, 2048], P('section', 'seq')
Inputs may be any that keep to these rules, and one draw needn't show every extreme that they name: `segment_ids`: never falling; each document holds 1 to 8192 tokens, one exactly 8192. `positions`: the token's index minus the index of the first token of its document.
All inputs are finite; a program needn't handle non-finite values.
Results may differ from a plain program's by a relative error of at most 0.011.
Values may be sent and summed in bfloat16 or wider, within the bound.
No kernel may reach another device: no remote copies, remote signals or barrier semaphores. Data moves between devices by JAX's collectives and lax.ppermute only.
A program may use at most 128 MiB of HBM per device.

v0:
```python
import functools
import math

import jax
import jax.numpy as jnp
from jax import lax
from jax.experimental import pallas as pl
from jax.experimental.pallas import tpu as pltpu
from jax.sharding import PartitionSpec as P

HQ = 8
HK = 4
HD = 256
WINDOW = 4096
ROWS = 256
PLANE = 2048
LAYERS = 4
HALF = HD // 2
VMEM = pltpu.VMEM
CAP = 50.0 / math.log(2.0)

SHARED_Y = [[z * 8 + y * 2 + c for y in range(4)] for z in range(8) for c in range(2)]
SHARED_XY = [
    [x * 64 + z * 8 + y * 2 + c for x in range(4) for y in range(4)]
    for z in range(8)
    for c in range(2)
]
NEXT_PLANE = [(i, i + 8) for i in range(56)]
OTHER_CORE = [(i, i ^ 1) for i in range(64)]


def vspec():
    return pl.BlockSpec(memory_space=VMEM)


def turned(x, cosine, sine):
    first = x[:, :HALF].astype(jnp.float32)
    second = x[:, HALF:].astype(jnp.float32)
    return (
        (first * cosine - second * sine).astype(jnp.bfloat16),
        (second * cosine + first * sine).astype(jnp.bfloat16),
    )


def rotate_kv_kernel(cos_ref, sin_ref, k_ref, v_ref, km_ref, vm_ref):
    for h in range(HK):
        a, b = turned(k_ref[:, h * HD : (h + 1) * HD], cos_ref[...], sin_ref[...])
        km_ref[h, :, :HALF] = a
        km_ref[h, :, HALF:] = b
        vm_ref[h] = v_ref[:, h * HD : (h + 1) * HD]


def rotate_q_kernel(cos_ref, sin_ref, place_ref, q_ref, qm_ref):
    for h in range(HQ):
        a, b = turned(q_ref[:, h * HD : (h + 1) * HD], cos_ref[...], sin_ref[...])
        rows = pl.ds((h % 2) * ROWS, ROWS)
        qm_ref[h // 2, rows, :HALF] = a
        qm_ref[h // 2, rows, HALF:] = b
    for h in range(HK):
        qm_ref[h, 2 * ROWS :] = place_ref[...]


def attend_kernel(back, q_ref, k_own, k_oth, v_own, v_oth, *refs):
    if back == 0:
        num, den = refs
    elif back == 1:
        num_in, den_in, num, den = refs
    else:
        num_in, den_in, out_ref = refs
    block = pl.program_id(0)
    device = lax.axis_index("seq")
    plane0 = device // 8 * PLANE
    core = lax.rem(device, 2)
    keys0 = plane0 - back * PLANE

    def sums(r):
        begin, end = {0: (0, r + 1), 1: (0, 4), 2: (r, 4)}[back]
        count = (end - begin) * ROWS
        query = q_ref[0, : 2 * ROWS]
        split = q_ref[0, 2 * ROWS :].astype(jnp.float32)
        place = (split[0:1] * 128.0 + split[1:2]).astype(jnp.int32)
        token = plane0 + r * 512 + core * ROWS + lax.broadcasted_iota(jnp.int32, (1, ROWS), 1)
        low = token - jnp.minimum(place, WINDOW - 1)
        low = jnp.transpose(jnp.broadcast_to(low, (HALF, ROWS)))
        low = jnp.concatenate([low, low], axis=0)
        low = jnp.concatenate([low] * (count // HALF), axis=1)
        col = lax.broadcasted_iota(jnp.int32, (1, count), 1)
        spread = col + lax.shift_right_logical(col, 8) * ROWS + begin * 512 + keys0
        total, added = None, None
        for k_ref, v_ref, side in ((k_own, v_own, core), (k_oth, v_oth, 1 - core)):
            score = lax.dot_general(
                query,
                k_ref[begin:end].reshape(count, HD),
                (((1,), (1,)), ((), ())),
                preferred_element_type=jnp.float32,
            )
            weight = jnp.exp2(jnp.tanh(score * (1.0 / 800.0)) * CAP)
            key = spread + side * ROWS
            ok = key >= low
            if back == 0:
                row = lax.broadcasted_iota(jnp.int32, (2 * ROWS, 1), 0) & (ROWS - 1)
                ok = ok & (key <= plane0 + r * 512 + core * ROWS + row)
            weight = jnp.where(ok, weight, 0.0)
            lanes = sum(weight[:, i * HALF : (i + 1) * HALF] for i in range(count // HALF))
            part = jnp.dot(
                weight.astype(jnp.bfloat16),
                v_ref[begin:end].reshape(count, HD),
                preferred_element_type=jnp.float32,
            )
            total = lanes if total is None else total + lanes
            added = part if added is None else added + part
        return total, added

    def finish(total, added):
        if back == 0:
            num[0] = added
            den[0] = total
        elif back == 1:
            num[0] = num_in[0] + added
            den[0] = den_in[0] + total
        else:
            whole = (num_in[0] + added) / jnp.sum(den_in[0] + total, axis=-1, keepdims=True)
            whole = whole.astype(jnp.bfloat16)
            for q in range(4):
                for h in range(2):
                    first = h * ROWS + q * 64
                    out_ref[q, 0, :, h * HD : (h + 1) * HD] = whole[first : first + 64]

    for r in range(4):

        @pl.when(block == r)
        def _():
            finish(*sums(r))


def attend(back, query, k_own, k_oth, v_own, v_oth, num, den):
    def step(*shape):
        return pl.BlockSpec((1,) + shape, lambda i: (i,) + (0,) * len(shape))

    whole = pl.BlockSpec(
        (4, ROWS, HD), lambda i: (0, 0, 0), pipeline_mode=pl.Buffered(1)
    )
    args = [query, k_own, k_oth, v_own, v_oth]
    in_specs = [step(2 * ROWS + 16, HD)] + [whole] * 4
    aliases = {}
    outs = [
        jax.ShapeDtypeStruct((4, 512, HD), jnp.float32),
        jax.ShapeDtypeStruct((4, 512, HALF), jnp.float32),
    ]
    out_specs = [step(512, HD), step(512, HALF)]
    if back:
        args += [num, den]
        in_specs += [step(512, HD), step(512, HALF)]
    if back == 1:
        aliases = {5: 0, 6: 1}
    if back == 2:
        outs = jax.ShapeDtypeStruct((4, 4, 64, 512), jnp.bfloat16)
        out_specs = pl.BlockSpec((4, 1, 64, 512), lambda i: (0, i, 0, 0))
    pairs = {0: 20, 1: 32, 2: 20}[back]
    return pl.pallas_call(
        functools.partial(attend_kernel, back),
        grid=(4,),
        out_shape=outs,
        in_specs=in_specs,
        out_specs=out_specs,
        input_output_aliases=aliases,
        compiler_params=pltpu.CompilerParams(
            vmem_limit_bytes=48 << 20, dimension_semantics=("arbitrary",)
        ),
        cost_estimate=pl.CostEstimate(
            flops=pairs * 512 * 256 * 256 * 4 * 3,
            bytes_accessed=8 << 20,
            transcendentals=pairs * 512 * 256 * 2,
        ),
        name="attend_%d" % back,
    )(*args)


def combine_kernel(got_ref, res_ref, g0_ref, g1_ref, g2_ref, g3_ref, out_ref, gain_ref):
    section = lax.axis_index("section")
    for r, ref in enumerate((g0_ref, g1_ref, g2_ref, g3_ref)):
        gain_ref[pl.ds(lax.rem(section + 4 - r, 4), 1), :] = ref[...]
    rows = pl.ds(pl.multiple_of(section * 64, 64), 64)
    running = res_ref[rows, :].astype(jnp.float32)
    running = [running[:, h * 512 : (h + 1) * 512] for h in range(4)]
    for layer in range(LAYERS):
        parts = [got_ref[layer * 4 + h].astype(jnp.float32) for h in range(4)]
        square = sum(jnp.sum(p * p, axis=-1, keepdims=True) for p in parts)
        norm = lax.rsqrt(square * (1.0 / (HQ * HD)) + 1e-06)
        for h in range(4):
            gain = gain_ref[layer : layer + 1, h * 512 : (h + 1) * 512]
            running[h] = running[h] + parts[h] * norm * gain
            out_ref[layer, :, h * 512 : (h + 1) * 512] = running[h].astype(jnp.bfloat16)


def per_device(queries, keys, values, segment_ids, positions, residual_in, post_gain):
    inverse = jnp.exp(-math.log(10000.0) * jnp.arange(HALF).astype(jnp.float32) / HALF)
    angle = positions.astype(jnp.float32)[:, None] * inverse[None, :]
    cosine = jnp.cos(angle)
    sine = jnp.sin(angle)
    split = jnp.stack([lax.shift_right_logical(positions, 7), positions & 127])
    places = jnp.concatenate([split, jnp.zeros((14, ROWS), jnp.int32)]).astype(jnp.bfloat16)

    def over_y(x):
        return lax.all_to_all(x, "seq", 0, 0, axis_index_groups=SHARED_Y)

    def onward(x):
        return lax.ppermute(x, "seq", NEXT_PLANE)

    def other(x):
        return lax.ppermute(x, "seq", OTHER_CORE)

    gains = [post_gain] + [
        lax.ppermute(post_gain, "section", [(i, (i + r) % 4) for i in range(4)])
        for r in (1, 2, 3)
    ]
    k_msg, v_msg = pl.pallas_call(
        rotate_kv_kernel,
        out_shape=[jax.ShapeDtypeStruct((HK, ROWS, HD), jnp.bfloat16)] * 2,
        in_specs=[vspec()] * 4,
        out_specs=[vspec()] * 2,
        name="rotate_kv",
    )(cosine, sine, keys[0], values[0])
    q_msg = pl.pallas_call(
        rotate_q_kernel,
        out_shape=jax.ShapeDtypeStruct((HK, 2 * ROWS + 16, HD), jnp.bfloat16),
        in_specs=[vspec()] * 4,
        out_specs=vspec(),
        name="rotate_q",
    )(cosine, sine, places, queries[0])

    k0 = over_y(k_msg)
    v0 = over_y(v_msg)
    query = over_y(q_msg)
    k1 = onward(k0)
    v1 = onward(v0)
    k2 = onward(k1)
    v2 = onward(v1)

    num, den = attend(0, query, k0, other(k0), v0, other(v0), None, None)
    num, den = attend(1, query, k1, other(k1), v1, other(v1), num, den)
    num, den, k2, v2 = lax.optimization_barrier((num, den, k2, v2))
    sent = attend(2, query, k2, other(k2), v2, other(v2), num, den)
    got = lax.all_to_all(
        sent.reshape(16, 64, 512), ("section", "seq"), 0, 0, axis_index_groups=SHARED_XY
    )
    back = pl.pallas_call(
        combine_kernel,
        out_shape=jax.ShapeDtypeStruct((LAYERS, 64, HQ * HD), jnp.bfloat16),
        in_specs=[vspec()] * 6,
        out_specs=vspec(),
        scratch_shapes=[VMEM((LAYERS, HQ * HD), jnp.float32)],
        name="combine",
    )(got, residual_in, *gains)
    mine = lax.all_to_all(back, "section", 0, 0)
    return mine.reshape(1, ROWS, HQ * HD)


def solution(mesh):
    placed = (
        P("section", "seq", None),
        P("section", "seq", None),
        P("section", "seq", None),
        P("seq"),
        P("seq"),
        P("seq", None),
        P("section", None),
    )
    return jax.shard_map(
        per_device, mesh=mesh, in_specs=placed, out_specs=P("section", "seq", None), check_vma=False
    )
```

profile of v0, /device:TPU:96, one launch (start us, length us, event | category | flops | bytes accessed | tf_op | source)
XLA Modules:
  0.0 143.9 jit_solution(2818826712738309532)
XLA Ops:
  0.0 0.8 shift-right-logical_convert_fusion
  0.8 1.3 multiply_sine_fusion
  2.0 2.5 %rotate_kv.1 = (bf16[4,256,256]{2,1,0:T(8,128)(2,1)}, bf16[4,256,256]{2,1,0:T(8,128)(2,1)}) custom-call(f32[256,128]{1,0:T(8,128)} %get-tuple-element.26.cos_ref, f32[256,128]{1,0:T(8,128)} %get-tuple-element.25.sin_ref, bf16[256,1024]{1,0:T(8,128)(2,1)} %bitcast.7, bf16[256,1024]{1,0:T(8,128)(2,1)} %bitcast.8), custom_call_target="tpu_custom_call" | custom-call | tf_op jit(solution)/shard_map/rotate_kv/pallas_call | solution.py:217
  4.5 13.9 %all_to_all.25.k_own = bf16[4,256,256]{2,1,0:T(8,128)(2,1)S(1)} all-to-all(bf16[4,256,256]{2,1,0:T(8,128)(2,1)} %get-tuple-element.15), channel_id=1, replica_groups={{0,2,4,6},{1,3,5,7},{8,10,12,14},{9,11,13,15},{16,18,20,22},{17,19,21,2..., dimensions={0} | all-to-all | bytes 1048576 | tf_op jit(solution)/shard_map/all_to_all | solution.py:205
  18.5 3.5 %all-to-all-start.2 = ((bf16[4,256,256]{2,1,0:T(8,128)(2,1)}), bf16[4,256,256]{2,1,0:T(8,128)(2,1)S(1)}, u32[]{:S(2)}, u32[]{:S(2)}) async-start(bf16[4,256,256]{2,1,0:T(8,128)(2,1)} %get-tuple-element.16), calls=%async_computation.2 | async-start | bytes 1048576 | tf_op jit(solution)/shard_map/all_to_all | solution.py:205
  22.0 0.1 pad.2.clone
  22.1 0.7 maximum_maximum_fusion.place_ref
  22.7 2.8 %rotate_q.1 = bf16[4,528,256]{2,1,0:T(8,128)(2,1)} custom-call(f32[256,128]{1,0:T(8,128)} %get-tuple-element.26.cos_ref, f32[256,128]{1,0:T(8,128)} %get-tuple-element.25.sin_ref, bf16[16,256]{1,0:T(8,128)(2,1)} %maximum_maximum_fusion.place_ref, bf16[256,2048]{1,0:T(8,128)(2,1)} %bitcast.6), custom_call_target="tpu_custom_call" | custom-call | tf_op jit(solution)/shard_map/rotate_q/pallas_call | solution.py:224
  25.5 5.0 %all-to-all-done.2.v_own = bf16[4,256,256]{2,1,0:T(8,128)(2,1)S(1)} async-done(((bf16[4,256,256]{2,1,0:T(8,128)(2,1)}), bf16[4,256,256]{2,1,0:T(8,128)(2,1)S(1)}, u32[]{:S(2)}, u32[]{:S(2)}) %all-to-all-start.2) | async-done | bytes 524320 | tf_op jit(solution)/shard_map/all_to_all | solution.py:205
  30.5 3.5 %all-to-all-start = ((bf16[4,528,256]{2,1,0:T(8,128)(2,1)}), bf16[4,528,256]{2,1,0:T(8,128)(2,1)S(1)}, u32[]{:S(2)}, u32[]{:S(2)}) async-start(bf16[4,528,256]{2,1,0:T(8,128)(2,1)} %rotate_q.1), calls=%async_computation | async-start | bytes 2162688 | tf_op jit(solution)/shard_map/all_to_all | solution.py:205
  34.0 5.0 %collective-permute-start = (bf16[4,256,256]{2,1,0:T(8,128)(2,1)S(1)}, bf16[4,256,256]{2,1,0:T(8,128)(2,1)S(1)}, u32[]{:S(2)}, u32[]{:S(2)}) collective-permute-start(bf16[4,256,256]{2,1,0:T(8,128)(2,1)S(1)} %all_to_all.25.k_own), channel_id=1, source_target_pairs={{0,8},{1,9},{2,10},{3,11},{4,12},{5,13},{6,14},{7,15},{8,16},{9,17... | collective-permute-start | bytes 1572872 | tf_op jit(solution)/shard_map/ppermute | solution.py:208
  39.0 2.9 %collective-permute-start.2 = (bf16[4,256,256]{2,1,0:T(8,128)(2,1)S(1)}, bf16[4,256,256]{2,1,0:T(8,128)(2,1)}, u32[]{:S(2)}, u32[]{:S(2)}) collective-permute-start(bf16[4,256,256]{2,1,0:T(8,128)(2,1)S(1)} %all-to-all-done.2.v_own), channel_id=1, source_target_pairs={{0,8},{1,9},{2,10},{3,11},{4,12},{5,13},{6,14},{7,15},{8,16},{9,17... | collective-permute-start | bytes 1572872 | tf_op jit(solution)/shard_map/ppermute | solution.py:208
  42.0 0.1 collective-permute-start.4
  42.1 0.5 collective-permute-start.5
  42.6 8.8 %collective-permute-done.k_own = bf16[4,256,256]{2,1,0:T(8,128)(2,1)S(1)} collective-permute-done((bf16[4,256,256]{2,1,0:T(8,128)(2,1)S(1)}, bf16[4,256,256]{2,1,0:T(8,128)(2,1)S(1)}, u32[]{:S(2)}, u32[]{:S(2)}) %collective-permute-start) | collective-permute-done | bytes 524320 | tf_op jit(solution)/shard_map/ppermute | solution.py:208
  51.4 0.0 collective-permute-start.1
  51.4 5.6 %collective-permute-start.6 = (bf16[4,256,256]{2,1,0:T(8,128)(2,1)S(1)}, bf16[4,256,256]{2,1,0:T(8,128)(2,1)S(1)}, u32[]{:S(2)}, u32[]{:S(2)}) collective-permute-start(bf16[4,256,256]{2,1,0:T(8,128)(2,1)S(1)} %collective-permute-done.k_own), channel_id=1, source_target_pairs={{0,8},{1,9},{2,10},{3,11},{4,12},{5,13},{6,14},{7,15},{8,16},{9,17... | collective-permute-start | bytes 1572872 | tf_op jit(solution)/shard_map/ppermute | solution.py:208
  57.0 3.4 %collective-permute-done.2.v_own = bf16[4,256,256]{2,1,0:T(8,128)(2,1)} collective-permute-done((bf16[4,256,256]{2,1,0:T(8,128)(2,1)S(1)}, bf16[4,256,256]{2,1,0:T(8,128)(2,1)}, u32[]{:S(2)}, u32[]{:S(2)}) %collective-permute-start.2) | collective-permute-done | bytes 524320 | tf_op jit(solution)/shard_map/ppermute | solution.py:208
  60.4 0.0 collective-permute-start.3
  60.4 0.0 collective-permute-done.4.k_oth
  60.4 0.8 copy-done
  61.2 5.7 %collective-permute-start.7 = (bf16[4,256,256]{2,1,0:T(8,128)(2,1)}, bf16[4,256,256]{2,1,0:T(8,128)(2,1)}, u32[]{:S(2)}, u32[]{:S(2)}) collective-permute-start(bf16[4,256,256]{2,1,0:T(8,128)(2,1)} %collective-permute-done.2.v_own), channel_id=1, source_target_pairs={{0,8},{1,9},{2,10},{3,11},{4,12},{5,13},{6,14},{7,15},{8,16},{9,17... | collective-permute-start | bytes 1572872 | tf_op jit(solution)/shard_map/ppermute | solution.py:208
  66.9 0.0 all-to-all-done.q_ref
  66.9 0.0 collective-permute-done.5.v_oth
  66.9 0.0 copy-start.1
  66.9 1.0 copy-done.1
  68.0 7.9 %attend_0.1 = (f32[4,512,256]{2,1,0:T(8,128)}, f32[4,512,128]{2,1,0:T(8,128)S(1)}) custom-call(bf16[4,528,256]{2,1,0:T(8,128)(2,1)S(1)} %all-to-all-done.q_ref, bf16[4,256,256]{2,1,0:T(8,128)(2,1)S(1)} %all_to_all.25.k_own, bf16[4,256,256]{2,1,0:T(8,128)(2,1)S(1)} %copy-done.1, bf16[4,256,256]{2,1,0:T(8,128)(2,1)S(1)} %all-to-all-done.2.v_own, ...), custom_call_target="tpu_custom_call" | custom-call | flops 8053063680 | bytes 8388608 | tf_op jit(solution)/shard_map/attend_0/pallas_call | solution.py:160
  75.8 10.8 %attend_1.1 = (f32[4,512,256]{2,1,0:T(8,128)}, f32[4,512,128]{2,1,0:T(8,128)S(1)}) custom-call(bf16[4,528,256]{2,1,0:T(8,128)(2,1)S(1)} %all-to-all-done.q_ref, bf16[4,256,256]{2,1,0:T(8,128)(2,1)S(1)} %collective-permute-done.k_own, bf16[4,256,256]{2,1,0:T(8,128)(2,1)} %collective-permute-done.1.k_oth, ...), custom_call_target="tpu_custom_call", output_to_operand_aliasing={{0}: (5, {}), {1}: (6, {})} | custom-call | flops 12884901888 | bytes 8388608 | tf_op jit(solution)/shard_map/attend_1/pallas_call | solution.py:160
  86.6 0.0 collective-permute-done.6.k_own
  86.6 0.0 collective-permute-done.7.v_own
  86.6 0.3 collective-permute-start.8
  86.9 0.3 collective-permute-start.9
  87.2 1.4 collective-permute-done.8.k_oth
  88.6 1.0 collective-permute-done.9.v_oth
  89.6 7.6 %attend_2.1 = bf16[4,4,64,512]{3,2,1,0:T(8,128)(2,1)} custom-call(bf16[4,528,256]{2,1,0:T(8,128)(2,1)S(1)} %all-to-all-done.q_ref, bf16[4,256,256]{2,1,0:T(8,128)(2,1)S(1)} %collective-permute-done.6.k_own, bf16[4,256,256]{2,1,0:T(8,128)(2,1)S(1)} %collective-permute-done.8.k_oth, bf16[4,256,256]{2,1,0:T(8,128)(2,1)} %collective-permute-done.7.v_own, ...), custom_call_target="tpu_custom_call" | custom-call | flops 8053063680 | bytes 8388608 | tf_op jit(solution)/shard_map/attend_2/pallas_call | solution.py:160
  97.2 6.9 %all-to-all-start.3 = ((bf16[16,64,512]{2,1,0:T(8,128)(2,1)}), bf16[16,64,512]{2,1,0:T(8,128)(2,1)S(1)}, u32[]{:S(2)}, u32[]{:S(2)}) async-start(bf16[16,64,512]{2,1,0:T(8,128)(2,1)} %bitcast.3), calls=%async_computation.3 | async-start | bytes 2097152 | tf_op jit(solution)/shard_map/all_to_all | solution.py:244
  104.1 2.0 %collective-permute-start.10 = (f32[1,2048]{1,0:T(1,128)S(1)}, f32[1,2048]{1,0:T(1,128)S(1)}, u32[]{:S(2)}, u32[]{:S(2)}) collective-permute-start(f32[1,2048]{1,0:T(1,128)S(1)} %copy-done.3), channel_id=1, source_target_pairs={{0,64},{64,128},{128,192},{192,0},{1,65},{65,129},{129,193},{193,1... | collective-permute-start | bytes 24584 | tf_op jit(solution)/shard_map/ppermute | solution.py:214
  106.1 2.7 %collective-permute-start.11 = (f32[1,2048]{1,0:T(1,128)S(1)}, f32[1,2048]{1,0:T(1,128)S(1)}, u32[]{:S(2)}, u32[]{:S(2)}) collective-permute-start(f32[1,2048]{1,0:T(1,128)S(1)} %copy-done.3), channel_id=1, source_target_pairs={{0,128},{64,192},{128,0},{192,64},{1,129},{65,193},{129,1},{193,65... | collective-permute-start | bytes 24584 | tf_op jit(solution)/shard_map/ppermute | solution.py:214
  108.8 1.5 %collective-permute-start.12 = (f32[1,2048]{1,0:T(1,128)S(1)}, f32[1,2048]{1,0:T(1,128)S(1)}, u32[]{:S(2)}, u32[]{:S(2)}) collective-permute-start(f32[1,2048]{1,0:T(1,128)S(1)} %copy-done.3), channel_id=1, source_target_pairs={{0,192},{64,0},{128,64},{192,128},{1,193},{65,1},{129,65},{193,129... | collective-permute-start | bytes 24584 | tf_op jit(solution)/shard_map/ppermute | solution.py:214
  110.3 7.2 %collective-permute-done.10.g1_ref = f32[1,2048]{1,0:T(1,128)S(1)} collective-permute-done((f32[1,2048]{1,0:T(1,128)S(1)}, f32[1,2048]{1,0:T(1,128)S(1)}, u32[]{:S(2)}, u32[]{:S(2)}) %collective-permute-start.10) | collective-permute-done | bytes 8224 | tf_op jit(solution)/shard_map/ppermute | solution.py:214
  117.5 2.4 %collective-permute-done.11.g2_ref = f32[1,2048]{1,0:T(1,128)S(1)} collective-permute-done((f32[1,2048]{1,0:T(1,128)S(1)}, f32[1,2048]{1,0:T(1,128)S(1)}, u32[]{:S(2)}, u32[]{:S(2)}) %collective-permute-start.11) | collective-permute-done | bytes 8224 | tf_op jit(solution)/shard_map/ppermute | solution.py:214
  119.9 0.0 collective-permute-done.12.g3_ref
  119.9 2.5 %all-to-all-done.3.got_ref = bf16[16,64,512]{2,1,0:T(8,128)(2,1)S(1)} async-done(((bf16[16,64,512]{2,1,0:T(8,128)(2,1)}), bf16[16,64,512]{2,1,0:T(8,128)(2,1)S(1)}, u32[]{:S(2)}, u32[]{:S(2)}) %all-to-all-start.3) | async-done | bytes 1048608 | tf_op jit(solution)/shard_map/all_to_all | solution.py:244
  122.3 0.0 copy-start.2
  122.3 1.0 copy-done.2
  123.3 3.1 %combine.1 = bf16[4,64,2048]{2,1,0:T(8,128)(2,1)} custom-call(bf16[16,64,512]{2,1,0:T(8,128)(2,1)} %copy-done.2, bf16[256,2048]{1,0:T(8,128)(2,1)} %res_ref.1, f32[1,2048]{1,0:T(1,128)} %g0_ref.1, f32[1,2048]{1,0:T(1,128)} %copy-done.4, f32[1,2048]{1,0:T(1,128)} %copy-done.5, f32[1,2048]{1,0:T(1,128)} %copy-done.6), custom_call_target="tpu_custom_call" | custom-call | tf_op jit(solution)/shard_map/combine/pallas_call | solution.py:247
  126.4 16.6 %all_to_all.26 = bf16[4,64,2048]{2,1,0:T(8,128)(2,1)S(1)} all-to-all(bf16[4,64,2048]{2,1,0:T(8,128)(2,1)} %combine.1), channel_id=1, replica_groups=mesh['section'=4,'seq'=64] {'section'}, dimensions={0} | all-to-all | bytes 2097152 | tf_op jit(solution)/shard_map/all_to_all | solution.py:255
  142.9 1.0 copy.12
  (15 shorter events, 0.0 us)
Async XLA Ops:
  18.5 12.0 %all-to-all-start.2 = ((bf16[4,256,256]{2,1,0:T(8,128)(2,1)}), bf16[4,256,256]{2,1,0:T(8,128)(2,1)S(1)}, u32[]{:S(2)}, u32[]{:S(2)}) async-start(bf16[4,256,256]{2,1,0:T(8,128)(2,1)} %get-tuple-element.16), calls=%async_computation.2 | async-start | bytes 1048576 | tf_op jit(solution)/shard_map/all_to_all | solution.py:205
  30.5 36.4 %all-to-all-start = ((bf16[4,528,256]{2,1,0:T(8,128)(2,1)}), bf16[4,528,256]{2,1,0:T(8,128)(2,1)S(1)}, u32[]{:S(2)}, u32[]{:S(2)}) async-start(bf16[4,528,256]{2,1,0:T(8,128)(2,1)} %rotate_q.1), calls=%async_computation | async-start | bytes 2162688 | tf_op jit(solution)/shard_map/all_to_all | solution.py:205
  34.0 17.4 %collective-permute-start = (bf16[4,256,256]{2,1,0:T(8,128)(2,1)S(1)}, bf16[4,256,256]{2,1,0:T(8,128)(2,1)S(1)}, u32[]{:S(2)}, u32[]{:S(2)}) collective-permute-start(bf16[4,256,256]{2,1,0:T(8,128)(2,1)S(1)} %all_to_all.25.k_own), channel_id=1, source_target_pairs={{0,8},{1,9},{2,10},{3,11},{4,12},{5,13},{6,14},{7,15},{8,16},{9,17... | collective-permute-start | bytes 1572872 | tf_op jit(solution)/shard_map/ppermute | solution.py:208
  39.0 21.4 %collective-permute-start.2 = (bf16[4,256,256]{2,1,0:T(8,128)(2,1)S(1)}, bf16[4,256,256]{2,1,0:T(8,128)(2,1)}, u32[]{:S(2)}, u32[]{:S(2)}) collective-permute-start(bf16[4,256,256]{2,1,0:T(8,128)(2,1)S(1)} %all-to-all-done.2.v_own), channel_id=1, source_target_pairs={{0,8},{1,9},{2,10},{3,11},{4,12},{5,13},{6,14},{7,15},{8,16},{9,17... | collective-permute-start | bytes 1572872 | tf_op jit(solution)/shard_map/ppermute | solution.py:208
  42.0 18.4 %collective-permute-start.4 = (bf16[4,256,256]{2,1,0:T(8,128)(2,1)S(1)}, bf16[4,256,256]{2,1,0:T(8,128)(2,1)S(1)}, u32[]{:S(2)}, u32[]{:S(2)}) collective-permute-start(bf16[4,256,256]{2,1,0:T(8,128)(2,1)S(1)} %all_to_all.25.k_own), channel_id=1, source_target_pairs={{0,1},{1,0},{2,3},{3,2},{4,5},{5,4},{6,7},{7,6},{8,9},{9,8},{10,11... | collective-permute-start | bytes 1572872 | tf_op jit(solution)/shard_map/ppermute | solution.py:211
  42.1 24.8 %collective-permute-start.5 = (bf16[4,256,256]{2,1,0:T(8,128)(2,1)S(1)}, bf16[4,256,256]{2,1,0:T(8,128)(2,1)}, u32[]{:S(2)}, u32[]{:S(2)}) collective-permute-start(bf16[4,256,256]{2,1,0:T(8,128)(2,1)S(1)} %all-to-all-done.2.v_own), channel_id=1, source_target_pairs={{0,1},{1,0},{2,3},{3,2},{4,5},{5,4},{6,7},{7,6},{8,9},{9,8},{10,11... | collective-permute-start | bytes 1572872 | tf_op jit(solution)/shard_map/ppermute | solution.py:211
  51.4 24.4 %collective-permute-start.1 = (bf16[4,256,256]{2,1,0:T(8,128)(2,1)S(1)}, bf16[4,256,256]{2,1,0:T(8,128)(2,1)}, u32[]{:S(2)}, u32[]{:S(2)}) collective-permute-start(bf16[4,256,256]{2,1,0:T(8,128)(2,1)S(1)} %collective-permute-done.k_own), channel_id=1, source_target_pairs={{0,1},{1,0},{2,3},{3,2},{4,5},{5,4},{6,7},{7,6},{8,9},{9,8},{10,11... | collective-permute-start | bytes 1572872 | tf_op jit(solution)/shard_map/ppermute | solution.py:211
  51.4 35.2 %collective-permute-start.6 = (bf16[4,256,256]{2,1,0:T(8,128)(2,1)S(1)}, bf16[4,256,256]{2,1,0:T(8,128)(2,1)S(1)}, u32[]{:S(2)}, u32[]{:S(2)}) collective-permute-start(bf16[4,256,256]{2,1,0:T(8,128)(2,1)S(1)} %collective-permute-done.k_own), channel_id=1, source_target_pairs={{0,8},{1,9},{2,10},{3,11},{4,12},{5,13},{6,14},{7,15},{8,16},{9,17... | collective-permute-start | bytes 1572872 | tf_op jit(solution)/shard_map/ppermute | solution.py:208
  60.4 15.4 %collective-permute-start.3 = (bf16[4,256,256]{2,1,0:T(8,128)(2,1)}, bf16[4,256,256]{2,1,0:T(8,128)(2,1)}, u32[]{:S(2)}, u32[]{:S(2)}) collective-permute-start(bf16[4,256,256]{2,1,0:T(8,128)(2,1)} %collective-permute-done.2.v_own), channel_id=1, source_target_pairs={{0,1},{1,0},{2,3},{3,2},{4,5},{5,4},{6,7},{7,6},{8,9},{9,8},{10,11... | collective-permute-start | bytes 1572872 | tf_op jit(solution)/shard_map/ppermute | solution.py:211
  60.4 0.8 copy-start
  61.2 25.4 %collective-permute-start.7 = (bf16[4,256,256]{2,1,0:T(8,128)(2,1)}, bf16[4,256,256]{2,1,0:T(8,128)(2,1)}, u32[]{:S(2)}, u32[]{:S(2)}) collective-permute-start(bf16[4,256,256]{2,1,0:T(8,128)(2,1)} %collective-permute-done.2.v_own), channel_id=1, source_target_pairs={{0,8},{1,9},{2,10},{3,11},{4,12},{5,13},{6,14},{7,15},{8,16},{9,17... | collective-permute-start | bytes 1572872 | tf_op jit(solution)/shard_map/ppermute | solution.py:208
  66.9 1.0 copy-start.1
  86.6 2.0 %collective-permute-start.8 = (bf16[4,256,256]{2,1,0:T(8,128)(2,1)S(1)}, bf16[4,256,256]{2,1,0:T(8,128)(2,1)S(1)}, u32[]{:S(2)}, u32[]{:S(2)}) collective-permute-start(bf16[4,256,256]{2,1,0:T(8,128)(2,1)S(1)} %collective-permute-done.6.k_own), channel_id=1, source_target_pairs={{0,1},{1,0},{2,3},{3,2},{4,5},{5,4},{6,7},{7,6},{8,9},{9,8},{10,11... | collective-permute-start | bytes 1572872 | tf_op jit(solution)/shard_map/ppermute | solution.py:211
  86.9 2.6 %collective-permute-start.9 = (bf16[4,256,256]{2,1,0:T(8,128)(2,1)}, bf16[4,256,256]{2,1,0:T(8,128)(2,1)S(1)}, u32[]{:S(2)}, u32[]{:S(2)}) collective-permute-start(bf16[4,256,256]{2,1,0:T(8,128)(2,1)} %collective-permute-done.7.v_own), channel_id=1, source_target_pairs={{0,1},{1,0},{2,3},{3,2},{4,5},{5,4},{6,7},{7,6},{8,9},{9,8},{10,11... | collective-permute-start | bytes 1572872 | tf_op jit(solution)/shard_map/ppermute | solution.py:211
  97.2 6.9 %copy-start.3 = (f32[1,2048]{1,0:T(1,128)S(1)}, f32[1,2048]{1,0:T(1,128)}, u32[]{:S(2)}) copy-start(f32[1,2048]{1,0:T(1,128)} %g0_ref.1) | copy-start | bytes 24580
  97.2 25.1 %all-to-all-start.3 = ((bf16[16,64,512]{2,1,0:T(8,128)(2,1)}), bf16[16,64,512]{2,1,0:T(8,128)(2,1)S(1)}, u32[]{:S(2)}, u32[]{:S(2)}) async-start(bf16[16,64,512]{2,1,0:T(8,128)(2,1)} %bitcast.3), calls=%async_computation.3 | async-start | bytes 2097152 | tf_op jit(solution)/shard_map/all_to_all | solution.py:244
  104.1 13.4 %collective-permute-start.10 = (f32[1,2048]{1,0:T(1,128)S(1)}, f32[1,2048]{1,0:T(1,128)S(1)}, u32[]{:S(2)}, u32[]{:S(2)}) collective-permute-start(f32[1,2048]{1,0:T(1,128)S(1)} %copy-done.3), channel_id=1, source_target_pairs={{0,64},{64,128},{128,192},{192,0},{1,65},{65,129},{129,193},{193,1... | collective-permute-start | bytes 24584 | tf_op jit(solution)/shard_map/ppermute | solution.py:214
  106.1 13.7 %collective-permute-start.11 = (f32[1,2048]{1,0:T(1,128)S(1)}, f32[1,2048]{1,0:T(1,128)S(1)}, u32[]{:S(2)}, u32[]{:S(2)}) collective-permute-start(f32[1,2048]{1,0:T(1,128)S(1)} %copy-done.3), channel_id=1, source_target_pairs={{0,128},{64,192},{128,0},{192,64},{1,129},{65,193},{129,1},{193,65... | collective-permute-start | bytes 24584 | tf_op jit(solution)/shard_map/ppermute | solution.py:214
  108.8 11.1 %collective-permute-start.12 = (f32[1,2048]{1,0:T(1,128)S(1)}, f32[1,2048]{1,0:T(1,128)S(1)}, u32[]{:S(2)}, u32[]{:S(2)}) collective-permute-start(f32[1,2048]{1,0:T(1,128)S(1)} %copy-done.3), channel_id=1, source_target_pairs={{0,192},{64,0},{128,64},{192,128},{1,193},{65,1},{129,65},{193,129... | collective-permute-start | bytes 24584 | tf_op jit(solution)/shard_map/ppermute | solution.py:214
  117.5 4.8 %copy-start.4 = (f32[1,2048]{1,0:T(1,128)}, f32[1,2048]{1,0:T(1,128)S(1)}, u32[]{:S(2)}) copy-start(f32[1,2048]{1,0:T(1,128)S(1)} %collective-permute-done.10.g1_ref) | copy-start | bytes 24580
  119.9 2.5 %copy-start.5 = (f32[1,2048]{1,0:T(1,128)}, f32[1,2048]{1,0:T(1,128)S(1)}, u32[]{:S(2)}) copy-start(f32[1,2048]{1,0:T(1,128)S(1)} %collective-permute-done.11.g2_ref) | copy-start | bytes 24580
  119.9 2.5 %copy-start.6 = (f32[1,2048]{1,0:T(1,128)}, f32[1,2048]{1,0:T(1,128)S(1)}, u32[]{:S(2)}) copy-start(f32[1,2048]{1,0:T(1,128)S(1)} %collective-permute-done.12.g3_ref) | copy-start | bytes 24580
  122.3 1.0 copy-start.2
where the time goes:
time: 145 us; the launch traced here: 144 us
  starting transfers between devices  40.4 us (28%)
  Pallas kernels  34.6 us (24%)
  waiting for transfers between devices  31.6 us (22%)
  blocking collectives  30.5 us (21%)
  local copies, waits for them, and re-layouts  3.87 us (3%)
  other arithmetic  2.72 us (2%)
    pallas_call x3, Pallas kernels, attend(): pl.pallas_call(functools.partial(attend_kernel, back), grid=(4,), out_sha...  26.3 us
    ppermute x4, starting transfers between devices, onward(): return lax.ppermute(x, 'seq', NEXT_PLANE)  19.2 us
    all_to_all x1, blocking collectives, per_device(): mine = lax.all_to_all(back, 'section', 0, 0)  16.6 us
    all_to_all x1, blocking collectives, over_y(): return lax.all_to_all(x, 'seq', 0, 0, axis_index_groups=SHARED_Y)  13.9 us
    ppermute x4, waiting for transfers between devices, onward(): return lax.ppermute(x, 'seq', NEXT_PLANE)  12.3 us
    ppermute x3, waiting for transfers between devices, per_device(): lax.ppermute(post_gain, 'section', [(i, (i + r) % 4) for i in range(4)])  9.59 us
    all_to_all x2, starting transfers between devices, over_y(): return lax.all_to_all(x, 'seq', 0, 0, axis_index_groups=SHARED_Y)  6.99 us
    all_to_all x1, starting transfers between devices, per_device(): lax.all_to_all(sent.reshape(16, 64, 512), ('section', 'seq'), 0, 0, axis_...  6.89 us
  transfers between devices with their start and end apart: 16, of which 8 were waited for; matrix products, arithmetic and copies ran while one was open for 1% of the time, Pallas kernels for 15%

commit v1 on v0

--- a/solution.py
+++ b/solution.py
@@ -42,12 +42,16 @@
     )
 
 
-def rotate_kv_kernel(cos_ref, sin_ref, k_ref, v_ref, km_ref, vm_ref):
+def split_v_kernel(v_ref, vm_ref):
+    for h in range(HK):
+        vm_ref[h] = v_ref[:, h * HD : (h + 1) * HD]
+
+
+def rotate_k_kernel(cos_ref, sin_ref, k_ref, km_ref):
     for h in range(HK):
         a, b = turned(k_ref[:, h * HD : (h + 1) * HD], cos_ref[...], sin_ref[...])
         km_ref[h, :, :HALF] = a
         km_ref[h, :, HALF:] = b
-        vm_ref[h] = v_ref[:, h * HD : (h + 1) * HD]
 
 
 def rotate_q_kernel(cos_ref, sin_ref, place_ref, q_ref, qm_ref):
@@ -67,17 +71,15 @@
         num_in, den_in, num, den = refs
     else:
         num_in, den_in, out_ref = refs
-    block = pl.program_id(0)
     device = lax.axis_index("seq")
     plane0 = device // 8 * PLANE
     core = lax.rem(device, 2)
     keys0 = plane0 - back * PLANE
-
-    def sums(r):
+    for r in range(4):
         begin, end = {0: (0, r + 1), 1: (0, 4), 2: (r, 4)}[back]
         count = (end - begin) * ROWS
-        query = q_ref[0, : 2 * ROWS]
-        split = q_ref[0, 2 * ROWS :].astype(jnp.float32)
+        query = q_ref[r, : 2 * ROWS]
+        split = q_ref[r, 2 * ROWS :].astype(jnp.float32)
         place = (split[0:1] * 128.0 + split[1:2]).astype(jnp.int32)
         token = plane0 + r * 512 + core * ROWS + lax.broadcasted_iota(jnp.int32, (1, ROWS), 1)
         low = token - jnp.minimum(place, WINDOW - 1)
@@ -109,66 +111,46 @@
             )
             total = lanes if total is None else total + lanes
             added = part if added is None else added + part
-        return total, added
-
-    def finish(total, added):
         if back == 0:
-            num[0] = added
-            den[0] = total
+            num[r] = added
+            den[r] = total
         elif back == 1:
-            num[0] = num_in[0] + added
-            den[0] = den_in[0] + total
+            num[r] = num_in[r] + added
+            den[r] = den_in[r] + total
         else:
-            whole = (num_in[0] + added) / jnp.sum(den_in[0] + total, axis=-1, keepdims=True)
-            whole = whole.astype(jnp.bfloat16)
+            scale = 1.0 / jnp.sum(den_in[r] + total, axis=-1, keepdims=True)
+            whole = ((num_in[r] + added) * scale).astype(jnp.bfloat16)
             for q in range(4):
                 for h in range(2):
                     first = h * ROWS + q * 64
-                    out_ref[q, 0, :, h * HD : (h + 1) * HD] = whole[first : first + 64]
-
-    for r in range(4):
-
-        @pl.when(block == r)
-        def _():
-            finish(*sums(r))
+                    out_ref[q, r, :, h * HD : (h + 1) * HD] = whole[first : first + 64]
 
 
 def attend(back, query, k_own, k_oth, v_own, v_oth, num, den):
-    def step(*shape):
-        return pl.BlockSpec((1,) + shape, lambda i: (i,) + (0,) * len(shape))
-
-    whole = pl.BlockSpec(
-        (4, ROWS, HD), lambda i: (0, 0, 0), pipeline_mode=pl.Buffered(1)
-    )
     args = [query, k_own, k_oth, v_own, v_oth]
-    in_specs = [step(2 * ROWS + 16, HD)] + [whole] * 4
     aliases = {}
     outs = [
         jax.ShapeDtypeStruct((4, 512, HD), jnp.float32),
         jax.ShapeDtypeStruct((4, 512, HALF), jnp.float32),
     ]
-    out_specs = [step(512, HD), step(512, HALF)]
+    out_specs = [vspec(), vspec()]
     if back:
         args += [num, den]
-        in_specs += [step(512, HD), step(512, HALF)]
     if back == 1:
         aliases = {5: 0, 6: 1}
     if back == 2:
         outs = jax.ShapeDtypeStruct((4, 4, 64, 512), jnp.bfloat16)
-        out_specs = pl.BlockSpec((4, 1, 64, 512), lambda i: (0, i, 0, 0))
+        out_specs = vspec()
     pairs = {0: 20, 1: 32, 2: 20}[back]
     return pl.pallas_call(
         functools.partial(attend_kernel, back),
-        grid=(4,),
         out_shape=outs,
-        in_specs=in_specs,
+        in_specs=[vspec()] * len(args),
         out_specs=out_specs,
         input_output_aliases=aliases,
-        compiler_params=pltpu.CompilerParams(
-            vmem_limit_bytes=48 << 20, dimension_semantics=("arbitrary",)
-        ),
+        compiler_params=pltpu.CompilerParams(vmem_limit_bytes=40 << 20),
         cost_estimate=pl.CostEstimate(
-            flops=pairs * 512 * 256 * 256 * 4 * 3,
+            flops=pairs * 512 * 256 * 256 * 4 * 2,
             bytes_accessed=8 << 20,
             transcendentals=pairs * 512 * 256 * 2,
         ),
@@ -214,13 +196,20 @@
         lax.ppermute(post_gain, "section", [(i, (i + r) % 4) for i in range(4)])
         for r in (1, 2, 3)
     ]
-    k_msg, v_msg = pl.pallas_call(
-        rotate_kv_kernel,
-        out_shape=[jax.ShapeDtypeStruct((HK, ROWS, HD), jnp.bfloat16)] * 2,
-        in_specs=[vspec()] * 4,
-        out_specs=[vspec()] * 2,
-        name="rotate_kv",
-    )(cosine, sine, keys[0], values[0])
+    v_msg = pl.pallas_call(
+        split_v_kernel,
+        out_shape=jax.ShapeDtypeStruct((HK, ROWS, HD), jnp.bfloat16),
+        in_specs=[vspec()],
+        out_specs=vspec(),
+        name="split_v",
+    )(values[0])
+    k_msg = pl.pallas_call(
+        rotate_k_kernel,
+        out_shape=jax.ShapeDtypeStruct((HK, ROWS, HD), jnp.bfloat16),
+        in_specs=[vspec()] * 3,
+        out_specs=vspec(),
+        name="rotate_k",
+    )(cosine, sine, keys[0])
     q_msg = pl.pallas_call(
         rotate_q_kernel,
         out_shape=jax.ShapeDtypeStruct((HK, 2 * ROWS + 16, HD), jnp.bfloat16),
@@ -229,13 +218,15 @@
         name="rotate_q",
     )(cosine, sine, places, queries[0])
 
+    v0 = over_y(v_msg)
+    v0, k_msg = lax.optimization_barrier((v0, k_msg))
+    v1 = onward(v0)
     k0 = over_y(k_msg)
-    v0 = over_y(v_msg)
+    k1 = onward(k0)
+    v1, q_msg = lax.optimization_barrier((v1, q_msg))
     query = over_y(q_msg)
-    k1 = onward(k0)
-    v1 = onward(v0)
+    v2 = onward(v1)
     k2 = onward(k1)
-    v2 = onward(v1)
 
     num, den = attend(0, query, k0, other(k0), v0, other(v0), None, None)
     num, den = attend(1, query, k1, other(k1), v1, other(v1), num, den)

time: 145 us -> 134 us (0.924)
  blocking collectives: 30.5 us -> 16.1 us
  waiting for transfers between devices: 31.6 us -> 38.4 us
  Pallas kernels: 34.6 us -> 28.2 us
  starting transfers between devices: 40.4 us -> 42.3 us
  local copies, waits for them, and re-layouts: 3.87 us -> 5.7 us
    all_to_all x1 -> x0, blocking collectives: 13.9 us -> none  [over_y(): return lax.all_to_all(x, 'seq', 0, 0, axis_index_groups=SHARED_Y)]
    pallas_call x4 -> x5, Pallas kernels: 28.7 us -> 22.3 us  [the longest x3 18.2 us: attend(): pl.pallas_call(functools.partial(attend_kernel, back), out_shape=outs, in...]
    all_to_all x2 -> x3, starting transfers between devices: 6.99 us -> 11.5 us  [over_y(): return lax.all_to_all(x, 'seq', 0, 0, axis_index_groups=SHARED_Y)]
    ppermute x4, waiting for transfers between devices: 12.3 us -> 16.2 us  [onward(): return lax.ppermute(x, 'seq', NEXT_PLANE)]
    all_to_all x2 -> x3, waiting for transfers between devices: 4.96 us -> 7.9 us  [over_y(): return lax.all_to_all(x, 'seq', 0, 0, axis_index_groups=SHARED_Y)]
    ppermute x4, starting transfers between devices: 19.2 us -> 16.3 us  [onward(): return lax.ppermute(x, 'seq', NEXT_PLANE)]
    unnamed x15 -> x21, local copies, waits for them, and re-layouts: 3.78 us -> 5.61 us
  transfers between devices with their start and end apart: 16 -> 17, of which waited for: 8 -> 10; matrix products, arithmetic and copies ran while one was open for 1% -> 2% of each run, Pallas kernels for 15% -> 13%
where the time goes in v1:
time: 134 us; the launch traced here: 133 us
  starting transfers between devices  42.3 us (32%)
  waiting for transfers between devices  38.4 us (29%)
  Pallas kernels  28.2 us (21%)
  blocking collectives  16.1 us (12%)
  local copies, waits for them, and re-layouts  5.7 us (4%)
  other arithmetic  1.92 us (1%)
    pallas_call x3, Pallas kernels, attend(): pl.pallas_call(functools.partial(attend_kernel, back), out_shape=outs, in...  18.2 us
    ppermute x4, starting transfers between devices, onward(): return lax.ppermute(x, 'seq', NEXT_PLANE)  16.3 us
    ppermute x4, waiting for transfers between devices, onward(): return lax.ppermute(x, 'seq', NEXT_PLANE)  16.2 us
    all_to_all x1, blocking collectives, per_device(): mine = lax.all_to_all(back, 'section', 0, 0)  16.1 us
    all_to_all x3, starting transfers between devices, over_y(): return lax.all_to_all(x, 'seq', 0, 0, axis_index_groups=SHARED_Y)  11.5 us
    ppermute x3, waiting for transfers between devices, per_device(): lax.ppermute(post_gain, 'section', [(i, (i + r) % 4) for i in range(4)])  9.49 us
    all_to_all x3, waiting for transfers between devices, over_y(): return lax.all_to_all(x, 'seq', 0, 0, axis_index_groups=SHARED_Y)  7.9 us
    all_to_all x1, starting transfers between devices, per_device(): lax.all_to_all(sent.reshape(16, 64, 512), ('section', 'seq'), 0, 0, axis_...  7.17 us
  transfers between devices with their start and end apart: 17, of which 10 were waited for; matrix products, arithmetic and copies ran while one was open for 2% of the time, Pallas kernels for 13%

profile of v1, /device:TPU:96, one launch (start us, length us, event | category | flops | bytes accessed | tf_op | source)
XLA Modules:
  0.0 132.8 jit_solution(17145141550138913547)
XLA Ops:
  0.0 1.9 %split_v.1 = bf16[4,256,256]{2,1,0:T(8,128)(2,1)} custom-call(bf16[256,1024]{1,0:T(8,128)(2,1)} %bitcast.7), custom_call_target="tpu_custom_call" | custom-call | tf_op jit(solution)/shard_map/split_v/pallas_call | solution.py:199
  1.9 4.5 %all-to-all-start = ((bf16[4,256,256]{2,1,0:T(8,128)(2,1)}), bf16[4,256,256]{2,1,0:T(8,128)(2,1)S(1)}, u32[]{:S(2)}, u32[]{:S(2)}) async-start(bf16[4,256,256]{2,1,0:T(8,128)(2,1)} %split_v.1), calls=%async_computation | async-start | bytes 1048576 | tf_op jit(solution)/shard_map/all_to_all | solution.py:187
  6.4 1.2 multiply_sine_fusion
  7.6 2.2 %rotate_k.1 = bf16[4,256,256]{2,1,0:T(8,128)(2,1)} custom-call(f32[256,128]{1,0:T(8,128)} %get-tuple-element.30.cos_ref, f32[256,128]{1,0:T(8,128)} %get-tuple-element.29.sin_ref, bf16[256,1024]{1,0:T(8,128)(2,1)} %bitcast.8), custom_call_target="tpu_custom_call" | custom-call | tf_op jit(solution)/shard_map/rotate_k/pallas_call | solution.py:206
  9.8 6.0 %all-to-all-done.v_own = bf16[4,256,256]{2,1,0:T(8,128)(2,1)S(1)} async-done(((bf16[4,256,256]{2,1,0:T(8,128)(2,1)}), bf16[4,256,256]{2,1,0:T(8,128)(2,1)S(1)}, u32[]{:S(2)}, u32[]{:S(2)}) %all-to-all-start) | async-done | bytes 524320 | tf_op jit(solution)/shard_map/all_to_all | solution.py:187
  15.8 5.0 %collective-permute-start = (bf16[4,256,256]{2,1,0:T(8,128)(2,1)S(1)}, bf16[4,256,256]{2,1,0:T(8,128)(2,1)S(1)}, u32[]{:S(2)}, u32[]{:S(2)}) collective-permute-start(bf16[4,256,256]{2,1,0:T(8,128)(2,1)S(1)} %all-to-all-done.v_own), channel_id=1, source_target_pairs={{0,8},{1,9},{2,10},{3,11},{4,12},{5,13},{6,14},{7,15},{8,16},{9,17... | collective-permute-start | bytes 1572872 | tf_op jit(solution)/shard_map/ppermute | solution.py:190
  20.9 3.5 %all-to-all-start.2 = ((bf16[4,256,256]{2,1,0:T(8,128)(2,1)}), bf16[4,256,256]{2,1,0:T(8,128)(2,1)S(1)}, u32[]{:S(2)}, u32[]{:S(2)}) async-start(bf16[4,256,256]{2,1,0:T(8,128)(2,1)} %rotate_k.1), calls=%async_computation.2 | async-start | bytes 1048576 | tf_op jit(solution)/shard_map/all_to_all | solution.py:187
  24.4 0.1 pad.2.clone
  24.5 0.7 maximum_maximum_fusion.place_ref
  25.1 2.8 %rotate_q.1 = bf16[4,528,256]{2,1,0:T(8,128)(2,1)} custom-call(f32[256,128]{1,0:T(8,128)} %get-tuple-element.30.cos_ref, f32[256,128]{1,0:T(8,128)} %get-tuple-element.29.sin_ref, bf16[16,256]{1,0:T(8,128)(2,1)} %maximum_maximum_fusion.place_ref, bf16[256,2048]{1,0:T(8,128)(2,1)} %bitcast.6), custom_call_target="tpu_custom_call" | custom-call | tf_op jit(solution)/shard_map/rotate_q/pallas_call | solution.py:213
  27.9 2.6 %collective-permute-done.v_own = bf16[4,256,256]{2,1,0:T(8,128)(2,1)S(1)} collective-permute-done((bf16[4,256,256]{2,1,0:T(8,128)(2,1)S(1)}, bf16[4,256,256]{2,1,0:T(8,128)(2,1)S(1)}, u32[]{:S(2)}, u32[]{:S(2)}) %collective-permute-start) | collective-permute-done | bytes 524320 | tf_op jit(solution)/shard_map/ppermute | solution.py:190
  30.5 1.9 %all-to-all-done.2.k_own = bf16[4,256,256]{2,1,0:T(8,128)(2,1)S(1)} async-done(((bf16[4,256,256]{2,1,0:T(8,128)(2,1)}), bf16[4,256,256]{2,1,0:T(8,128)(2,1)S(1)}, u32[]{:S(2)}, u32[]{:S(2)}) %all-to-all-start.2) | async-done | bytes 524320 | tf_op jit(solution)/shard_map/all_to_all | solution.py:187
  32.4 3.5 %all-to-all-start.1 = ((bf16[4,528,256]{2,1,0:T(8,128)(2,1)}), bf16[4,528,256]{2,1,0:T(8,128)(2,1)S(1)}, u32[]{:S(2)}, u32[]{:S(2)}) async-start(bf16[4,528,256]{2,1,0:T(8,128)(2,1)} %rotate_q.1), calls=%async_computation.1 | async-start | bytes 2162688 | tf_op jit(solution)/shard_map/all_to_all | solution.py:187
  35.9 3.7 %collective-permute-start.1 = (bf16[4,256,256]{2,1,0:T(8,128)(2,1)S(1)}, bf16[4,256,256]{2,1,0:T(8,128)(2,1)S(1)}, u32[]{:S(2)}, u32[]{:S(2)}) collective-permute-start(bf16[4,256,256]{2,1,0:T(8,128)(2,1)S(1)} %all-to-all-done.2.k_own), channel_id=1, source_target_pairs={{0,8},{1,9},{2,10},{3,11},{4,12},{5,13},{6,14},{7,15},{8,16},{9,17... | collective-permute-start | bytes 1572872 | tf_op jit(solution)/shard_map/ppermute | solution.py:190
  39.7 0.1 collective-permute-start.5
  39.8 0.5 collective-permute-start.4
  40.3 0.1 collective-permute-start.3
  40.4 8.2 %collective-permute-done.1.k_own = bf16[4,256,256]{2,1,0:T(8,128)(2,1)S(1)} collective-permute-done((bf16[4,256,256]{2,1,0:T(8,128)(2,1)S(1)}, bf16[4,256,256]{2,1,0:T(8,128)(2,1)S(1)}, u32[]{:S(2)}, u32[]{:S(2)}) %collective-permute-start.1) | collective-permute-done | bytes 524320 | tf_op jit(solution)/shard_map/ppermute | solution.py:190
  48.6 0.0 collective-permute-start.2
  48.6 5.4 %collective-permute-start.7 = (bf16[4,256,256]{2,1,0:T(8,128)(2,1)S(1)}, bf16[4,256,256]{2,1,0:T(8,128)(2,1)}, u32[]{:S(2)}, u32[]{:S(2)}) collective-permute-start(bf16[4,256,256]{2,1,0:T(8,128)(2,1)S(1)} %collective-permute-done.v_own), channel_id=1, source_target_pairs={{0,8},{1,9},{2,10},{3,11},{4,12},{5,13},{6,14},{7,15},{8,16},{9,17... | collective-permute-start | bytes 1572872 | tf_op jit(solution)/shard_map/ppermute | solution.py:190
  54.0 0.0 collective-permute-done.5.v_oth
  54.0 0.8 copy-done
  54.8 2.1 %collective-permute-start.6 = (bf16[4,256,256]{2,1,0:T(8,128)(2,1)S(1)}, bf16[4,256,256]{2,1,0:T(8,128)(2,1)}, u32[]{:S(2)}, u32[]{:S(2)}) collective-permute-start(bf16[4,256,256]{2,1,0:T(8,128)(2,1)S(1)} %collective-permute-done.1.k_own), channel_id=1, source_target_pairs={{0,8},{1,9},{2,10},{3,11},{4,12},{5,13},{6,14},{7,15},{8,16},{9,17... | collective-permute-start | bytes 1572872 | tf_op jit(solution)/shard_map/ppermute | solution.py:190
  56.9 0.0 collective-permute-done.4.k_oth
  56.9 0.0 copy-start.2
  57.0 0.8 copy-done.2
  57.7 0.0 all-to-all-done.1.q_ref
  57.7 1.0 copy-done.1
  58.8 1.0 copy-done.3
  59.8 4.7 %attend_0.1 = (f32[4,512,256]{2,1,0:T(8,128)S(1)}, f32[4,512,128]{2,1,0:T(8,128)S(1)}) custom-call(bf16[4,528,256]{2,1,0:T(8,128)(2,1)S(1)} %all-to-all-done.1.q_ref, bf16[4,256,256]{2,1,0:T(8,128)(2,1)S(1)} %all-to-all-done.2.k_own, bf16[4,256,256]{2,1,0:T(8,128)(2,1)S(1)} %copy-done.3, bf16[4,256,256]{2,1,0:T(8,128)(2,1)S(1)} %all-to-all-done.v_own, ...), custom_call_target="tpu_custom_call" | custom-call | flops 5368709120 | bytes 8388608 | tf_op jit(solution)/shard_map/attend_0/pallas_call | solution.py:145
  64.5 7.2 %attend_1.1 = (f32[4,512,256]{2,1,0:T(8,128)S(1)}, f32[4,512,128]{2,1,0:T(8,128)S(1)}) custom-call(bf16[4,528,256]{2,1,0:T(8,128)(2,1)S(1)} %all-to-all-done.1.q_ref, bf16[4,256,256]{2,1,0:T(8,128)(2,1)S(1)} %collective-permute-done.1.k_own, bf16[4,256,256]{2,1,0:T(8,128)(2,1)} %collective-permute-done.2.k_oth, ...), custom_call_target="tpu_custom_call", output_to_operand_aliasing={{0}: (5, {}), {1}: (6, {})} | custom-call | flops 8589934592 | bytes 8388608 | tf_op jit(solution)/shard_map/attend_1/pallas_call | solution.py:145
  71.7 5.4 %collective-permute-done.6.k_own = bf16[4,256,256]{2,1,0:T(8,128)(2,1)} collective-permute-done((bf16[4,256,256]{2,1,0:T(8,128)(2,1)S(1)}, bf16[4,256,256]{2,1,0:T(8,128)(2,1)}, u32[]{:S(2)}, u32[]{:S(2)}) %collective-permute-start.6) | collective-permute-done | bytes 524320 | tf_op jit(solution)/shard_map/ppermute | solution.py:190
  77.1 0.5 collective-permute-start.9
  77.6 1.6 %collective-permute-done.8.k_oth = bf16[4,256,256]{2,1,0:T(8,128)(2,1)S(1)} collective-permute-done((bf16[4,256,256]{2,1,0:T(8,128)(2,1)}, bf16[4,256,256]{2,1,0:T(8,128)(2,1)S(1)}, u32[]{:S(2)}, u32[]{:S(2)}) %collective-permute-start.8) | collective-permute-done | bytes 524320 | tf_op jit(solution)/shard_map/ppermute | solution.py:193
  79.2 0.7 collective-permute-done.9.v_oth
  80.0 6.4 %attend_2.1 = bf16[4,4,64,512]{3,2,1,0:T(8,128)(2,1)} custom-call(bf16[4,528,256]{2,1,0:T(8,128)(2,1)S(1)} %all-to-all-done.1.q_ref, bf16[4,256,256]{2,1,0:T(8,128)(2,1)} %collective-permute-done.6.k_own, bf16[4,256,256]{2,1,0:T(8,128)(2,1)S(1)} %collective-permute-done.8.k_oth, bf16[4,256,256]{2,1,0:T(8,128)(2,1)} %collective-permute-done.7.v_own, ...), custom_call_target="tpu_custom_call" | custom-call | flops 5368709120 | bytes 8388608 | tf_op jit(solution)/shard_map/attend_2/pallas_call | solution.py:145
  86.4 7.2 %all-to-all-start.3 = ((bf16[16,64,512]{2,1,0:T(8,128)(2,1)}), bf16[16,64,512]{2,1,0:T(8,128)(2,1)S(1)}, u32[]{:S(2)}, u32[]{:S(2)}) async-start(bf16[16,64,512]{2,1,0:T(8,128)(2,1)} %bitcast.3), calls=%async_computation.3 | async-start | bytes 2097152 | tf_op jit(solution)/shard_map/all_to_all | solution.py:235
  93.6 2.0 %collective-permute-start.10 = (f32[1,2048]{1,0:T(1,128)S(1)}, f32[1,2048]{1,0:T(1,128)S(1)}, u32[]{:S(2)}, u32[]{:S(2)}) collective-permute-start(f32[1,2048]{1,0:T(1,128)S(1)} %copy-done.5), channel_id=1, source_target_pairs={{0,64},{64,128},{128,192},{192,0},{1,65},{65,129},{129,193},{193,1... | collective-permute-start | bytes 24584 | tf_op jit(solution)/shard_map/ppermute | solution.py:196
  95.6 2.7 %collective-permute-start.11 = (f32[1,2048]{1,0:T(1,128)S(1)}, f32[1,2048]{1,0:T(1,128)S(1)}, u32[]{:S(2)}, u32[]{:S(2)}) collective-permute-start(f32[1,2048]{1,0:T(1,128)S(1)} %copy-done.5), channel_id=1, source_target_pairs={{0,128},{64,192},{128,0},{192,64},{1,129},{65,193},{129,1},{193,65... | collective-permute-start | bytes 24584 | tf_op jit(solution)/shard_map/ppermute | solution.py:196
  98.2 1.5 %collective-permute-start.12 = (f32[1,2048]{1,0:T(1,128)S(1)}, f32[1,2048]{1,0:T(1,128)S(1)}, u32[]{:S(2)}, u32[]{:S(2)}) collective-permute-start(f32[1,2048]{1,0:T(1,128)S(1)} %copy-done.5), channel_id=1, source_target_pairs={{0,192},{64,0},{128,64},{192,128},{1,193},{65,1},{129,65},{193,129... | collective-permute-start | bytes 24584 | tf_op jit(solution)/shard_map/ppermute | solution.py:196
  99.7 7.2 %collective-permute-done.10.g1_ref = f32[1,2048]{1,0:T(1,128)S(1)} collective-permute-done((f32[1,2048]{1,0:T(1,128)S(1)}, f32[1,2048]{1,0:T(1,128)S(1)}, u32[]{:S(2)}, u32[]{:S(2)}) %collective-permute-start.10) | collective-permute-done | bytes 8224 | tf_op jit(solution)/shard_map/ppermute | solution.py:196
  106.9 2.3 %collective-permute-done.11.g2_ref = f32[1,2048]{1,0:T(1,128)S(1)} collective-permute-done((f32[1,2048]{1,0:T(1,128)S(1)}, f32[1,2048]{1,0:T(1,128)S(1)}, u32[]{:S(2)}, u32[]{:S(2)}) %collective-permute-start.11) | collective-permute-done | bytes 8224 | tf_op jit(solution)/shard_map/ppermute | solution.py:196
  109.2 2.5 %all-to-all-done.3.got_ref = bf16[16,64,512]{2,1,0:T(8,128)(2,1)S(1)} async-done(((bf16[16,64,512]{2,1,0:T(8,128)(2,1)}), bf16[16,64,512]{2,1,0:T(8,128)(2,1)S(1)}, u32[]{:S(2)}, u32[]{:S(2)}) %all-to-all-start.3) | async-done | bytes 1048608 | tf_op jit(solution)/shard_map/all_to_all | solution.py:235
  111.7 0.0 copy-start.4
  111.7 1.0 copy-done.4
  112.6 3.1 %combine.1 = bf16[4,64,2048]{2,1,0:T(8,128)(2,1)} custom-call(bf16[16,64,512]{2,1,0:T(8,128)(2,1)} %copy-done.4, bf16[256,2048]{1,0:T(8,128)(2,1)} %res_ref.1, f32[1,2048]{1,0:T(1,128)} %g0_ref.1, f32[1,2048]{1,0:T(1,128)} %copy-done.6, f32[1,2048]{1,0:T(1,128)} %copy-done.7, f32[1,2048]{1,0:T(1,128)} %copy-done.8), custom_call_target="tpu_custom_call" | custom-call | tf_op jit(solution)/shard_map/combine/pallas_call | solution.py:238
  115.7 16.1 %all_to_all.25 = bf16[4,64,2048]{2,1,0:T(8,128)(2,1)S(1)} all-to-all(bf16[4,64,2048]{2,1,0:T(8,128)(2,1)} %combine.1), channel_id=1, replica_groups=mesh['section'=4,'seq'=64] {'section'}, dimensions={0} | all-to-all | bytes 2097152 | tf_op jit(solution)/shard_map/all_to_all | solution.py:246
  131.8 1.0 copy.12
  (23 shorter events, 0.1 us)
Async XLA Ops:
  0.0 6.4 %copy-start.9 = (s32[256]{0:T(256)S(1)}, s32[256]{0:T(256)}, u32[]{:S(2)}) copy-start(s32[256]{0:T(256)} %param.10) | copy-start | bytes 3076
  1.9 13.9 %all-to-all-start = ((bf16[4,256,256]{2,1,0:T(8,128)(2,1)}), bf16[4,256,256]{2,1,0:T(8,128)(2,1)S(1)}, u32[]{:S(2)}, u32[]{:S(2)}) async-start(bf16[4,256,256]{2,1,0:T(8,128)(2,1)} %split_v.1), calls=%async_computation | async-start | bytes 1048576 | tf_op jit(solution)/shard_map/all_to_all | solution.py:187
  15.8 14.7 %collective-permute-start = (bf16[4,256,256]{2,1,0:T(8,128)(2,1)S(1)}, bf16[4,256,256]{2,1,0:T(8,128)(2,1)S(1)}, u32[]{:S(2)}, u32[]{:S(2)}) collective-permute-start(bf16[4,256,256]{2,1,0:T(8,128)(2,1)S(1)} %all-to-all-done.v_own), channel_id=1, source_target_pairs={{0,8},{1,9},{2,10},{3,11},{4,12},{5,13},{6,14},{7,15},{8,16},{9,17... | collective-permute-start | bytes 1572872 | tf_op jit(solution)/shard_map/ppermute | solution.py:190
  20.9 11.5 %all-to-all-start.2 = ((bf16[4,256,256]{2,1,0:T(8,128)(2,1)}), bf16[4,256,256]{2,1,0:T(8,128)(2,1)S(1)}, u32[]{:S(2)}, u32[]{:S(2)}) async-start(bf16[4,256,256]{2,1,0:T(8,128)(2,1)} %rotate_k.1), calls=%async_computation.2 | async-start | bytes 1048576 | tf_op jit(solution)/shard_map/all_to_all | solution.py:187
  32.4 25.3 %all-to-all-start.1 = ((bf16[4,528,256]{2,1,0:T(8,128)(2,1)}), bf16[4,528,256]{2,1,0:T(8,128)(2,1)S(1)}, u32[]{:S(2)}, u32[]{:S(2)}) async-start(bf16[4,528,256]{2,1,0:T(8,128)(2,1)} %rotate_q.1), calls=%async_computation.1 | async-start | bytes 2162688 | tf_op jit(solution)/shard_map/all_to_all | solution.py:187
  35.9 12.7 %collective-permute-start.1 = (bf16[4,256,256]{2,1,0:T(8,128)(2,1)S(1)}, bf16[4,256,256]{2,1,0:T(8,128)(2,1)S(1)}, u32[]{:S(2)}, u32[]{:S(2)}) collective-permute-start(bf16[4,256,256]{2,1,0:T(8,128)(2,1)S(1)} %all-to-all-done.2.k_own), channel_id=1, source_target_pairs={{0,8},{1,9},{2,10},{3,11},{4,12},{5,13},{6,14},{7,15},{8,16},{9,17... | collective-permute-start | bytes 1572872 | tf_op jit(solution)/shard_map/ppermute | solution.py:190
  39.7 14.4 %collective-permute-start.5 = (bf16[4,256,256]{2,1,0:T(8,128)(2,1)S(1)}, bf16[4,256,256]{2,1,0:T(8,128)(2,1)S(1)}, u32[]{:S(2)}, u32[]{:S(2)}) collective-permute-start(bf16[4,256,256]{2,1,0:T(8,128)(2,1)S(1)} %all-to-all-done.v_own), channel_id=1, source_target_pairs={{0,1},{1,0},{2,3},{3,2},{4,5},{5,4},{6,7},{7,6},{8,9},{9,8},{10,11... | collective-permute-start | bytes 1572872 | tf_op jit(solution)/shard_map/ppermute | solution.py:193
  39.8 17.2 %collective-permute-start.4 = (bf16[4,256,256]{2,1,0:T(8,128)(2,1)S(1)}, bf16[4,256,256]{2,1,0:T(8,128)(2,1)S(1)}, u32[]{:S(2)}, u32[]{:S(2)}) collective-permute-start(bf16[4,256,256]{2,1,0:T(8,128)(2,1)S(1)} %all-to-all-done.2.k_own), channel_id=1, source_target_pairs={{0,1},{1,0},{2,3},{3,2},{4,5},{5,4},{6,7},{7,6},{8,9},{9,8},{10,11... | collective-permute-start | bytes 1572872 | tf_op jit(solution)/shard_map/ppermute | solution.py:193
  40.3 24.2 %collective-permute-start.3 = (bf16[4,256,256]{2,1,0:T(8,128)(2,1)S(1)}, bf16[4,256,256]{2,1,0:T(8,128)(2,1)}, u32[]{:S(2)}, u32[]{:S(2)}) collective-permute-start(bf16[4,256,256]{2,1,0:T(8,128)(2,1)S(1)} %collective-permute-done.v_own), channel_id=1, source_target_pairs={{0,1},{1,0},{2,3},{3,2},{4,5},{5,4},{6,7},{7,6},{8,9},{9,8},{10,11... | collective-permute-start | bytes 1572872 | tf_op jit(solution)/shard_map/ppermute | solution.py:193
  48.6 15.9 %collective-permute-start.2 = (bf16[4,256,256]{2,1,0:T(8,128)(2,1)S(1)}, bf16[4,256,256]{2,1,0:T(8,128)(2,1)}, u32[]{:S(2)}, u32[]{:S(2)}) collective-permute-start(bf16[4,256,256]{2,1,0:T(8,128)(2,1)S(1)} %collective-permute-done.1.k_own), channel_id=1, source_target_pairs={{0,1},{1,0},{2,3},{3,2},{4,5},{5,4},{6,7},{7,6},{8,9},{9,8},{10,11... | collective-permute-start | bytes 1572872 | tf_op jit(solution)/shard_map/ppermute | solution.py:193
  48.6 23.1 %collective-permute-start.7 = (bf16[4,256,256]{2,1,0:T(8,128)(2,1)S(1)}, bf16[4,256,256]{2,1,0:T(8,128)(2,1)}, u32[]{:S(2)}, u32[]{:S(2)}) collective-permute-start(bf16[4,256,256]{2,1,0:T(8,128)(2,1)S(1)} %collective-permute-done.v_own), channel_id=1, source_target_pairs={{0,8},{1,9},{2,10},{3,11},{4,12},{5,13},{6,14},{7,15},{8,16},{9,17... | collective-permute-start | bytes 1572872 | tf_op jit(solution)/shard_map/ppermute | solution.py:190
  54.0 0.8 copy-start
  54.8 22.3 %collective-permute-start.6 = (bf16[4,256,256]{2,1,0:T(8,128)(2,1)S(1)}, bf16[4,256,256]{2,1,0:T(8,128)(2,1)}, u32[]{:S(2)}, u32[]{:S(2)}) collective-permute-start(bf16[4,256,256]{2,1,0:T(8,128)(2,1)S(1)} %collective-permute-done.1.k_own), channel_id=1, source_target_pairs={{0,8},{1,9},{2,10},{3,11},{4,12},{5,13},{6,14},{7,15},{8,16},{9,17... | collective-permute-start | bytes 1572872 | tf_op jit(solution)/shard_map/ppermute | solution.py:190
  56.9 0.8 copy-start.2
  57.7 1.0 copy-start.1
  58.8 1.0 copy-start.3
  77.1 2.1 %collective-permute-start.8 = (bf16[4,256,256]{2,1,0:T(8,128)(2,1)}, bf16[4,256,256]{2,1,0:T(8,128)(2,1)S(1)}, u32[]{:S(2)}, u32[]{:S(2)}) collective-permute-start(bf16[4,256,256]{2,1,0:T(8,128)(2,1)} %collective-permute-done.6.k_own), channel_id=1, source_target_pairs={{0,1},{1,0},{2,3},{3,2},{4,5},{5,4},{6,7},{7,6},{8,9},{9,8},{10,11... | collective-permute-start | bytes 1572872 | tf_op jit(solution)/shard_map/ppermute | solution.py:193
  77.1 2.9 %collective-permute-start.9 = (bf16[4,256,256]{2,1,0:T(8,128)(2,1)}, bf16[4,256,256]{2,1,0:T(8,128)(2,1)S(1)}, u32[]{:S(2)}, u32[]{:S(2)}) collective-permute-start(bf16[4,256,256]{2,1,0:T(8,128)(2,1)} %collective-permute-done.7.v_own), channel_id=1, source_target_pairs={{0,1},{1,0},{2,3},{3,2},{4,5},{5,4},{6,7},{7,6},{8,9},{9,8},{10,11... | collective-permute-start | bytes 1572872 | tf_op jit(solution)/shard_map/ppermute | solution.py:193
  86.4 7.2 %copy-start.5 = (f32[1,2048]{1,0:T(1,128)S(1)}, f32[1,2048]{1,0:T(1,128)}, u32[]{:S(2)}) copy-start(f32[1,2048]{1,0:T(1,128)} %g0_ref.1) | copy-start | bytes 24580
  86.4 25.3 %all-to-all-start.3 = ((bf16[16,64,512]{2,1,0:T(8,128)(2,1)}), bf16[16,64,512]{2,1,0:T(8,128)(2,1)S(1)}, u32[]{:S(2)}, u32[]{:S(2)}) async-start(bf16[16,64,512]{2,1,0:T(8,128)(2,1)} %bitcast.3), calls=%async_computation.3 | async-start | bytes 2097152 | tf_op jit(solution)/shard_map/all_to_all | solution.py:235
  93.6 13.4 %collective-permute-start.10 = (f32[1,2048]{1,0:T(1,128)S(1)}, f32[1,2048]{1,0:T(1,128)S(1)}, u32[]{:S(2)}, u32[]{:S(2)}) collective-permute-start(f32[1,2048]{1,0:T(1,128)S(1)} %copy-done.5), channel_id=1, source_target_pairs={{0,64},{64,128},{128,192},{192,0},{1,65},{65,129},{129,193},{193,1... | collective-permute-start | bytes 24584 | tf_op jit(solution)/shard_map/ppermute | solution.py:196
  95.6 13.6 %collective-permute-start.11 = (f32[1,2048]{1,0:T(1,128)S(1)}, f32[1,2048]{1,0:T(1,128)S(1)}, u32[]{:S(2)}, u32[]{:S(2)}) collective-permute-start(f32[1,2048]{1,0:T(1,128)S(1)} %copy-done.5), channel_id=1, source_target_pairs={{0,128},{64,192},{128,0},{192,64},{1,129},{65,193},{129,1},{193,65... | collective-permute-start | bytes 24584 | tf_op jit(solution)/shard_map/ppermute | solution.py:196
  98.2 11.0 %collective-permute-start.12 = (f32[1,2048]{1,0:T(1,128)S(1)}, f32[1,2048]{1,0:T(1,128)S(1)}, u32[]{:S(2)}, u32[]{:S(2)}) collective-permute-start(f32[1,2048]{1,0:T(1,128)S(1)} %copy-done.5), channel_id=1, source_target_pairs={{0,192},{64,0},{128,64},{192,128},{1,193},{65,1},{129,65},{193,129... | collective-permute-start | bytes 24584 | tf_op jit(solution)/shard_map/ppermute | solution.py:196
  106.9 4.7 %copy-start.6 = (f32[1,2048]{1,0:T(1,128)}, f32[1,2048]{1,0:T(1,128)S(1)}, u32[]{:S(2)}) copy-start(f32[1,2048]{1,0:T(1,128)S(1)} %collective-permute-done.10.g1_ref) | copy-start | bytes 24580
  109.2 2.5 %copy-start.7 = (f32[1,2048]{1,0:T(1,128)}, f32[1,2048]{1,0:T(1,128)S(1)}, u32[]{:S(2)}) copy-start(f32[1,2048]{1,0:T(1,128)S(1)} %collective-permute-done.11.g2_ref) | copy-start | bytes 24580
  109.2 2.5 %copy-start.8 = (f32[1,2048]{1,0:T(1,128)}, f32[1,2048]{1,0:T(1,128)S(1)}, u32[]{:S(2)}) copy-start(f32[1,2048]{1,0:T(1,128)S(1)} %collective-permute-done.12.g3_ref) | copy-start | bytes 24580
  111.7 1.0 copy-start.4

commit v2 on v1

--- a/solution.py
+++ b/solution.py
@@ -148,7 +148,7 @@
         in_specs=[vspec()] * len(args),
         out_specs=out_specs,
         input_output_aliases=aliases,
-        compiler_params=pltpu.CompilerParams(vmem_limit_bytes=40 << 20),
+        compiler_params=pltpu.CompilerParams(vmem_limit_bytes=24 << 20),
         cost_estimate=pl.CostEstimate(
             flops=pairs * 512 * 256 * 256 * 4 * 2,
             bytes_accessed=8 << 20,
@@ -226,11 +226,12 @@
     v1, q_msg = lax.optimization_barrier((v1, q_msg))
     query = over_y(q_msg)
     v2 = onward(v1)
+    query, v2 = lax.optimization_barrier((query, v2))
     k2 = onward(k1)
 
     num, den = attend(0, query, k0, other(k0), v0, other(v0), None, None)
     num, den = attend(1, query, k1, other(k1), v1, other(v1), num, den)
-    num, den, k2, v2 = lax.optimization_barrier((num, den, k2, v2))
+    num, den, k2 = lax.optimization_barrier((num, den, k2))
     sent = attend(2, query, k2, other(k2), v2, other(v2), num, den)
     got = lax.all_to_all(
         sent.reshape(16, 64, 512), ("section", "seq"), 0, 0, axis_index_groups=SHARED_XY

time: 134 us -> 136 us (1.015)
  local copies, waits for them, and re-layouts: 5.7 us -> 2.04 us
  waiting for transfers between devices: 38.4 us -> 41.8 us
    ppermute x4, waiting for transfers between devices: 16.2 us -> 19.9 us  [onward(): return lax.ppermute(x, 'seq', NEXT_PLANE)]
    unnamed x21 -> x13, local copies, waits for them, and re-layouts: 5.61 us -> 1.95 us
  transfers between devices with their start and end apart: 17 -> 17, of which waited for: 10 -> 9; matrix products, arithmetic and copies ran while one was open for 2% -> 1% of each run, Pallas kernels for 13% -> 13%
where the time goes in v2:
time: 136 us; the launch traced here: 135 us
  starting transfers between devices  42.9 us (32%)
  waiting for transfers between devices  41.8 us (31%)
  Pallas kernels  29.4 us (22%)
  blocking collectives  16.6 us (12%)
  local copies, waits for them, and re-layouts  2.04 us (2%)
  other arithmetic  1.93 us (1%)
    ppermute x4, waiting for transfers between devices, onward(): return lax.ppermute(x, 'seq', NEXT_PLANE)  19.9 us
    pallas_call x3, Pallas kernels, attend(): pl.pallas_call(functools.partial(attend_kernel, back), out_shape=outs, in...  19.4 us
    all_to_all x1, blocking collectives, per_device(): mine = lax.all_to_all(back, 'section', 0, 0)  16.6 us
    ppermute x4, starting transfers between devices, onward(): return lax.ppermute(x, 'seq', NEXT_PLANE)  16.3 us
    all_to_all x3, starting transfers between devices, over_y(): return lax.all_to_all(x, 'seq', 0, 0, axis_index_groups=SHARED_Y)  11.5 us
    ppermute x3, waiting for transfers between devices, per_device(): lax.ppermute(post_gain, 'section', [(i, (i + r) % 4) for i in range(4)])  9.77 us
    all_to_all x3, waiting for transfers between devices, over_y(): return lax.all_to_all(x, 'seq', 0, 0, axis_index_groups=SHARED_Y)  7.9 us
    all_to_all x1, starting transfers between devices, per_device(): lax.all_to_all(sent.reshape(16, 64, 512), ('section', 'seq'), 0, 0, axis_...  7.2 us
  transfers between devices with their start and end apart: 17, of which 9 were waited for; matrix products, arithmetic and copies ran while one was open for 1% of the time, Pallas kernels for 13%

profile of v2, /device:TPU:96, one launch (start us, length us, event | category | flops | bytes accessed | tf_op | source)
XLA Modules:
  0.0 134.8 jit_solution(14606445102786062081)
XLA Ops:
  0.0 1.9 %split_v.1 = bf16[4,256,256]{2,1,0:T(8,128)(2,1)} custom-call(bf16[256,1024]{1,0:T(8,128)(2,1)} %bitcast.7), custom_call_target="tpu_custom_call" | custom-call | tf_op jit(solution)/shard_map/split_v/pallas_call | solution.py:199
  1.9 4.5 %all-to-all-start = ((bf16[4,256,256]{2,1,0:T(8,128)(2,1)}), bf16[4,256,256]{2,1,0:T(8,128)(2,1)S(1)}, u32[]{:S(2)}, u32[]{:S(2)}) async-start(bf16[4,256,256]{2,1,0:T(8,128)(2,1)} %split_v.1), calls=%async_computation | async-start | bytes 1048576 | tf_op jit(solution)/shard_map/all_to_all | solution.py:187
  6.4 1.2 multiply_sine_fusion
  7.6 2.2 %rotate_k.1 = bf16[4,256,256]{2,1,0:T(8,128)(2,1)} custom-call(f32[256,128]{1,0:T(8,128)} %get-tuple-element.32.cos_ref, f32[256,128]{1,0:T(8,128)} %get-tuple-element.31.sin_ref, bf16[256,1024]{1,0:T(8,128)(2,1)} %bitcast.8), custom_call_target="tpu_custom_call" | custom-call | tf_op jit(solution)/shard_map/rotate_k/pallas_call | solution.py:206
  9.8 6.0 %all-to-all-done.v_own = bf16[4,256,256]{2,1,0:T(8,128)(2,1)S(1)} async-done(((bf16[4,256,256]{2,1,0:T(8,128)(2,1)}), bf16[4,256,256]{2,1,0:T(8,128)(2,1)S(1)}, u32[]{:S(2)}, u32[]{:S(2)}) %all-to-all-start) | async-done | bytes 524320 | tf_op jit(solution)/shard_map/all_to_all | solution.py:187
  15.9 5.0 %collective-permute-start = (bf16[4,256,256]{2,1,0:T(8,128)(2,1)S(1)}, bf16[4,256,256]{2,1,0:T(8,128)(2,1)S(1)}, u32[]{:S(2)}, u32[]{:S(2)}) collective-permute-start(bf16[4,256,256]{2,1,0:T(8,128)(2,1)S(1)} %all-to-all-done.v_own), channel_id=1, source_target_pairs={{0,8},{1,9},{2,10},{3,11},{4,12},{5,13},{6,14},{7,15},{8,16},{9,17... | collective-permute-start | bytes 1572872 | tf_op jit(solution)/shard_map/ppermute | solution.py:190
  20.9 3.5 %all-to-all-start.2 = ((bf16[4,256,256]{2,1,0:T(8,128)(2,1)}), bf16[4,256,256]{2,1,0:T(8,128)(2,1)S(1)}, u32[]{:S(2)}, u32[]{:S(2)}) async-start(bf16[4,256,256]{2,1,0:T(8,128)(2,1)} %rotate_k.1), calls=%async_computation.2 | async-start | bytes 1048576 | tf_op jit(solution)/shard_map/all_to_all | solution.py:187
  24.4 0.1 pad.2.clone
  24.5 0.7 maximum_maximum_fusion.place_ref
  25.2 2.8 %rotate_q.1 = bf16[4,528,256]{2,1,0:T(8,128)(2,1)} custom-call(f32[256,128]{1,0:T(8,128)} %get-tuple-element.32.cos_ref, f32[256,128]{1,0:T(8,128)} %get-tuple-element.31.sin_ref, bf16[16,256]{1,0:T(8,128)(2,1)} %maximum_maximum_fusion.place_ref, bf16[256,2048]{1,0:T(8,128)(2,1)} %bitcast.6), custom_call_target="tpu_custom_call" | custom-call | tf_op jit(solution)/shard_map/rotate_q/pallas_call | solution.py:213
  28.0 2.6 %collective-permute-done.v_own = bf16[4,256,256]{2,1,0:T(8,128)(2,1)S(1)} collective-permute-done((bf16[4,256,256]{2,1,0:T(8,128)(2,1)S(1)}, bf16[4,256,256]{2,1,0:T(8,128)(2,1)S(1)}, u32[]{:S(2)}, u32[]{:S(2)}) %collective-permute-start) | collective-permute-done | bytes 524320 | tf_op jit(solution)/shard_map/ppermute | solution.py:190
  30.6 1.9 %all-to-all-done.2.k_own = bf16[4,256,256]{2,1,0:T(8,128)(2,1)S(1)} async-done(((bf16[4,256,256]{2,1,0:T(8,128)(2,1)}), bf16[4,256,256]{2,1,0:T(8,128)(2,1)S(1)}, u32[]{:S(2)}, u32[]{:S(2)}) %all-to-all-start.2) | async-done | bytes 524320 | tf_op jit(solution)/shard_map/all_to_all | solution.py:187
  32.4 3.5 %all-to-all-start.1 = ((bf16[4,528,256]{2,1,0:T(8,128)(2,1)}), bf16[4,528,256]{2,1,0:T(8,128)(2,1)S(1)}, u32[]{:S(2)}, u32[]{:S(2)}) async-start(bf16[4,528,256]{2,1,0:T(8,128)(2,1)} %rotate_q.1), calls=%async_computation.1 | async-start | bytes 2162688 | tf_op jit(solution)/shard_map/all_to_all | solution.py:187
  36.0 3.7 %collective-permute-start.2 = (bf16[4,256,256]{2,1,0:T(8,128)(2,1)S(1)}, bf16[4,256,256]{2,1,0:T(8,128)(2,1)}, u32[]{:S(2)}, u32[]{:S(2)}) collective-permute-start(bf16[4,256,256]{2,1,0:T(8,128)(2,1)S(1)} %all-to-all-done.2.k_own), channel_id=1, source_target_pairs={{0,8},{1,9},{2,10},{3,11},{4,12},{5,13},{6,14},{7,15},{8,16},{9,17... | collective-permute-start | bytes 1572872 | tf_op jit(solution)/shard_map/ppermute | solution.py:190
  39.7 2.1 %collective-permute-start.1 = (bf16[4,256,256]{2,1,0:T(8,128)(2,1)S(1)}, bf16[4,256,256]{2,1,0:T(8,128)(2,1)S(1)}, u32[]{:S(2)}, u32[]{:S(2)}) collective-permute-start(bf16[4,256,256]{2,1,0:T(8,128)(2,1)S(1)} %collective-permute-done.v_own), channel_id=1, source_target_pairs={{0,8},{1,9},{2,10},{3,11},{4,12},{5,13},{6,14},{7,15},{8,16},{9,17... | collective-permute-start | bytes 1572872 | tf_op jit(solution)/shard_map/ppermute | solution.py:190
  41.8 0.1 collective-permute-start.6
  41.9 0.5 collective-permute-start.5
  42.4 0.1 collective-permute-start.4
  42.5 10.3 %collective-permute-done.2.k_own = bf16[4,256,256]{2,1,0:T(8,128)(2,1)} collective-permute-done((bf16[4,256,256]{2,1,0:T(8,128)(2,1)S(1)}, bf16[4,256,256]{2,1,0:T(8,128)(2,1)}, u32[]{:S(2)}, u32[]{:S(2)}) %collective-permute-start.2) | collective-permute-done | bytes 524320 | tf_op jit(solution)/shard_map/ppermute | solution.py:190
  52.8 0.0 collective-permute-start.3
  52.8 7.0 %collective-permute-done.1.v_own = bf16[4,256,256]{2,1,0:T(8,128)(2,1)S(1)} collective-permute-done((bf16[4,256,256]{2,1,0:T(8,128)(2,1)S(1)}, bf16[4,256,256]{2,1,0:T(8,128)(2,1)S(1)}, u32[]{:S(2)}, u32[]{:S(2)}) %collective-permute-start.1) | collective-permute-done | bytes 524320 | tf_op jit(solution)/shard_map/ppermute | solution.py:190
  59.9 5.4 %collective-permute-start.7 = (bf16[4,256,256]{2,1,0:T(8,128)(2,1)}, bf16[4,256,256]{2,1,0:T(8,128)(2,1)}, u32[]{:S(2)}, u32[]{:S(2)}) collective-permute-start(bf16[4,256,256]{2,1,0:T(8,128)(2,1)} %collective-permute-done.2.k_own), channel_id=1, source_target_pairs={{0,8},{1,9},{2,10},{3,11},{4,12},{5,13},{6,14},{7,15},{8,16},{9,17... | collective-permute-start | bytes 1572872 | tf_op jit(solution)/shard_map/ppermute | solution.py:190
  65.3 0.0 all-to-all-done.1.q_ref
  65.3 0.0 collective-permute-done.6.v_oth
  65.3 0.3 collective-permute-start.9
  65.6 0.0 collective-permute-done.5.k_oth
  65.6 5.8 %attend_0.1 = (f32[4,512,256]{2,1,0:T(8,128)S(1)}, f32[4,512,128]{2,1,0:T(8,128)S(1)}) custom-call(bf16[4,528,256]{2,1,0:T(8,128)(2,1)S(1)} %all-to-all-done.1.q_ref, bf16[4,256,256]{2,1,0:T(8,128)(2,1)S(1)} %all-to-all-done.2.k_own, bf16[4,256,256]{2,1,0:T(8,128)(2,1)} %collective-permute-done.5.k_oth, bf16[4,256,256]{2,1,0:T(8,128)(2,1)S(1)} %all-to-all-done.v_own, ...), custom_call_target="tpu_custom_call" | custom-call | flops 5368709120 | bytes 8388608 | tf_op jit(solution)/shard_map/attend_0/pallas_call | solution.py:145
  71.5 0.0 collective-permute-done.4.v_oth
  71.5 0.0 collective-permute-done.3.k_oth
  71.5 7.3 %attend_1.1 = (f32[4,512,256]{2,1,0:T(8,128)S(1)}, f32[4,512,128]{2,1,0:T(8,128)S(1)}) custom-call(bf16[4,528,256]{2,1,0:T(8,128)(2,1)S(1)} %all-to-all-done.1.q_ref, bf16[4,256,256]{2,1,0:T(8,128)(2,1)} %collective-permute-done.2.k_own, bf16[4,256,256]{2,1,0:T(8,128)(2,1)} %collective-permute-done.3.k_oth, ...), custom_call_target="tpu_custom_call", output_to_operand_aliasing={{0}: (5, {}), {1}: (6, {})} | custom-call | flops 8589934592 | bytes 8388608 | tf_op jit(solution)/shard_map/attend_1/pallas_call | solution.py:145
  78.8 0.0 collective-permute-done.7.k_own
  78.8 0.8 collective-permute-start.8
  79.6 0.0 collective-permute-done.9.v_oth
  79.6 1.7 %collective-permute-done.8.k_oth = bf16[4,256,256]{2,1,0:T(8,128)(2,1)S(1)} collective-permute-done((bf16[4,256,256]{2,1,0:T(8,128)(2,1)}, bf16[4,256,256]{2,1,0:T(8,128)(2,1)S(1)}, u32[]{:S(2)}, u32[]{:S(2)}) %collective-permute-start.8) | collective-permute-done | bytes 524320 | tf_op jit(solution)/shard_map/ppermute | solution.py:193
  81.4 6.2 %attend_2.1 = bf16[4,4,64,512]{3,2,1,0:T(8,128)(2,1)} custom-call(bf16[4,528,256]{2,1,0:T(8,128)(2,1)S(1)} %all-to-all-done.1.q_ref, bf16[4,256,256]{2,1,0:T(8,128)(2,1)} %collective-permute-done.7.k_own, bf16[4,256,256]{2,1,0:T(8,128)(2,1)S(1)} %collective-permute-done.8.k_oth, bf16[4,256,256]{2,1,0:T(8,128)(2,1)S(1)} %collective-permute-done.1.v_own, ...), custom_call_target="tpu_custom_call" | custom-call | flops 5368709120 | bytes 8388608 | tf_op jit(solution)/shard_map/attend_2/pallas_call | solution.py:145
  87.6 7.2 %all-to-all-start.3 = ((bf16[16,64,512]{2,1,0:T(8,128)(2,1)}), bf16[16,64,512]{2,1,0:T(8,128)(2,1)S(1)}, u32[]{:S(2)}, u32[]{:S(2)}) async-start(bf16[16,64,512]{2,1,0:T(8,128)(2,1)} %bitcast.3), calls=%async_computation.3 | async-start | bytes 2097152 | tf_op jit(solution)/shard_map/all_to_all | solution.py:236
  94.8 2.0 %collective-permute-start.10 = (f32[1,2048]{1,0:T(1,128)S(1)}, f32[1,2048]{1,0:T(1,128)S(1)}, u32[]{:S(2)}, u32[]{:S(2)}) collective-permute-start(f32[1,2048]{1,0:T(1,128)S(1)} %copy-done.1), channel_id=1, source_target_pairs={{0,64},{64,128},{128,192},{192,0},{1,65},{65,129},{129,193},{193,1... | collective-permute-start | bytes 24584 | tf_op jit(solution)/shard_map/ppermute | solution.py:196
  96.8 2.7 %collective-permute-start.11 = (f32[1,2048]{1,0:T(1,128)S(1)}, f32[1,2048]{1,0:T(1,128)S(1)}, u32[]{:S(2)}, u32[]{:S(2)}) collective-permute-start(f32[1,2048]{1,0:T(1,128)S(1)} %copy-done.1), channel_id=1, source_target_pairs={{0,128},{64,192},{128,0},{192,64},{1,129},{65,193},{129,1},{193,65... | collective-permute-start | bytes 24584 | tf_op jit(solution)/shard_map/ppermute | solution.py:196
  99.5 1.5 %collective-permute-start.12 = (f32[1,2048]{1,0:T(1,128)S(1)}, f32[1,2048]{1,0:T(1,128)S(1)}, u32[]{:S(2)}, u32[]{:S(2)}) collective-permute-start(f32[1,2048]{1,0:T(1,128)S(1)} %copy-done.1), channel_id=1, source_target_pairs={{0,192},{64,0},{128,64},{192,128},{1,193},{65,1},{129,65},{193,129... | collective-permute-start | bytes 24584 | tf_op jit(solution)/shard_map/ppermute | solution.py:196
  101.0 7.2 %collective-permute-done.10.g1_ref = f32[1,2048]{1,0:T(1,128)S(1)} collective-permute-done((f32[1,2048]{1,0:T(1,128)S(1)}, f32[1,2048]{1,0:T(1,128)S(1)}, u32[]{:S(2)}, u32[]{:S(2)}) %collective-permute-start.10) | collective-permute-done | bytes 8224 | tf_op jit(solution)/shard_map/ppermute | solution.py:196
  108.1 2.6 %collective-permute-done.11.g2_ref = f32[1,2048]{1,0:T(1,128)S(1)} collective-permute-done((f32[1,2048]{1,0:T(1,128)S(1)}, f32[1,2048]{1,0:T(1,128)S(1)}, u32[]{:S(2)}, u32[]{:S(2)}) %collective-permute-start.11) | collective-permute-done | bytes 8224 | tf_op jit(solution)/shard_map/ppermute | solution.py:196
  110.7 0.0 collective-permute-done.12.g3_ref
  110.7 2.4 %all-to-all-done.3.got_ref = bf16[16,64,512]{2,1,0:T(8,128)(2,1)S(1)} async-done(((bf16[16,64,512]{2,1,0:T(8,128)(2,1)}), bf16[16,64,512]{2,1,0:T(8,128)(2,1)S(1)}, u32[]{:S(2)}, u32[]{:S(2)}) %all-to-all-start.3) | async-done | bytes 1048608 | tf_op jit(solution)/shard_map/all_to_all | solution.py:236
  113.2 0.0 copy-start
  113.2 1.0 copy-done
  114.1 3.1 %combine.1 = bf16[4,64,2048]{2,1,0:T(8,128)(2,1)} custom-call(bf16[16,64,512]{2,1,0:T(8,128)(2,1)} %copy-done, bf16[256,2048]{1,0:T(8,128)(2,1)} %res_ref.1, f32[1,2048]{1,0:T(1,128)} %g0_ref.1, f32[1,2048]{1,0:T(1,128)} %copy-done.2, f32[1,2048]{1,0:T(1,128)} %copy-done.3, f32[1,2048]{1,0:T(1,128)} %copy-done.4), custom_call_target="tpu_custom_call" | custom-call | tf_op jit(solution)/shard_map/combine/pallas_call | solution.py:239
  117.2 16.6 %all_to_all.25 = bf16[4,64,2048]{2,1,0:T(8,128)(2,1)S(1)} all-to-all(bf16[4,64,2048]{2,1,0:T(8,128)(2,1)} %combine.1), channel_id=1, replica_groups=mesh['section'=4,'seq'=64] {'section'}, dimensions={0} | all-to-all | bytes 2097152 | tf_op jit(solution)/shard_map/all_to_all | solution.py:247
  133.8 1.0 copy.12
  (15 shorter events, 0.0 us)
Async XLA Ops:
  0.0 6.4 %copy-start.5 = (s32[256]{0:T(256)S(1)}, s32[256]{0:T(256)}, u32[]{:S(2)}) copy-start(s32[256]{0:T(256)} %param.10) | copy-start | bytes 3076
  1.9 13.9 %all-to-all-start = ((bf16[4,256,256]{2,1,0:T(8,128)(2,1)}), bf16[4,256,256]{2,1,0:T(8,128)(2,1)S(1)}, u32[]{:S(2)}, u32[]{:S(2)}) async-start(bf16[4,256,256]{2,1,0:T(8,128)(2,1)} %split_v.1), calls=%async_computation | async-start | bytes 1048576 | tf_op jit(solution)/shard_map/all_to_all | solution.py:187
  15.9 14.7 %collective-permute-start = (bf16[4,256,256]{2,1,0:T(8,128)(2,1)S(1)}, bf16[4,256,256]{2,1,0:T(8,128)(2,1)S(1)}, u32[]{:S(2)}, u32[]{:S(2)}) collective-permute-start(bf16[4,256,256]{2,1,0:T(8,128)(2,1)S(1)} %all-to-all-done.v_own), channel_id=1, source_target_pairs={{0,8},{1,9},{2,10},{3,11},{4,12},{5,13},{6,14},{7,15},{8,16},{9,17... | collective-permute-start | bytes 1572872 | tf_op jit(solution)/shard_map/ppermute | solution.py:190
  20.9 11.5 %all-to-all-start.2 = ((bf16[4,256,256]{2,1,0:T(8,128)(2,1)}), bf16[4,256,256]{2,1,0:T(8,128)(2,1)S(1)}, u32[]{:S(2)}, u32[]{:S(2)}) async-start(bf16[4,256,256]{2,1,0:T(8,128)(2,1)} %rotate_k.1), calls=%async_computation.2 | async-start | bytes 1048576 | tf_op jit(solution)/shard_map/all_to_all | solution.py:187
  32.4 32.9 %all-to-all-start.1 = ((bf16[4,528,256]{2,1,0:T(8,128)(2,1)}), bf16[4,528,256]{2,1,0:T(8,128)(2,1)S(1)}, u32[]{:S(2)}, u32[]{:S(2)}) async-start(bf16[4,528,256]{2,1,0:T(8,128)(2,1)} %rotate_q.1), calls=%async_computation.1 | async-start | bytes 2162688 | tf_op jit(solution)/shard_map/all_to_all | solution.py:187
  36.0 16.9 %collective-permute-start.2 = (bf16[4,256,256]{2,1,0:T(8,128)(2,1)S(1)}, bf16[4,256,256]{2,1,0:T(8,128)(2,1)}, u32[]{:S(2)}, u32[]{:S(2)}) collective-permute-start(bf16[4,256,256]{2,1,0:T(8,128)(2,1)S(1)} %all-to-all-done.2.k_own), channel_id=1, source_target_pairs={{0,8},{1,9},{2,10},{3,11},{4,12},{5,13},{6,14},{7,15},{8,16},{9,17... | collective-permute-start | bytes 1572872 | tf_op jit(solution)/shard_map/ppermute | solution.py:190
  39.7 20.1 %collective-permute-start.1 = (bf16[4,256,256]{2,1,0:T(8,128)(2,1)S(1)}, bf16[4,256,256]{2,1,0:T(8,128)(2,1)S(1)}, u32[]{:S(2)}, u32[]{:S(2)}) collective-permute-start(bf16[4,256,256]{2,1,0:T(8,128)(2,1)S(1)} %collective-permute-done.v_own), channel_id=1, source_target_pairs={{0,8},{1,9},{2,10},{3,11},{4,12},{5,13},{6,14},{7,15},{8,16},{9,17... | collective-permute-start | bytes 1572872 | tf_op jit(solution)/shard_map/ppermute | solution.py:190
  41.8 23.5 %collective-permute-start.6 = (bf16[4,256,256]{2,1,0:T(8,128)(2,1)S(1)}, bf16[4,256,256]{2,1,0:T(8,128)(2,1)}, u32[]{:S(2)}, u32[]{:S(2)}) collective-permute-start(bf16[4,256,256]{2,1,0:T(8,128)(2,1)S(1)} %all-to-all-done.v_own), channel_id=1, source_target_pairs={{0,1},{1,0},{2,3},{3,2},{4,5},{5,4},{6,7},{7,6},{8,9},{9,8},{10,11... | collective-permute-start | bytes 1572872 | tf_op jit(solution)/shard_map/ppermute | solution.py:193
  41.9 23.7 %collective-permute-start.5 = (bf16[4,256,256]{2,1,0:T(8,128)(2,1)S(1)}, bf16[4,256,256]{2,1,0:T(8,128)(2,1)}, u32[]{:S(2)}, u32[]{:S(2)}) collective-permute-start(bf16[4,256,256]{2,1,0:T(8,128)(2,1)S(1)} %all-to-all-done.2.k_own), channel_id=1, source_target_pairs={{0,1},{1,0},{2,3},{3,2},{4,5},{5,4},{6,7},{7,6},{8,9},{9,8},{10,11... | collective-permute-start | bytes 1572872 | tf_op jit(solution)/shard_map/ppermute | solution.py:193
  42.4 29.0 %collective-permute-start.4 = (bf16[4,256,256]{2,1,0:T(8,128)(2,1)S(1)}, bf16[4,256,256]{2,1,0:T(8,128)(2,1)}, u32[]{:S(2)}, u32[]{:S(2)}) collective-permute-start(bf16[4,256,256]{2,1,0:T(8,128)(2,1)S(1)} %collective-permute-done.v_own), channel_id=1, source_target_pairs={{0,1},{1,0},{2,3},{3,2},{4,5},{5,4},{6,7},{7,6},{8,9},{9,8},{10,11... | collective-permute-start | bytes 1572872 | tf_op jit(solution)/shard_map/ppermute | solution.py:193
  52.8 18.7 %collective-permute-start.3 = (bf16[4,256,256]{2,1,0:T(8,128)(2,1)}, bf16[4,256,256]{2,1,0:T(8,128)(2,1)}, u32[]{:S(2)}, u32[]{:S(2)}) collective-permute-start(bf16[4,256,256]{2,1,0:T(8,128)(2,1)} %collective-permute-done.2.k_own), channel_id=1, source_target_pairs={{0,1},{1,0},{2,3},{3,2},{4,5},{5,4},{6,7},{7,6},{8,9},{9,8},{10,11... | collective-permute-start | bytes 1572872 | tf_op jit(solution)/shard_map/ppermute | solution.py:193
  59.9 19.0 %collective-permute-start.7 = (bf16[4,256,256]{2,1,0:T(8,128)(2,1)}, bf16[4,256,256]{2,1,0:T(8,128)(2,1)}, u32[]{:S(2)}, u32[]{:S(2)}) collective-permute-start(bf16[4,256,256]{2,1,0:T(8,128)(2,1)} %collective-permute-done.2.k_own), channel_id=1, source_target_pairs={{0,8},{1,9},{2,10},{3,11},{4,12},{5,13},{6,14},{7,15},{8,16},{9,17... | collective-permute-start | bytes 1572872 | tf_op jit(solution)/shard_map/ppermute | solution.py:190
  65.3 14.3 %collective-permute-start.9 = (bf16[4,256,256]{2,1,0:T(8,128)(2,1)S(1)}, bf16[4,256,256]{2,1,0:T(8,128)(2,1)S(1)}, u32[]{:S(2)}, u32[]{:S(2)}) collective-permute-start(bf16[4,256,256]{2,1,0:T(8,128)(2,1)S(1)} %collective-permute-done.1.v_own), channel_id=1, source_target_pairs={{0,1},{1,0},{2,3},{3,2},{4,5},{5,4},{6,7},{7,6},{8,9},{9,8},{10,11... | collective-permute-start | bytes 1572872 | tf_op jit(solution)/shard_map/ppermute | solution.py:193
  78.8 2.5 %collective-permute-start.8 = (bf16[4,256,256]{2,1,0:T(8,128)(2,1)}, bf16[4,256,256]{2,1,0:T(8,128)(2,1)S(1)}, u32[]{:S(2)}, u32[]{:S(2)}) collective-permute-start(bf16[4,256,256]{2,1,0:T(8,128)(2,1)} %collective-permute-done.7.k_own), channel_id=1, source_target_pairs={{0,1},{1,0},{2,3},{3,2},{4,5},{5,4},{6,7},{7,6},{8,9},{9,8},{10,11... | collective-permute-start | bytes 1572872 | tf_op jit(solution)/shard_map/ppermute | solution.py:193
  87.6 7.2 %copy-start.1 = (f32[1,2048]{1,0:T(1,128)S(1)}, f32[1,2048]{1,0:T(1,128)}, u32[]{:S(2)}) copy-start(f32[1,2048]{1,0:T(1,128)} %g0_ref.1) | copy-start | bytes 24580
  87.6 25.5 %all-to-all-start.3 = ((bf16[16,64,512]{2,1,0:T(8,128)(2,1)}), bf16[16,64,512]{2,1,0:T(8,128)(2,1)S(1)}, u32[]{:S(2)}, u32[]{:S(2)}) async-start(bf16[16,64,512]{2,1,0:T(8,128)(2,1)} %bitcast.3), calls=%async_computation.3 | async-start | bytes 2097152 | tf_op jit(solution)/shard_map/all_to_all | solution.py:236
  94.8 13.3 %collective-permute-start.10 = (f32[1,2048]{1,0:T(1,128)S(1)}, f32[1,2048]{1,0:T(1,128)S(1)}, u32[]{:S(2)}, u32[]{:S(2)}) collective-permute-start(f32[1,2048]{1,0:T(1,128)S(1)} %copy-done.1), channel_id=1, source_target_pairs={{0,64},{64,128},{128,192},{192,0},{1,65},{65,129},{129,193},{193,1... | collective-permute-start | bytes 24584 | tf_op jit(solution)/shard_map/ppermute | solution.py:196
  96.8 13.9 %collective-permute-start.11 = (f32[1,2048]{1,0:T(1,128)S(1)}, f32[1,2048]{1,0:T(1,128)S(1)}, u32[]{:S(2)}, u32[]{:S(2)}) collective-permute-start(f32[1,2048]{1,0:T(1,128)S(1)} %copy-done.1), channel_id=1, source_target_pairs={{0,128},{64,192},{128,0},{192,64},{1,129},{65,193},{129,1},{193,65... | collective-permute-start | bytes 24584 | tf_op jit(solution)/shard_map/ppermute | solution.py:196
  99.5 11.2 %collective-permute-start.12 = (f32[1,2048]{1,0:T(1,128)S(1)}, f32[1,2048]{1,0:T(1,128)S(1)}, u32[]{:S(2)}, u32[]{:S(2)}) collective-permute-start(f32[1,2048]{1,0:T(1,128)S(1)} %copy-done.1), channel_id=1, source_target_pairs={{0,192},{64,0},{128,64},{192,128},{1,193},{65,1},{129,65},{193,129... | collective-permute-start | bytes 24584 | tf_op jit(solution)/shard_map/ppermute | solution.py:196
  108.1 5.0 %copy-start.2 = (f32[1,2048]{1,0:T(1,128)}, f32[1,2048]{1,0:T(1,128)S(1)}, u32[]{:S(2)}) copy-start(f32[1,2048]{1,0:T(1,128)S(1)} %collective-permute-done.10.g1_ref) | copy-start | bytes 24580
  110.7 2.4 %copy-start.3 = (f32[1,2048]{1,0:T(1,128)}, f32[1,2048]{1,0:T(1,128)S(1)}, u32[]{:S(2)}) copy-start(f32[1,2048]{1,0:T(1,128)S(1)} %collective-permute-done.11.g2_ref) | copy-start | bytes 24580
  110.7 2.4 %copy-start.4 = (f32[1,2048]{1,0:T(1,128)}, f32[1,2048]{1,0:T(1,128)S(1)}, u32[]{:S(2)}) copy-start(f32[1,2048]{1,0:T(1,128)S(1)} %collective-permute-done.12.g3_ref) | copy-start | bytes 24580
  113.2 1.0 copy-start

commit v3 on v2

--- a/solution.py
+++ b/solution.py
@@ -150,9 +150,9 @@
         input_output_aliases=aliases,
         compiler_params=pltpu.CompilerParams(vmem_limit_bytes=24 << 20),
         cost_estimate=pl.CostEstimate(
-            flops=pairs * 512 * 256 * 256 * 4 * 2,
-            bytes_accessed=8 << 20,
-            transcendentals=pairs * 512 * 256 * 2,
+            flops=int(pairs * 512 * 256 * 256 * 4 * 0.2),
+            bytes_accessed=1 << 16,
+            transcendentals=1,
         ),
         name="attend_%d" % back,
     )(*args)
@@ -226,10 +226,10 @@
     v1, q_msg = lax.optimization_barrier((v1, q_msg))
     query = over_y(q_msg)
     v2 = onward(v1)
-    query, v2 = lax.optimization_barrier((query, v2))
     k2 = onward(k1)
 
     num, den = attend(0, query, k0, other(k0), v0, other(v0), None, None)
+    num, den, v2 = lax.optimization_barrier((num, den, v2))
     num, den = attend(1, query, k1, other(k1), v1, other(v1), num, den)
     num, den, k2 = lax.optimization_barrier((num, den, k2))
     sent = attend(2, query, k2, other(k2), v2, other(v2), num, den)

time: 136 us -> 126 us (0.926)
  waiting for transfers between devices: 41.8 us -> 27.2 us
  local copies, waits for them, and re-layouts: 2.04 us -> 5.7 us
  starting transfers between devices: 42.9 us -> 46 us
  Pallas kernels: 29.4 us -> 27.3 us
    ppermute x4, waiting for transfers between devices: 19.9 us -> 4.29 us  [onward(): return lax.ppermute(x, 'seq', NEXT_PLANE)]
    unnamed x13 -> x21, local copies, waits for them, and re-layouts: 1.95 us -> 5.61 us
    ppermute x4, starting transfers between devices: 16.3 us -> 19 us  [onward(): return lax.ppermute(x, 'seq', NEXT_PLANE)]
    pallas_call x3, Pallas kernels: 19.4 us -> 17.3 us  [attend(): pl.pallas_call(functools.partial(attend_kernel, back), out_shape=outs, in...]
  transfers between devices with their start and end apart: 17 -> 17, of which waited for: 9 -> 9; matrix products, arithmetic and copies ran while one was open for 1% -> 2% of each run, Pallas kernels for 13% -> 14%
where the time goes in v3:
time: 126 us; the launch traced here: 124 us
  starting transfers between devices  46 us (37%)
  Pallas kernels  27.3 us (22%)
  waiting for transfers between devices  27.2 us (22%)
  blocking collectives  16.1 us (13%)
  local copies, waits for them, and re-layouts  5.7 us (5%)
  other arithmetic  1.92 us (2%)
    ppermute x4, starting transfers between devices, onward(): return lax.ppermute(x, 'seq', NEXT_PLANE)  19 us
    pallas_call x3, Pallas kernels, attend(): pl.pallas_call(functools.partial(attend_kernel, back), out_shape=outs, in...  17.3 us
    all_to_all x1, blocking collectives, per_device(): mine = lax.all_to_all(back, 'section', 0, 0)  16.1 us
    all_to_all x3, starting transfers between devices, over_y(): return lax.all_to_all(x, 'seq', 0, 0, axis_index_groups=SHARED_Y)  12.7 us
    ppermute x3, waiting for transfers between devices, per_device(): lax.ppermute(post_gain, 'section', [(i, (i + r) % 4) for i in range(4)])  9.5 us
    all_to_all x3, waiting for transfers between devices, over_y(): return lax.all_to_all(x, 'seq', 0, 0, axis_index_groups=SHARED_Y)  9.08 us
    all_to_all x1, starting transfers between devices, per_device(): lax.all_to_all(sent.reshape(16, 64, 512), ('section', 'seq'), 0, 0, axis_...  7.5 us
    ppermute x3, starting transfers between devices, per_device(): lax.ppermute(post_gain, 'section', [(i, (i + r) % 4) for i in range(4)])  6.14 us
  transfers between devices with their start and end apart: 17, of which 9 were waited for; matrix products, arithmetic and copies ran while one was open for 2% of the time, Pallas kernels for 14%

profile of v3, /device:TPU:96, one launch (start us, length us, event | category | flops | bytes accessed | tf_op | source)
XLA Modules:
  0.0 124.4 jit_solution(9291635699018819196)
XLA Ops:
  0.0 1.9 %split_v.1 = bf16[4,256,256]{2,1,0:T(8,128)(2,1)} custom-call(bf16[256,1024]{1,0:T(8,128)(2,1)} %bitcast.7), custom_call_target="tpu_custom_call" | custom-call | tf_op jit(solution)/shard_map/split_v/pallas_call | solution.py:199
  1.9 4.5 %all-to-all-start = ((bf16[4,256,256]{2,1,0:T(8,128)(2,1)}), bf16[4,256,256]{2,1,0:T(8,128)(2,1)S(1)}, u32[]{:S(2)}, u32[]{:S(2)}) async-start(bf16[4,256,256]{2,1,0:T(8,128)(2,1)} %split_v.1), calls=%async_computation | async-start | bytes 1048576 | tf_op jit(solution)/shard_map/all_to_all | solution.py:187
  6.4 1.2 multiply_sine_fusion
  7.6 2.2 %rotate_k.1 = bf16[4,256,256]{2,1,0:T(8,128)(2,1)} custom-call(f32[256,128]{1,0:T(8,128)} %get-tuple-element.34.cos_ref, f32[256,128]{1,0:T(8,128)} %get-tuple-element.33.sin_ref, bf16[256,1024]{1,0:T(8,128)(2,1)} %bitcast.8), custom_call_target="tpu_custom_call" | custom-call | tf_op jit(solution)/shard_map/rotate_k/pallas_call | solution.py:206
  9.8 6.0 %all-to-all-done.v_own = bf16[4,256,256]{2,1,0:T(8,128)(2,1)S(1)} async-done(((bf16[4,256,256]{2,1,0:T(8,128)(2,1)}), bf16[4,256,256]{2,1,0:T(8,128)(2,1)S(1)}, u32[]{:S(2)}, u32[]{:S(2)}) %all-to-all-start) | async-done | bytes 524320 | tf_op jit(solution)/shard_map/all_to_all | solution.py:187
  15.8 3.5 %all-to-all-start.2 = ((bf16[4,256,256]{2,1,0:T(8,128)(2,1)}), bf16[4,256,256]{2,1,0:T(8,128)(2,1)S(1)}, u32[]{:S(2)}, u32[]{:S(2)}) async-start(bf16[4,256,256]{2,1,0:T(8,128)(2,1)} %rotate_k.1), calls=%async_computation.2 | async-start | bytes 1048576 | tf_op jit(solution)/shard_map/all_to_all | solution.py:187
  19.3 5.0 %collective-permute-start = (bf16[4,256,256]{2,1,0:T(8,128)(2,1)S(1)}, bf16[4,256,256]{2,1,0:T(8,128)(2,1)}, u32[]{:S(2)}, u32[]{:S(2)}) collective-permute-start(bf16[4,256,256]{2,1,0:T(8,128)(2,1)S(1)} %all-to-all-done.v_own), channel_id=1, source_target_pairs={{0,8},{1,9},{2,10},{3,11},{4,12},{5,13},{6,14},{7,15},{8,16},{9,17... | collective-permute-start | bytes 1572872 | tf_op jit(solution)/shard_map/ppermute | solution.py:190
  24.4 0.1 pad.2.clone
  24.5 0.0 collective-permute-start.5
  24.5 3.0 %all-to-all-done.2.k_own = bf16[4,256,256]{2,1,0:T(8,128)(2,1)S(1)} async-done(((bf16[4,256,256]{2,1,0:T(8,128)(2,1)}), bf16[4,256,256]{2,1,0:T(8,128)(2,1)S(1)}, u32[]{:S(2)}, u32[]{:S(2)}) %all-to-all-start.2) | async-done | bytes 524320 | tf_op jit(solution)/shard_map/all_to_all | solution.py:187
  27.5 5.0 %collective-permute-start.1 = (bf16[4,256,256]{2,1,0:T(8,128)(2,1)S(1)}, bf16[4,256,256]{2,1,0:T(8,128)(2,1)}, u32[]{:S(2)}, u32[]{:S(2)}) collective-permute-start(bf16[4,256,256]{2,1,0:T(8,128)(2,1)S(1)} %all-to-all-done.2.k_own), channel_id=1, source_target_pairs={{0,8},{1,9},{2,10},{3,11},{4,12},{5,13},{6,14},{7,15},{8,16},{9,17... | collective-permute-start | bytes 1572872 | tf_op jit(solution)/shard_map/ppermute | solution.py:190
  32.6 0.7 maximum_maximum_fusion.place_ref
  33.3 2.8 %rotate_q.1 = bf16[4,528,256]{2,1,0:T(8,128)(2,1)} custom-call(f32[256,128]{1,0:T(8,128)} %get-tuple-element.34.cos_ref, f32[256,128]{1,0:T(8,128)} %get-tuple-element.33.sin_ref, bf16[16,256]{1,0:T(8,128)(2,1)} %maximum_maximum_fusion.place_ref, bf16[256,2048]{1,0:T(8,128)(2,1)} %bitcast.6), custom_call_target="tpu_custom_call" | custom-call | tf_op jit(solution)/shard_map/rotate_q/pallas_call | solution.py:213
  36.0 0.7 collective-permute-done.v_own
  36.7 4.7 %all-to-all-start.1 = ((bf16[4,528,256]{2,1,0:T(8,128)(2,1)}), bf16[4,528,256]{2,1,0:T(8,128)(2,1)S(1)}, u32[]{:S(2)}, u32[]{:S(2)}) async-start(bf16[4,528,256]{2,1,0:T(8,128)(2,1)} %rotate_q.1), calls=%async_computation.1 | async-start | bytes 2162688 | tf_op jit(solution)/shard_map/all_to_all | solution.py:187
  41.5 0.0 collective-permute-start.4
  41.5 5.7 %collective-permute-start.6 = (bf16[4,256,256]{2,1,0:T(8,128)(2,1)}, bf16[4,256,256]{2,1,0:T(8,128)(2,1)S(1)}, u32[]{:S(2)}, u32[]{:S(2)}) collective-permute-start(bf16[4,256,256]{2,1,0:T(8,128)(2,1)} %collective-permute-done.v_own), channel_id=1, source_target_pairs={{0,8},{1,9},{2,10},{3,11},{4,12},{5,13},{6,14},{7,15},{8,16},{9,17... | collective-permute-start | bytes 1572872 | tf_op jit(solution)/shard_map/ppermute | solution.py:190
  47.2 0.3 collective-permute-start.3
  47.5 0.0 collective-permute-done.1.k_own
  47.5 0.3 collective-permute-start.2
  47.8 0.0 collective-permute-done.5.v_oth
  47.8 0.8 copy-done
  48.6 3.2 %collective-permute-start.7 = (bf16[4,256,256]{2,1,0:T(8,128)(2,1)}, bf16[4,256,256]{2,1,0:T(8,128)(2,1)S(1)}, u32[]{:S(2)}, u32[]{:S(2)}) collective-permute-start(bf16[4,256,256]{2,1,0:T(8,128)(2,1)} %collective-permute-done.1.k_own), channel_id=1, source_target_pairs={{0,8},{1,9},{2,10},{3,11},{4,12},{5,13},{6,14},{7,15},{8,16},{9,17... | collective-permute-start | bytes 1572872 | tf_op jit(solution)/shard_map/ppermute | solution.py:190
  51.8 0.0 collective-permute-done.4.k_oth
  51.8 0.0 copy-start.2
  51.8 0.8 copy-done.2
  52.6 1.0 copy-done.1
  53.6 1.0 copy-done.3
  54.7 4.7 %attend_0.1 = (f32[4,512,256]{2,1,0:T(8,128)S(1)}, f32[4,512,128]{2,1,0:T(8,128)S(1)}) custom-call(bf16[4,528,256]{2,1,0:T(8,128)(2,1)S(1)} %all-to-all-done.1.q_ref, bf16[4,256,256]{2,1,0:T(8,128)(2,1)S(1)} %all-to-all-done.2.k_own, bf16[4,256,256]{2,1,0:T(8,128)(2,1)S(1)} %copy-done.3, bf16[4,256,256]{2,1,0:T(8,128)(2,1)S(1)} %all-to-all-done.v_own, ...), custom_call_target="tpu_custom_call" | custom-call | flops 536870912 | bytes 65536 | tf_op jit(solution)/shard_map/attend_0/pallas_call | solution.py:145
  59.3 0.4 collective-permute-done.6.v_own
  59.7 0.1 collective-permute-start.9
  59.8 0.0 collective-permute-done.3.v_oth
  59.8 7.5 %attend_1.1 = (f32[4,512,256]{2,1,0:T(8,128)S(1)}, f32[4,512,128]{2,1,0:T(8,128)S(1)}) custom-call(bf16[4,528,256]{2,1,0:T(8,128)(2,1)S(1)} %all-to-all-done.1.q_ref, bf16[4,256,256]{2,1,0:T(8,128)(2,1)} %collective-permute-done.1.k_own, bf16[4,256,256]{2,1,0:T(8,128)(2,1)} %collective-permute-done.2.k_oth, ...), custom_call_target="tpu_custom_call", output_to_operand_aliasing={{0}: (5, {}), {1}: (6, {})} | custom-call | flops 858993472 | bytes 65536 | tf_op jit(solution)/shard_map/attend_1/pallas_call | solution.py:145
  67.3 3.2 %collective-permute-done.7.k_own = bf16[4,256,256]{2,1,0:T(8,128)(2,1)S(1)} collective-permute-done((bf16[4,256,256]{2,1,0:T(8,128)(2,1)}, bf16[4,256,256]{2,1,0:T(8,128)(2,1)S(1)}, u32[]{:S(2)}, u32[]{:S(2)}) %collective-permute-start.7) | collective-permute-done | bytes 524320 | tf_op jit(solution)/shard_map/ppermute | solution.py:190
  70.6 1.9 %collective-permute-done.8.k_oth = bf16[4,256,256]{2,1,0:T(8,128)(2,1)S(1)} collective-permute-done((bf16[4,256,256]{2,1,0:T(8,128)(2,1)S(1)}, bf16[4,256,256]{2,1,0:T(8,128)(2,1)S(1)}, u32[]{:S(2)}, u32[]{:S(2)}) %collective-permute-start.8) | collective-permute-done | bytes 524320 | tf_op jit(solution)/shard_map/ppermute | solution.py:193
  72.5 5.2 %attend_2.1 = bf16[4,4,64,512]{3,2,1,0:T(8,128)(2,1)} custom-call(bf16[4,528,256]{2,1,0:T(8,128)(2,1)S(1)} %all-to-all-done.1.q_ref, bf16[4,256,256]{2,1,0:T(8,128)(2,1)S(1)} %collective-permute-done.7.k_own, bf16[4,256,256]{2,1,0:T(8,128)(2,1)S(1)} %collective-permute-done.8.k_oth, bf16[4,256,256]{2,1,0:T(8,128)(2,1)S(1)} %collective-permute-done.6.v_own, ...), custom_call_target="tpu_custom_call" | custom-call | flops 536870912 | bytes 65536 | tf_op jit(solution)/shard_map/attend_2/pallas_call | solution.py:145
  77.7 7.5 %all-to-all-start.3 = ((bf16[16,64,512]{2,1,0:T(8,128)(2,1)}), bf16[16,64,512]{2,1,0:T(8,128)(2,1)S(1)}, u32[]{:S(2)}, u32[]{:S(2)}) async-start(bf16[16,64,512]{2,1,0:T(8,128)(2,1)} %bitcast.3), calls=%async_computation.3 | async-start | bytes 2097152 | tf_op jit(solution)/shard_map/all_to_all | solution.py:236
  85.2 2.0 %collective-permute-start.10 = (f32[1,2048]{1,0:T(1,128)S(1)}, f32[1,2048]{1,0:T(1,128)S(1)}, u32[]{:S(2)}, u32[]{:S(2)}) collective-permute-start(f32[1,2048]{1,0:T(1,128)S(1)} %copy-done.5), channel_id=1, source_target_pairs={{0,64},{64,128},{128,192},{192,0},{1,65},{65,129},{129,193},{193,1... | collective-permute-start | bytes 24584 | tf_op jit(solution)/shard_map/ppermute | solution.py:196
  87.2 2.7 %collective-permute-start.11 = (f32[1,2048]{1,0:T(1,128)S(1)}, f32[1,2048]{1,0:T(1,128)S(1)}, u32[]{:S(2)}, u32[]{:S(2)}) collective-permute-start(f32[1,2048]{1,0:T(1,128)S(1)} %copy-done.5), channel_id=1, source_target_pairs={{0,128},{64,192},{128,0},{192,64},{1,129},{65,193},{129,1},{193,65... | collective-permute-start | bytes 24584 | tf_op jit(solution)/shard_map/ppermute | solution.py:196
  89.9 1.5 %collective-permute-start.12 = (f32[1,2048]{1,0:T(1,128)S(1)}, f32[1,2048]{1,0:T(1,128)S(1)}, u32[]{:S(2)}, u32[]{:S(2)}) collective-permute-start(f32[1,2048]{1,0:T(1,128)S(1)} %copy-done.5), channel_id=1, source_target_pairs={{0,192},{64,0},{128,64},{192,128},{1,193},{65,1},{129,65},{193,129... | collective-permute-start | bytes 24584 | tf_op jit(solution)/shard_map/ppermute | solution.py:196
  91.3 7.2 %collective-permute-done.10.g1_ref = f32[1,2048]{1,0:T(1,128)S(1)} collective-permute-done((f32[1,2048]{1,0:T(1,128)S(1)}, f32[1,2048]{1,0:T(1,128)S(1)}, u32[]{:S(2)}, u32[]{:S(2)}) %collective-permute-start.10) | collective-permute-done | bytes 8224 | tf_op jit(solution)/shard_map/ppermute | solution.py:196
  98.6 2.3 %collective-permute-done.11.g2_ref = f32[1,2048]{1,0:T(1,128)S(1)} collective-permute-done((f32[1,2048]{1,0:T(1,128)S(1)}, f32[1,2048]{1,0:T(1,128)S(1)}, u32[]{:S(2)}, u32[]{:S(2)}) %collective-permute-start.11) | collective-permute-done | bytes 8224 | tf_op jit(solution)/shard_map/ppermute | solution.py:196
  100.8 2.5 %all-to-all-done.3.got_ref = bf16[16,64,512]{2,1,0:T(8,128)(2,1)S(1)} async-done(((bf16[16,64,512]{2,1,0:T(8,128)(2,1)}), bf16[16,64,512]{2,1,0:T(8,128)(2,1)S(1)}, u32[]{:S(2)}, u32[]{:S(2)}) %all-to-all-start.3) | async-done | bytes 1048608 | tf_op jit(solution)/shard_map/all_to_all | solution.py:236
  103.3 0.0 copy-start.4
  103.3 1.0 copy-done.4
  104.3 3.1 %combine.1 = bf16[4,64,2048]{2,1,0:T(8,128)(2,1)} custom-call(bf16[16,64,512]{2,1,0:T(8,128)(2,1)} %copy-done.4, bf16[256,2048]{1,0:T(8,128)(2,1)} %res_ref.1, f32[1,2048]{1,0:T(1,128)} %g0_ref.1, f32[1,2048]{1,0:T(1,128)} %copy-done.6, f32[1,2048]{1,0:T(1,128)} %copy-done.7, f32[1,2048]{1,0:T(1,128)} %copy-done.8), custom_call_target="tpu_custom_call" | custom-call | tf_op jit(solution)/shard_map/combine/pallas_call | solution.py:239
  107.3 16.1 %all_to_all.25 = bf16[4,64,2048]{2,1,0:T(8,128)(2,1)S(1)} all-to-all(bf16[4,64,2048]{2,1,0:T(8,128)(2,1)} %combine.1), channel_id=1, replica_groups=mesh['section'=4,'seq'=64] {'section'}, dimensions={0} | all-to-all | bytes 2097152 | tf_op jit(solution)/shard_map/all_to_all | solution.py:247
  123.5 1.0 copy.12
  (23 shorter events, 0.1 us)
Async XLA Ops:
  0.0 6.4 %copy-start.9 = (s32[256]{0:T(256)S(1)}, s32[256]{0:T(256)}, u32[]{:S(2)}) copy-start(s32[256]{0:T(256)} %param.10) | copy-start | bytes 3076
  1.9 13.9 %all-to-all-start = ((bf16[4,256,256]{2,1,0:T(8,128)(2,1)}), bf16[4,256,256]{2,1,0:T(8,128)(2,1)S(1)}, u32[]{:S(2)}, u32[]{:S(2)}) async-start(bf16[4,256,256]{2,1,0:T(8,128)(2,1)} %split_v.1), calls=%async_computation | async-start | bytes 1048576 | tf_op jit(solution)/shard_map/all_to_all | solution.py:187
  15.8 11.7 %all-to-all-start.2 = ((bf16[4,256,256]{2,1,0:T(8,128)(2,1)}), bf16[4,256,256]{2,1,0:T(8,128)(2,1)S(1)}, u32[]{:S(2)}, u32[]{:S(2)}) async-start(bf16[4,256,256]{2,1,0:T(8,128)(2,1)} %rotate_k.1), calls=%async_computation.2 | async-start | bytes 1048576 | tf_op jit(solution)/shard_map/all_to_all | solution.py:187
  19.3 17.4 %collective-permute-start = (bf16[4,256,256]{2,1,0:T(8,128)(2,1)S(1)}, bf16[4,256,256]{2,1,0:T(8,128)(2,1)}, u32[]{:S(2)}, u32[]{:S(2)}) collective-permute-start(bf16[4,256,256]{2,1,0:T(8,128)(2,1)S(1)} %all-to-all-done.v_own), channel_id=1, source_target_pairs={{0,8},{1,9},{2,10},{3,11},{4,12},{5,13},{6,14},{7,15},{8,16},{9,17... | collective-permute-start | bytes 1572872 | tf_op jit(solution)/shard_map/ppermute | solution.py:190
  24.5 23.3 %collective-permute-start.5 = (bf16[4,256,256]{2,1,0:T(8,128)(2,1)S(1)}, bf16[4,256,256]{2,1,0:T(8,128)(2,1)S(1)}, u32[]{:S(2)}, u32[]{:S(2)}) collective-permute-start(bf16[4,256,256]{2,1,0:T(8,128)(2,1)S(1)} %all-to-all-done.v_own), channel_id=1, source_target_pairs={{0,1},{1,0},{2,3},{3,2},{4,5},{5,4},{6,7},{7,6},{8,9},{9,8},{10,11... | collective-permute-start | bytes 1572872 | tf_op jit(solution)/shard_map/ppermute | solution.py:193
  27.5 19.9 %collective-permute-start.1 = (bf16[4,256,256]{2,1,0:T(8,128)(2,1)S(1)}, bf16[4,256,256]{2,1,0:T(8,128)(2,1)}, u32[]{:S(2)}, u32[]{:S(2)}) collective-permute-start(bf16[4,256,256]{2,1,0:T(8,128)(2,1)S(1)} %all-to-all-done.2.k_own), channel_id=1, source_target_pairs={{0,8},{1,9},{2,10},{3,11},{4,12},{5,13},{6,14},{7,15},{8,16},{9,17... | collective-permute-start | bytes 1572872 | tf_op jit(solution)/shard_map/ppermute | solution.py:190
  36.7 15.9 %all-to-all-start.1 = ((bf16[4,528,256]{2,1,0:T(8,128)(2,1)}), bf16[4,528,256]{2,1,0:T(8,128)(2,1)S(1)}, u32[]{:S(2)}, u32[]{:S(2)}) async-start(bf16[4,528,256]{2,1,0:T(8,128)(2,1)} %rotate_q.1), calls=%async_computation.1 | async-start | bytes 2162688 | tf_op jit(solution)/shard_map/all_to_all | solution.py:187
  41.5 10.3 %collective-permute-start.4 = (bf16[4,256,256]{2,1,0:T(8,128)(2,1)S(1)}, bf16[4,256,256]{2,1,0:T(8,128)(2,1)S(1)}, u32[]{:S(2)}, u32[]{:S(2)}) collective-permute-start(bf16[4,256,256]{2,1,0:T(8,128)(2,1)S(1)} %all-to-all-done.2.k_own), channel_id=1, source_target_pairs={{0,1},{1,0},{2,3},{3,2},{4,5},{5,4},{6,7},{7,6},{8,9},{9,8},{10,11... | collective-permute-start | bytes 1572872 | tf_op jit(solution)/shard_map/ppermute | solution.py:193
  41.5 18.2 %collective-permute-start.6 = (bf16[4,256,256]{2,1,0:T(8,128)(2,1)}, bf16[4,256,256]{2,1,0:T(8,128)(2,1)S(1)}, u32[]{:S(2)}, u32[]{:S(2)}) collective-permute-start(bf16[4,256,256]{2,1,0:T(8,128)(2,1)} %collective-permute-done.v_own), channel_id=1, source_target_pairs={{0,8},{1,9},{2,10},{3,11},{4,12},{5,13},{6,14},{7,15},{8,16},{9,17... | collective-permute-start | bytes 1572872 | tf_op jit(solution)/shard_map/ppermute | solution.py:190
  47.2 12.7 %collective-permute-start.3 = (bf16[4,256,256]{2,1,0:T(8,128)(2,1)}, bf16[4,256,256]{2,1,0:T(8,128)(2,1)}, u32[]{:S(2)}, u32[]{:S(2)}) collective-permute-start(bf16[4,256,256]{2,1,0:T(8,128)(2,1)} %collective-permute-done.v_own), channel_id=1, source_target_pairs={{0,1},{1,0},{2,3},{3,2},{4,5},{5,4},{6,7},{7,6},{8,9},{9,8},{10,11... | collective-permute-start | bytes 1572872 | tf_op jit(solution)/shard_map/ppermute | solution.py:193
  47.5 12.3 %collective-permute-start.2 = (bf16[4,256,256]{2,1,0:T(8,128)(2,1)}, bf16[4,256,256]{2,1,0:T(8,128)(2,1)}, u32[]{:S(2)}, u32[]{:S(2)}) collective-permute-start(bf16[4,256,256]{2,1,0:T(8,128)(2,1)} %collective-permute-done.1.k_own), channel_id=1, source_target_pairs={{0,1},{1,0},{2,3},{3,2},{4,5},{5,4},{6,7},{7,6},{8,9},{9,8},{10,11... | collective-permute-start | bytes 1572872 | tf_op jit(solution)/shard_map/ppermute | solution.py:193
  47.8 0.8 copy-start
  48.6 22.0 %collective-permute-start.7 = (bf16[4,256,256]{2,1,0:T(8,128)(2,1)}, bf16[4,256,256]{2,1,0:T(8,128)(2,1)S(1)}, u32[]{:S(2)}, u32[]{:S(2)}) collective-permute-start(bf16[4,256,256]{2,1,0:T(8,128)(2,1)} %collective-permute-done.1.k_own), channel_id=1, source_target_pairs={{0,8},{1,9},{2,10},{3,11},{4,12},{5,13},{6,14},{7,15},{8,16},{9,17... | collective-permute-start | bytes 1572872 | tf_op jit(solution)/shard_map/ppermute | solution.py:190
  51.8 0.8 copy-start.2
  52.6 1.0 copy-start.1
  53.6 1.0 copy-start.3
  59.7 10.9 %collective-permute-start.9 = (bf16[4,256,256]{2,1,0:T(8,128)(2,1)S(1)}, bf16[4,256,256]{2,1,0:T(8,128)(2,1)S(1)}, u32[]{:S(2)}, u32[]{:S(2)}) collective-permute-start(bf16[4,256,256]{2,1,0:T(8,128)(2,1)S(1)} %collective-permute-done.6.v_own), channel_id=1, source_target_pairs={{0,1},{1,0},{2,3},{3,2},{4,5},{5,4},{6,7},{7,6},{8,9},{9,8},{10,11... | collective-permute-start | bytes 1572872 | tf_op jit(solution)/shard_map/ppermute | solution.py:193
  70.5 1.9 %collective-permute-start.8 = (bf16[4,256,256]{2,1,0:T(8,128)(2,1)S(1)}, bf16[4,256,256]{2,1,0:T(8,128)(2,1)S(1)}, u32[]{:S(2)}, u32[]{:S(2)}) collective-permute-start(bf16[4,256,256]{2,1,0:T(8,128)(2,1)S(1)} %collective-permute-done.7.k_own), channel_id=1, source_target_pairs={{0,1},{1,0},{2,3},{3,2},{4,5},{5,4},{6,7},{7,6},{8,9},{9,8},{10,11... | collective-permute-start | bytes 1572872 | tf_op jit(solution)/shard_map/ppermute | solution.py:193
  77.7 7.5 %copy-start.5 = (f32[1,2048]{1,0:T(1,128)S(1)}, f32[1,2048]{1,0:T(1,128)}, u32[]{:S(2)}) copy-start(f32[1,2048]{1,0:T(1,128)} %g0_ref.1) | copy-start | bytes 24580
  77.7 25.6 %all-to-all-start.3 = ((bf16[16,64,512]{2,1,0:T(8,128)(2,1)}), bf16[16,64,512]{2,1,0:T(8,128)(2,1)S(1)}, u32[]{:S(2)}, u32[]{:S(2)}) async-start(bf16[16,64,512]{2,1,0:T(8,128)(2,1)} %bitcast.3), calls=%async_computation.3 | async-start | bytes 2097152 | tf_op jit(solution)/shard_map/all_to_all | solution.py:236
  85.2 13.4 %collective-permute-start.10 = (f32[1,2048]{1,0:T(1,128)S(1)}, f32[1,2048]{1,0:T(1,128)S(1)}, u32[]{:S(2)}, u32[]{:S(2)}) collective-permute-start(f32[1,2048]{1,0:T(1,128)S(1)} %copy-done.5), channel_id=1, source_target_pairs={{0,64},{64,128},{128,192},{192,0},{1,65},{65,129},{129,193},{193,1... | collective-permute-start | bytes 24584 | tf_op jit(solution)/shard_map/ppermute | solution.py:196
  87.2 13.6 %collective-permute-start.11 = (f32[1,2048]{1,0:T(1,128)S(1)}, f32[1,2048]{1,0:T(1,128)S(1)}, u32[]{:S(2)}, u32[]{:S(2)}) collective-permute-start(f32[1,2048]{1,0:T(1,128)S(1)} %copy-done.5), channel_id=1, source_target_pairs={{0,128},{64,192},{128,0},{192,64},{1,129},{65,193},{129,1},{193,65... | collective-permute-start | bytes 24584 | tf_op jit(solution)/shard_map/ppermute | solution.py:196
  89.9 11.0 %collective-permute-start.12 = (f32[1,2048]{1,0:T(1,128)S(1)}, f32[1,2048]{1,0:T(1,128)S(1)}, u32[]{:S(2)}, u32[]{:S(2)}) collective-permute-start(f32[1,2048]{1,0:T(1,128)S(1)} %copy-done.5), channel_id=1, source_target_pairs={{0,192},{64,0},{128,64},{192,128},{1,193},{65,1},{129,65},{193,129... | collective-permute-start | bytes 24584 | tf_op jit(solution)/shard_map/ppermute | solution.py:196
  98.5 4.7 %copy-start.6 = (f32[1,2048]{1,0:T(1,128)}, f32[1,2048]{1,0:T(1,128)S(1)}, u32[]{:S(2)}) copy-start(f32[1,2048]{1,0:T(1,128)S(1)} %collective-permute-done.10.g1_ref) | copy-start | bytes 24580
  100.8 2.5 %copy-start.7 = (f32[1,2048]{1,0:T(1,128)}, f32[1,2048]{1,0:T(1,128)S(1)}, u32[]{:S(2)}) copy-start(f32[1,2048]{1,0:T(1,128)S(1)} %collective-permute-done.11.g2_ref) | copy-start | bytes 24580
  100.8 2.5 %copy-start.8 = (f32[1,2048]{1,0:T(1,128)}, f32[1,2048]{1,0:T(1,128)S(1)}, u32[]{:S(2)}) copy-start(f32[1,2048]{1,0:T(1,128)S(1)} %collective-permute-done.12.g3_ref) | copy-start | bytes 24580
  103.3 1.0 copy-start.4

commit v4 on v3

--- a/solution.py
+++ b/solution.py
@@ -162,8 +162,7 @@
     section = lax.axis_index("section")
     for r, ref in enumerate((g0_ref, g1_ref, g2_ref, g3_ref)):
         gain_ref[pl.ds(lax.rem(section + 4 - r, 4), 1), :] = ref[...]
-    rows = pl.ds(pl.multiple_of(section * 64, 64), 64)
-    running = res_ref[rows, :].astype(jnp.float32)
+    running = res_ref[...].astype(jnp.float32)
     running = [running[:, h * 512 : (h + 1) * 512] for h in range(4)]
     for layer in range(LAYERS):
         parts = [got_ref[layer * 4 + h].astype(jnp.float32) for h in range(4)]
@@ -218,6 +217,7 @@
         name="rotate_q",
     )(cosine, sine, places, queries[0])
 
+    residual = lax.dynamic_slice_in_dim(residual_in, lax.axis_index("section") * 64, 64, 0)
     v0 = over_y(v_msg)
     v0, k_msg = lax.optimization_barrier((v0, k_msg))
     v1 = onward(v0)
@@ -231,7 +231,7 @@
     num, den = attend(0, query, k0, other(k0), v0, other(v0), None, None)
     num, den, v2 = lax.optimization_barrier((num, den, v2))
     num, den = attend(1, query, k1, other(k1), v1, other(v1), num, den)
-    num, den, k2 = lax.optimization_barrier((num, den, k2))
+    num, den, k2, residual, *gains = lax.optimization_barrier((num, den, k2, residual, *gains))
     sent = attend(2, query, k2, other(k2), v2, other(v2), num, den)
     got = lax.all_to_all(
         sent.reshape(16, 64, 512), ("section", "seq"), 0, 0, axis_index_groups=SHARED_XY
@@ -242,8 +242,9 @@
         in_specs=[vspec()] * 6,
         out_specs=vspec(),
         scratch_shapes=[VMEM((LAYERS, HQ * HD), jnp.float32)],
+        compiler_params=pltpu.CompilerParams(vmem_limit_bytes=12 << 20),
         name="combine",
-    )(got, residual_in, *gains)
+    )(got, residual, *gains)
     mine = lax.all_to_all(back, "section", 0, 0)
     return mine.reshape(1, ROWS, HQ * HD)
 

time: 126 us -> 123 us (0.976)
  blocking collectives: 16.1 us -> 39.6 us
  waiting for transfers between devices: 27.2 us -> 11.9 us
  starting transfers between devices: 46 us -> 39.1 us
  local copies, waits for them, and re-layouts: 5.7 us -> 1.89 us
    all_to_all x0 -> x1, blocking collectives: none -> 23.3 us  [per_device(): lax.all_to_all(sent.reshape(16, 64, 512), ('section', 'seq'), 0, 0, axis_...]
    ppermute x3, waiting for transfers between devices: 9.5 us -> 0.01 us  [per_device(): lax.ppermute(post_gain, 'section', [(i, (i + r) % 4) for i in range(4)])]
    all_to_all x1 -> x0, starting transfers between devices: 7.5 us -> none  [per_device(): lax.all_to_all(sent.reshape(16, 64, 512), ('section', 'seq'), 0, 0, axis_...]
    unnamed x21 -> x11, local copies, waits for them, and re-layouts: 5.61 us -> 1.78 us
    ppermute x4, waiting for transfers between devices: 4.29 us -> 1.04 us  [onward(): return lax.ppermute(x, 'seq', NEXT_PLANE)]
    pallas_call x1, Pallas kernels: 3.07 us -> 0.51 us  [per_device(): pl.pallas_call(combine_kernel, out_shape=jax.ShapeDtypeStruct((LAYERS, 64...]
    all_to_all x1 -> x0, waiting for transfers between devices: 2.45 us -> none  [per_device(): lax.all_to_all(sent.reshape(16, 64, 512), ('section', 'seq'), 0, 0, axis_...]
    pallas_call x3, Pallas kernels: 17.3 us -> 19.4 us  [attend(): pl.pallas_call(functools.partial(attend_kernel, back), out_shape=outs, in...]
  transfers between devices with their start and end apart: 17 -> 16, of which waited for: 9 -> 5; matrix products, arithmetic and copies ran while one was open for 2% -> 2% of each run, Pallas kernels for 14% -> 15%
where the time goes in v4:
time: 123 us; the launch traced here: 122 us
  blocking collectives  39.6 us (32%)
  starting transfers between devices  39.1 us (32%)
  Pallas kernels  26.9 us (22%)
  waiting for transfers between devices  11.9 us (10%)
  other arithmetic  1.92 us (2%)
  local copies, waits for them, and re-layouts  1.89 us (2%)
    all_to_all x1, blocking collectives, per_device(): lax.all_to_all(sent.reshape(16, 64, 512), ('section', 'seq'), 0, 0, axis_...  23.3 us
    pallas_call x3, Pallas kernels, attend(): pl.pallas_call(functools.partial(attend_kernel, back), out_shape=outs, in...  19.4 us
    ppermute x4, starting transfers between devices, onward(): return lax.ppermute(x, 'seq', NEXT_PLANE)  18.2 us
    all_to_all x1, blocking collectives, per_device(): mine = lax.all_to_all(back, 'section', 0, 0)  16.4 us
    all_to_all x3, starting transfers between devices, over_y(): return lax.all_to_all(x, 'seq', 0, 0, axis_index_groups=SHARED_Y)  12.7 us
    all_to_all x3, waiting for transfers between devices, over_y(): return lax.all_to_all(x, 'seq', 0, 0, axis_index_groups=SHARED_Y)  9.08 us
    ppermute x3, starting transfers between devices, per_device(): lax.ppermute(post_gain, 'section', [(i, (i + r) % 4) for i in range(4)])  7.06 us
    pallas_call x1, Pallas kernels, per_device(): pl.pallas_call(rotate_q_kernel, out_shape=jax.ShapeDtypeStruct((HK, 2 * R...  2.82 us
  transfers between devices with their start and end apart: 16, of which 5 were waited for; matrix products, arithmetic and copies ran while one was open for 2% of the time, Pallas kernels for 15%

profile of v4, /device:TPU:96, one launch (start us, length us, event | category | flops | bytes accessed | tf_op | source)
XLA Modules:
  0.0 121.6 jit_solution(1772750496886104111)
XLA Ops:
  0.0 0.0 copy-start
  0.0 2.0 %split_v.1 = bf16[4,256,256]{2,1,0:T(8,128)(2,1)} custom-call(bf16[256,1024]{1,0:T(8,128)(2,1)} %bitcast.8), custom_call_target="tpu_custom_call" | custom-call | tf_op jit(solution)/shard_map/split_v/pallas_call | solution.py:198
  2.0 4.5 %all-to-all-start = ((bf16[4,256,256]{2,1,0:T(8,128)(2,1)}), bf16[4,256,256]{2,1,0:T(8,128)(2,1)S(1)}, u32[]{:S(2)}, u32[]{:S(2)}) async-start(bf16[4,256,256]{2,1,0:T(8,128)(2,1)} %split_v.1), calls=%async_computation | async-start | bytes 1048576 | tf_op jit(solution)/shard_map/all_to_all | solution.py:186
  6.5 0.0 copy-done.4
  6.5 1.2 %multiply_sine_fusion = (f32[256,128]{1,0:T(8,128)}, f32[256,128]{1,0:T(8,128)}) fusion(f32[128]{0:T(128)S(1)} %multiply_exponential_fusion, f32[256]{0:T(256)S(1)} %get-tuple-element.46), kind=kLoop, calls=%fused_computation | loop fusion | flops 32768 | bytes 263680 | tf_op jit(solution)/shard_map/sin | solution.py:181
  7.7 2.2 %rotate_k.1 = bf16[4,256,256]{2,1,0:T(8,128)(2,1)} custom-call(f32[256,128]{1,0:T(8,128)} %get-tuple-element.44.cos_ref, f32[256,128]{1,0:T(8,128)} %get-tuple-element.43.sin_ref, bf16[256,1024]{1,0:T(8,128)(2,1)} %bitcast.9), custom_call_target="tpu_custom_call" | custom-call | tf_op jit(solution)/shard_map/rotate_k/pallas_call | solution.py:205
  9.9 6.0 %all-to-all-done.v_own = bf16[4,256,256]{2,1,0:T(8,128)(2,1)S(1)} async-done(((bf16[4,256,256]{2,1,0:T(8,128)(2,1)}), bf16[4,256,256]{2,1,0:T(8,128)(2,1)S(1)}, u32[]{:S(2)}, u32[]{:S(2)}) %all-to-all-start) | async-done | bytes 524320 | tf_op jit(solution)/shard_map/all_to_all | solution.py:186
  15.9 3.5 %all-to-all-start.2 = ((bf16[4,256,256]{2,1,0:T(8,128)(2,1)}), bf16[4,256,256]{2,1,0:T(8,128)(2,1)S(1)}, u32[]{:S(2)}, u32[]{:S(2)}) async-start(bf16[4,256,256]{2,1,0:T(8,128)(2,1)} %rotate_k.1), calls=%async_computation.2 | async-start | bytes 1048576 | tf_op jit(solution)/shard_map/all_to_all | solution.py:186
  19.4 5.0 %collective-permute-start = (bf16[4,256,256]{2,1,0:T(8,128)(2,1)S(1)}, bf16[4,256,256]{2,1,0:T(8,128)(2,1)S(1)}, u32[]{:S(2)}, u32[]{:S(2)}) collective-permute-start(bf16[4,256,256]{2,1,0:T(8,128)(2,1)S(1)} %all-to-all-done.v_own), channel_id=1, source_target_pairs={{0,8},{1,9},{2,10},{3,11},{4,12},{5,13},{6,14},{7,15},{8,16},{9,17... | collective-permute-start | bytes 1572872 | tf_op jit(solution)/shard_map/ppermute | solution.py:189
  24.5 0.1 pad.2.clone
  24.6 0.0 collective-permute-start.5
  24.6 3.0 %all-to-all-done.2.k_own = bf16[4,256,256]{2,1,0:T(8,128)(2,1)S(1)} async-done(((bf16[4,256,256]{2,1,0:T(8,128)(2,1)}), bf16[4,256,256]{2,1,0:T(8,128)(2,1)S(1)}, u32[]{:S(2)}, u32[]{:S(2)}) %all-to-all-start.2) | async-done | bytes 524320 | tf_op jit(solution)/shard_map/all_to_all | solution.py:186
  27.7 5.0 %collective-permute-start.1 = (bf16[4,256,256]{2,1,0:T(8,128)(2,1)S(1)}, bf16[4,256,256]{2,1,0:T(8,128)(2,1)}, u32[]{:S(2)}, u32[]{:S(2)}) collective-permute-start(bf16[4,256,256]{2,1,0:T(8,128)(2,1)S(1)} %all-to-all-done.2.k_own), channel_id=1, source_target_pairs={{0,8},{1,9},{2,10},{3,11},{4,12},{5,13},{6,14},{7,15},{8,16},{9,17... | collective-permute-start | bytes 1572872 | tf_op jit(solution)/shard_map/ppermute | solution.py:189
  32.7 0.7 maximum_maximum_fusion.place_ref
  33.4 2.8 %rotate_q.1 = bf16[4,528,256]{2,1,0:T(8,128)(2,1)} custom-call(f32[256,128]{1,0:T(8,128)} %get-tuple-element.44.cos_ref, f32[256,128]{1,0:T(8,128)} %get-tuple-element.43.sin_ref, bf16[16,256]{1,0:T(8,128)(2,1)} %maximum_maximum_fusion.place_ref, bf16[256,2048]{1,0:T(8,128)(2,1)} %bitcast.7), custom_call_target="tpu_custom_call" | custom-call | tf_op jit(solution)/shard_map/rotate_q/pallas_call | solution.py:212
  36.2 0.6 collective-permute-done.v_own
  36.8 0.8 copy-done.1
  37.6 4.7 %all-to-all-start.1 = ((bf16[4,528,256]{2,1,0:T(8,128)(2,1)}), bf16[4,528,256]{2,1,0:T(8,128)(2,1)S(1)}, u32[]{:S(2)}, u32[]{:S(2)}) async-start(bf16[4,528,256]{2,1,0:T(8,128)(2,1)} %rotate_q.1), calls=%async_computation.1 | async-start | bytes 2162688 | tf_op jit(solution)/shard_map/all_to_all | solution.py:186
  42.4 0.0 collective-permute-start.4
  42.4 5.6 %collective-permute-start.6 = (bf16[4,256,256]{2,1,0:T(8,128)(2,1)}, bf16[4,256,256]{2,1,0:T(8,128)(2,1)}, u32[]{:S(2)}, u32[]{:S(2)}) collective-permute-start(bf16[4,256,256]{2,1,0:T(8,128)(2,1)} %copy-done.1), channel_id=1, source_target_pairs={{0,8},{1,9},{2,10},{3,11},{4,12},{5,13},{6,14},{7,15},{8,16},{9,17... | collective-permute-start | bytes 1572872 | tf_op jit(solution)/shard_map/ppermute | solution.py:189
  48.0 0.3 collective-permute-start.3
  48.3 0.0 collective-permute-done.1.k_own
  48.3 0.3 collective-permute-start.2
  48.6 0.0 collective-permute-done.5.v_oth
  48.6 2.5 %collective-permute-start.7 = (bf16[4,256,256]{2,1,0:T(8,128)(2,1)}, bf16[4,256,256]{2,1,0:T(8,128)(2,1)}, u32[]{:S(2)}, u32[]{:S(2)}) collective-permute-start(bf16[4,256,256]{2,1,0:T(8,128)(2,1)} %collective-permute-done.1.k_own), channel_id=1, source_target_pairs={{0,8},{1,9},{2,10},{3,11},{4,12},{5,13},{6,14},{7,15},{8,16},{9,17... | collective-permute-start | bytes 1572872 | tf_op jit(solution)/shard_map/ppermute | solution.py:189
  51.1 0.0 collective-permute-done.4.k_oth
  51.1 2.8 %collective-permute-start.10 = (f32[1,2048]{1,0:T(1,128)S(1)}, f32[1,2048]{1,0:T(1,128)S(1)}, u32[]{:S(2)}, u32[]{:S(2)}) collective-permute-start(f32[1,2048]{1,0:T(1,128)S(1)} %copy-done.3), channel_id=1, source_target_pairs={{0,192},{64,0},{128,64},{192,128},{1,193},{65,1},{129,65},{193,129... | collective-permute-start | bytes 24584 | tf_op jit(solution)/shard_map/ppermute | solution.py:195
  54.0 0.0 all-to-all-done.1.q_ref
  54.0 6.1 %attend_0.1 = (f32[4,512,256]{2,1,0:T(8,128)S(1)}, f32[4,512,128]{2,1,0:T(8,128)S(1)}) custom-call(bf16[4,528,256]{2,1,0:T(8,128)(2,1)S(1)} %all-to-all-done.1.q_ref, bf16[4,256,256]{2,1,0:T(8,128)(2,1)S(1)} %all-to-all-done.2.k_own, bf16[4,256,256]{2,1,0:T(8,128)(2,1)} %collective-permute-done.4.k_oth, bf16[4,256,256]{2,1,0:T(8,128)(2,1)S(1)} %all-to-all-done.v_own, ...), custom_call_target="tpu_custom_call" | custom-call | flops 536870912 | bytes 65536 | tf_op jit(solution)/shard_map/attend_0/pallas_call | solution.py:145
  60.1 0.4 collective-permute-done.6.v_own
  60.5 1.5 %collective-permute-start.8 = (f32[1,2048]{1,0:T(1,128)S(1)}, f32[1,2048]{1,0:T(1,128)S(1)}, u32[]{:S(2)}, u32[]{:S(2)}) collective-permute-start(f32[1,2048]{1,0:T(1,128)S(1)} %copy-done.3), channel_id=1, source_target_pairs={{0,64},{64,128},{128,192},{192,0},{1,65},{65,129},{129,193},{193,1... | collective-permute-start | bytes 24584 | tf_op jit(solution)/shard_map/ppermute | solution.py:195
  62.0 0.0 collective-permute-done.3.v_oth
  62.0 2.7 %collective-permute-start.9 = (f32[1,2048]{1,0:T(1,128)S(1)}, f32[1,2048]{1,0:T(1,128)S(1)}, u32[]{:S(2)}, u32[]{:S(2)}) collective-permute-start(f32[1,2048]{1,0:T(1,128)S(1)} %copy-done.3), channel_id=1, source_target_pairs={{0,128},{64,192},{128,0},{192,64},{1,129},{65,193},{129,1},{193,65... | collective-permute-start | bytes 24584 | tf_op jit(solution)/shard_map/ppermute | solution.py:195
  64.7 0.0 collective-permute-done.2.k_oth
  64.7 0.0 collective-permute-start.12
  64.7 7.7 %attend_1.1 = (f32[4,512,256]{2,1,0:T(8,128)S(1)}, f32[4,512,128]{2,1,0:T(8,128)S(1)}) custom-call(bf16[4,528,256]{2,1,0:T(8,128)(2,1)S(1)} %all-to-all-done.1.q_ref, bf16[4,256,256]{2,1,0:T(8,128)(2,1)} %collective-permute-done.1.k_own, bf16[4,256,256]{2,1,0:T(8,128)(2,1)} %collective-permute-done.2.k_oth, ...), custom_call_target="tpu_custom_call", output_to_operand_aliasing={{0}: (5, {}), {1}: (6, {})} | custom-call | flops 858993472 | bytes 65536 | tf_op jit(solution)/shard_map/attend_1/pallas_call | solution.py:145
  72.4 0.0 collective-permute-done.10.g3_ref
  72.4 0.0 collective-permute-done.8.g1_ref
  72.4 0.0 collective-permute-done.9.g2_ref
  72.4 0.0 collective-permute-done.7.k_own
  72.4 0.6 collective-permute-start.11
  73.0 0.0 collective-permute-done.12.v_oth
  73.0 1.7 %collective-permute-done.11.k_oth = bf16[4,256,256]{2,1,0:T(8,128)(2,1)S(1)} collective-permute-done((bf16[4,256,256]{2,1,0:T(8,128)(2,1)}, bf16[4,256,256]{2,1,0:T(8,128)(2,1)S(1)}, u32[]{:S(2)}, u32[]{:S(2)}) %collective-permute-start.11) | collective-permute-done | bytes 524320 | tf_op jit(solution)/shard_map/ppermute | solution.py:192
  74.8 5.6 %attend_2.1 = bf16[4,4,64,512]{3,2,1,0:T(8,128)(2,1)S(1)} custom-call(bf16[4,528,256]{2,1,0:T(8,128)(2,1)S(1)} %all-to-all-done.1.q_ref, bf16[4,256,256]{2,1,0:T(8,128)(2,1)} %collective-permute-done.7.k_own, bf16[4,256,256]{2,1,0:T(8,128)(2,1)S(1)} %collective-permute-done.11.k_oth, bf16[4,256,256]{2,1,0:T(8,128)(2,1)} %collective-permute-done.6.v_own, ...), custom_call_target="tpu_custom_call" | custom-call | flops 536870912 | bytes 65536 | tf_op jit(solution)/shard_map/attend_2/pallas_call | solution.py:145
  80.4 23.3 %all_to_all.25.got_ref = bf16[16,64,512]{2,1,0:T(8,128)(2,1)S(1)} all-to-all(bf16[16,64,512]{2,1,0:T(8,128)(2,1)S(1)} %bitcast.5), channel_id=1, replica_groups={{0,2,4,6,64,66,68,70,128,130,132,134,192,194,196,198},{1,3,5,7,65,67,69..., dimensions={0} | all-to-all | bytes 2097152 | tf_op jit(solution)/shard_map/all_to_all | solution.py:236
  103.7 0.5 combine.1
  104.2 16.4 %all_to_all.26 = bf16[4,64,2048]{2,1,0:T(8,128)(2,1)S(1)} all-to-all(bf16[4,64,2048]{2,1,0:T(8,128)(2,1)S(1)} %combine.1), channel_id=1, replica_groups=mesh['section'=4,'seq'=64] {'section'}, dimensions={0} | all-to-all | bytes 2097152 | tf_op jit(solution)/shard_map/all_to_all | solution.py:248
  120.6 1.0 copy.12
  (13 shorter events, 0.1 us)
Async XLA Ops:
  0.0 51.1 %copy-start = (bf16[256,2048]{1,0:T(8,128)(2,1)S(1)}, bf16[256,2048]{1,0:T(8,128)(2,1)}, u32[]{:S(2)}) copy-start(bf16[256,2048]{1,0:T(8,128)(2,1)} %param.11) | copy-start | bytes 3145732
  0.0 6.5 %copy-start.4 = (s32[256]{0:T(256)S(1)}, s32[256]{0:T(256)}, u32[]{:S(2)}) copy-start(s32[256]{0:T(256)} %param.10) | copy-start | bytes 3076
  2.0 13.9 %all-to-all-start = ((bf16[4,256,256]{2,1,0:T(8,128)(2,1)}), bf16[4,256,256]{2,1,0:T(8,128)(2,1)S(1)}, u32[]{:S(2)}, u32[]{:S(2)}) async-start(bf16[4,256,256]{2,1,0:T(8,128)(2,1)} %split_v.1), calls=%async_computation | async-start | bytes 1048576 | tf_op jit(solution)/shard_map/all_to_all | solution.py:186
  15.9 11.7 %all-to-all-start.2 = ((bf16[4,256,256]{2,1,0:T(8,128)(2,1)}), bf16[4,256,256]{2,1,0:T(8,128)(2,1)S(1)}, u32[]{:S(2)}, u32[]{:S(2)}) async-start(bf16[4,256,256]{2,1,0:T(8,128)(2,1)} %rotate_k.1), calls=%async_computation.2 | async-start | bytes 1048576 | tf_op jit(solution)/shard_map/all_to_all | solution.py:186
  19.4 17.4 %collective-permute-start = (bf16[4,256,256]{2,1,0:T(8,128)(2,1)S(1)}, bf16[4,256,256]{2,1,0:T(8,128)(2,1)S(1)}, u32[]{:S(2)}, u32[]{:S(2)}) collective-permute-start(bf16[4,256,256]{2,1,0:T(8,128)(2,1)S(1)} %all-to-all-done.v_own), channel_id=1, source_target_pairs={{0,8},{1,9},{2,10},{3,11},{4,12},{5,13},{6,14},{7,15},{8,16},{9,17... | collective-permute-start | bytes 1572872 | tf_op jit(solution)/shard_map/ppermute | solution.py:189
  24.6 24.0 %collective-permute-start.5 = (bf16[4,256,256]{2,1,0:T(8,128)(2,1)S(1)}, bf16[4,256,256]{2,1,0:T(8,128)(2,1)}, u32[]{:S(2)}, u32[]{:S(2)}) collective-permute-start(bf16[4,256,256]{2,1,0:T(8,128)(2,1)S(1)} %all-to-all-done.v_own), channel_id=1, source_target_pairs={{0,1},{1,0},{2,3},{3,2},{4,5},{5,4},{6,7},{7,6},{8,9},{9,8},{10,11... | collective-permute-start | bytes 1572872 | tf_op jit(solution)/shard_map/ppermute | solution.py:192
  27.7 20.6 %collective-permute-start.1 = (bf16[4,256,256]{2,1,0:T(8,128)(2,1)S(1)}, bf16[4,256,256]{2,1,0:T(8,128)(2,1)}, u32[]{:S(2)}, u32[]{:S(2)}) collective-permute-start(bf16[4,256,256]{2,1,0:T(8,128)(2,1)S(1)} %all-to-all-done.2.k_own), channel_id=1, source_target_pairs={{0,8},{1,9},{2,10},{3,11},{4,12},{5,13},{6,14},{7,15},{8,16},{9,17... | collective-permute-start | bytes 1572872 | tf_op jit(solution)/shard_map/ppermute | solution.py:189
  33.4 17.8 %copy-start.3 = (f32[1,2048]{1,0:T(1,128)S(1)}, f32[1,2048]{1,0:T(1,128)}, u32[]{:S(2)}) copy-start(f32[1,2048]{1,0:T(1,128)} %g0_ref) | copy-start | bytes 24580
  36.8 0.8 copy-start.1
  37.6 16.4 %all-to-all-start.1 = ((bf16[4,528,256]{2,1,0:T(8,128)(2,1)}), bf16[4,528,256]{2,1,0:T(8,128)(2,1)S(1)}, u32[]{:S(2)}, u32[]{:S(2)}) async-start(bf16[4,528,256]{2,1,0:T(8,128)(2,1)} %rotate_q.1), calls=%async_computation.1 | async-start | bytes 2162688 | tf_op jit(solution)/shard_map/all_to_all | solution.py:186
  42.4 8.8 %collective-permute-start.4 = (bf16[4,256,256]{2,1,0:T(8,128)(2,1)S(1)}, bf16[4,256,256]{2,1,0:T(8,128)(2,1)}, u32[]{:S(2)}, u32[]{:S(2)}) collective-permute-start(bf16[4,256,256]{2,1,0:T(8,128)(2,1)S(1)} %all-to-all-done.2.k_own), channel_id=1, source_target_pairs={{0,1},{1,0},{2,3},{3,2},{4,5},{5,4},{6,7},{7,6},{8,9},{9,8},{10,11... | collective-permute-start | bytes 1572872 | tf_op jit(solution)/shard_map/ppermute | solution.py:192
  42.4 18.1 %collective-permute-start.6 = (bf16[4,256,256]{2,1,0:T(8,128)(2,1)}, bf16[4,256,256]{2,1,0:T(8,128)(2,1)}, u32[]{:S(2)}, u32[]{:S(2)}) collective-permute-start(bf16[4,256,256]{2,1,0:T(8,128)(2,1)} %copy-done.1), channel_id=1, source_target_pairs={{0,8},{1,9},{2,10},{3,11},{4,12},{5,13},{6,14},{7,15},{8,16},{9,17... | collective-permute-start | bytes 1572872 | tf_op jit(solution)/shard_map/ppermute | solution.py:189
  48.0 14.0 %collective-permute-start.3 = (bf16[4,256,256]{2,1,0:T(8,128)(2,1)}, bf16[4,256,256]{2,1,0:T(8,128)(2,1)}, u32[]{:S(2)}, u32[]{:S(2)}) collective-permute-start(bf16[4,256,256]{2,1,0:T(8,128)(2,1)} %copy-done.1), channel_id=1, source_target_pairs={{0,1},{1,0},{2,3},{3,2},{4,5},{5,4},{6,7},{7,6},{8,9},{9,8},{10,11... | collective-permute-start | bytes 1572872 | tf_op jit(solution)/shard_map/ppermute | solution.py:192
  48.3 16.4 %collective-permute-start.2 = (bf16[4,256,256]{2,1,0:T(8,128)(2,1)}, bf16[4,256,256]{2,1,0:T(8,128)(2,1)}, u32[]{:S(2)}, u32[]{:S(2)}) collective-permute-start(bf16[4,256,256]{2,1,0:T(8,128)(2,1)} %collective-permute-done.1.k_own), channel_id=1, source_target_pairs={{0,1},{1,0},{2,3},{3,2},{4,5},{5,4},{6,7},{7,6},{8,9},{9,8},{10,11... | collective-permute-start | bytes 1572872 | tf_op jit(solution)/shard_map/ppermute | solution.py:192
  48.6 23.9 %collective-permute-start.7 = (bf16[4,256,256]{2,1,0:T(8,128)(2,1)}, bf16[4,256,256]{2,1,0:T(8,128)(2,1)}, u32[]{:S(2)}, u32[]{:S(2)}) collective-permute-start(bf16[4,256,256]{2,1,0:T(8,128)(2,1)} %collective-permute-done.1.k_own), channel_id=1, source_target_pairs={{0,8},{1,9},{2,10},{3,11},{4,12},{5,13},{6,14},{7,15},{8,16},{9,17... | collective-permute-start | bytes 1572872 | tf_op jit(solution)/shard_map/ppermute | solution.py:189
  51.1 21.3 %collective-permute-start.10 = (f32[1,2048]{1,0:T(1,128)S(1)}, f32[1,2048]{1,0:T(1,128)S(1)}, u32[]{:S(2)}, u32[]{:S(2)}) collective-permute-start(f32[1,2048]{1,0:T(1,128)S(1)} %copy-done.3), channel_id=1, source_target_pairs={{0,192},{64,0},{128,64},{192,128},{1,193},{65,1},{129,65},{193,129... | collective-permute-start | bytes 24584 | tf_op jit(solution)/shard_map/ppermute | solution.py:195
  54.0 10.7 %copy-start.2 = (bf16[4,256,256]{2,1,0:T(8,128)(2,1)S(1)}, bf16[4,256,256]{2,1,0:T(8,128)(2,1)}, u32[]{:S(2)}) copy-start(bf16[4,256,256]{2,1,0:T(8,128)(2,1)} %copy-done.1) | copy-start | bytes 1572868
  60.5 11.9 %collective-permute-start.8 = (f32[1,2048]{1,0:T(1,128)S(1)}, f32[1,2048]{1,0:T(1,128)S(1)}, u32[]{:S(2)}, u32[]{:S(2)}) collective-permute-start(f32[1,2048]{1,0:T(1,128)S(1)} %copy-done.3), channel_id=1, source_target_pairs={{0,64},{64,128},{128,192},{192,0},{1,65},{65,129},{129,193},{193,1... | collective-permute-start | bytes 24584 | tf_op jit(solution)/shard_map/ppermute | solution.py:195
  62.0 10.4 %collective-permute-start.9 = (f32[1,2048]{1,0:T(1,128)S(1)}, f32[1,2048]{1,0:T(1,128)S(1)}, u32[]{:S(2)}, u32[]{:S(2)}) collective-permute-start(f32[1,2048]{1,0:T(1,128)S(1)} %copy-done.3), channel_id=1, source_target_pairs={{0,128},{64,192},{128,0},{192,64},{1,129},{65,193},{129,1},{193,65... | collective-permute-start | bytes 24584 | tf_op jit(solution)/shard_map/ppermute | solution.py:195
  64.7 8.3 %collective-permute-start.12 = (bf16[4,256,256]{2,1,0:T(8,128)(2,1)}, bf16[4,256,256]{2,1,0:T(8,128)(2,1)S(1)}, u32[]{:S(2)}, u32[]{:S(2)}) collective-permute-start(bf16[4,256,256]{2,1,0:T(8,128)(2,1)} %collective-permute-done.6.v_own), channel_id=1, source_target_pairs={{0,1},{1,0},{2,3},{3,2},{4,5},{5,4},{6,7},{7,6},{8,9},{9,8},{10,11... | collective-permute-start | bytes 1572872 | tf_op jit(solution)/shard_map/ppermute | solution.py:192
  72.4 2.3 %collective-permute-start.11 = (bf16[4,256,256]{2,1,0:T(8,128)(2,1)}, bf16[4,256,256]{2,1,0:T(8,128)(2,1)S(1)}, u32[]{:S(2)}, u32[]{:S(2)}) collective-permute-start(bf16[4,256,256]{2,1,0:T(8,128)(2,1)} %collective-permute-done.7.k_own), channel_id=1, source_target_pairs={{0,1},{1,0},{2,3},{3,2},{4,5},{5,4},{6,7},{7,6},{8,9},{9,8},{10,11... | collective-permute-start | bytes 1572872 | tf_op jit(solution)/shard_map/ppermute | solution.py:192

commit v5 on v4

--- a/solution.py
+++ b/solution.py
@@ -42,9 +42,17 @@
     )
 
 
-def split_v_kernel(v_ref, vm_ref):
-    for h in range(HK):
-        vm_ref[h] = v_ref[:, h * HD : (h + 1) * HD]
+def split_v_kernel(v_ref, *out_refs):
+    y = lax.rem(lax.axis_index("seq") // 2, 4)
+    for i, out_ref in enumerate(out_refs):
+        lanes = pl.ds(pl.multiple_of(lax.rem(y + i, 4) * HD, HD), HD)
+        out_ref[...] = v_ref[:, lanes]
+
+
+def order_v_kernel(v0_ref, v1_ref, v2_ref, v3_ref, out_ref):
+    y = lax.rem(lax.axis_index("seq") // 2, 4)
+    for i, ref in enumerate((v0_ref, v1_ref, v2_ref, v3_ref)):
+        out_ref[lax.rem(y + 4 - i, 4)] = ref[...]
 
 
 def rotate_k_kernel(cos_ref, sin_ref, k_ref, km_ref):
@@ -195,13 +203,25 @@
         lax.ppermute(post_gain, "section", [(i, (i + r) % 4) for i in range(4)])
         for r in (1, 2, 3)
     ]
-    v_msg = pl.pallas_call(
+    pieces = pl.pallas_call(
         split_v_kernel,
-        out_shape=jax.ShapeDtypeStruct((HK, ROWS, HD), jnp.bfloat16),
+        out_shape=[jax.ShapeDtypeStruct((ROWS, HD), jnp.bfloat16)] * 4,
         in_specs=[vspec()],
-        out_specs=vspec(),
+        out_specs=[vspec()] * 4,
         name="split_v",
     )(values[0])
+    pieces = [pieces[0]] + [
+        lax.ppermute(pieces[i], "seq", [(d, d // 8 * 8 + (d + 2 * i) % 8) for d in range(64)])
+        for i in (1, 2, 3)
+    ]
+    v0 = pl.pallas_call(
+        order_v_kernel,
+        out_shape=jax.ShapeDtypeStruct((HK, ROWS, HD), jnp.bfloat16),
+        in_specs=[vspec()] * 4,
+        out_specs=vspec(),
+        compiler_params=pltpu.CompilerParams(vmem_limit_bytes=8 << 20),
+        name="order_v",
+    )(*pieces)
     k_msg = pl.pallas_call(
         rotate_k_kernel,
         out_shape=jax.ShapeDtypeStruct((HK, ROWS, HD), jnp.bfloat16),
@@ -218,8 +238,6 @@
     )(cosine, sine, places, queries[0])
 
     residual = lax.dynamic_slice_in_dim(residual_in, lax.axis_index("section") * 64, 64, 0)
-    v0 = over_y(v_msg)
-    v0, k_msg = lax.optimization_barrier((v0, k_msg))
     v1 = onward(v0)
     k0 = over_y(k_msg)
     k1 = onward(k0)

time: 123 us -> 120 us (0.976)
  waiting for transfers between devices: 11.9 us -> 7.11 us
    ppermute x0 -> x3, starting transfers between devices: none -> 5.83 us  [per_device(): lax.ppermute(pieces[i], 'seq', [(d, d // 8 * 8 + (d + 2 * i) % 8) for d i...]
    all_to_all x3 -> x2, waiting for transfers between devices: 9.08 us -> 4.6 us  [over_y(): return lax.all_to_all(x, 'seq', 0, 0, axis_index_groups=SHARED_Y)]
    all_to_all x3 -> x2, starting transfers between devices: 12.7 us -> 8.21 us  [over_y(): return lax.all_to_all(x, 'seq', 0, 0, axis_index_groups=SHARED_Y)]
  transfers between devices with their start and end apart: 16 -> 18, of which waited for: 5 -> 5; matrix products, arithmetic and copies ran while one was open for 2% -> 2% of each run, Pallas kernels for 15% -> 16%
where the time goes in v5:
time: 120 us; the launch traced here: 118 us
  starting transfers between devices  40.1 us (33%)
  blocking collectives  39.5 us (33%)
  Pallas kernels  27 us (22%)
  waiting for transfers between devices  7.11 us (6%)
  other arithmetic  2.68 us (2%)
  local copies, waits for them, and re-layouts  1.89 us (2%)
    all_to_all x1, blocking collectives, per_device(): lax.all_to_all(sent.reshape(16, 64, 512), ('section', 'seq'), 0, 0, axis_...  23.1 us
    pallas_call x3, Pallas kernels, attend(): pl.pallas_call(functools.partial(attend_kernel, back), out_shape=outs, in...  19.4 us
    ppermute x4, starting transfers between devices, onward(): return lax.ppermute(x, 'seq', NEXT_PLANE)  18.8 us
    all_to_all x1, blocking collectives, per_device(): mine = lax.all_to_all(back, 'section', 0, 0)  16.4 us
    all_to_all x2, starting transfers between devices, over_y(): return lax.all_to_all(x, 'seq', 0, 0, axis_index_groups=SHARED_Y)  8.21 us
    ppermute x3, starting transfers between devices, per_device(): lax.ppermute(post_gain, 'section', [(i, (i + r) % 4) for i in range(4)])  6 us
    ppermute x3, starting transfers between devices, per_device(): lax.ppermute(pieces[i], 'seq', [(d, d // 8 * 8 + (d + 2 * i) % 8) for d i...  5.83 us
    all_to_all x2, waiting for transfers between devices, over_y(): return lax.all_to_all(x, 'seq', 0, 0, axis_index_groups=SHARED_Y)  4.6 us
  transfers between devices with their start and end apart: 18, of which 5 were waited for; matrix products, arithmetic and copies ran while one was open for 2% of the time, Pallas kernels for 16%

profile of v5, /device:TPU:96, one launch (start us, length us, event | category | flops | bytes accessed | tf_op | source)
XLA Modules:
  0.0 118.5 jit_solution(1193345508289241048)
XLA Ops:
  0.0 2.0 %split_v.1 = (bf16[256,256]{1,0:T(8,128)(2,1)}, bf16[256,256]{1,0:T(8,128)(2,1)}, bf16[256,256]{1,0:T(8,128)(2,1)}, bf16[256,256]{1,0:T(8,128)(2,1)}) custom-call(bf16[256,1024]{1,0:T(8,128)(2,1)} %bitcast.8), custom_call_target="tpu_custom_call" | custom-call | tf_op jit(solution)/shard_map/split_v/pallas_call | solution.py:206
  2.0 1.6 %collective-permute-start = (bf16[256,256]{1,0:T(8,128)(2,1)}, bf16[256,256]{1,0:T(8,128)(2,1)S(1)}, u32[]{:S(2)}, u32[]{:S(2)}) collective-permute-start(bf16[256,256]{1,0:T(8,128)(2,1)} %get-tuple-element.27), channel_id=1, source_target_pairs={{0,2},{1,3},{2,4},{3,5},{4,6},{5,7},{6,0},{7,1},{8,10},{9,11},{10,... | collective-permute-start | bytes 393224 | tf_op jit(solution)/shard_map/ppermute | solution.py:214
  3.6 2.9 %collective-permute-start.1 = (bf16[256,256]{1,0:T(8,128)(2,1)}, bf16[256,256]{1,0:T(8,128)(2,1)S(1)}, u32[]{:S(2)}, u32[]{:S(2)}) collective-permute-start(bf16[256,256]{1,0:T(8,128)(2,1)} %get-tuple-element.28), channel_id=1, source_target_pairs={{0,4},{1,5},{2,6},{3,7},{4,0},{5,1},{6,2},{7,3},{8,12},{9,13},{10,... | collective-permute-start | bytes 393224 | tf_op jit(solution)/shard_map/ppermute | solution.py:214
  6.5 1.3 %collective-permute-start.2 = (bf16[256,256]{1,0:T(8,128)(2,1)}, bf16[256,256]{1,0:T(8,128)(2,1)S(1)}, u32[]{:S(2)}, u32[]{:S(2)}) collective-permute-start(bf16[256,256]{1,0:T(8,128)(2,1)} %get-tuple-element.29), channel_id=1, source_target_pairs={{0,6},{1,7},{2,0},{3,1},{4,2},{5,3},{6,4},{7,5},{8,14},{9,15},{10,... | collective-permute-start | bytes 393224 | tf_op jit(solution)/shard_map/ppermute | solution.py:214
  7.9 0.8 shift-right-logical_convert_fusion
  8.6 1.2 %multiply_sine_fusion = (f32[256,128]{1,0:T(8,128)}, f32[256,128]{1,0:T(8,128)}) fusion(f32[128]{0:T(128)S(1)} %multiply_exponential_fusion, f32[256]{0:T(256)S(1)} %get-tuple-element.50), kind=kLoop, calls=%fused_computation | loop fusion | flops 32768 | bytes 263680 | tf_op jit(solution)/shard_map/sin | solution.py:189
  9.9 2.2 %rotate_k.1 = bf16[4,256,256]{2,1,0:T(8,128)(2,1)} custom-call(f32[256,128]{1,0:T(8,128)} %get-tuple-element.48.cos_ref, f32[256,128]{1,0:T(8,128)} %get-tuple-element.47.sin_ref, bf16[256,1024]{1,0:T(8,128)(2,1)} %bitcast.9), custom_call_target="tpu_custom_call" | custom-call | tf_op jit(solution)/shard_map/rotate_k/pallas_call | solution.py:225
  12.0 3.5 %all-to-all-start.1 = ((bf16[4,256,256]{2,1,0:T(8,128)(2,1)}), bf16[4,256,256]{2,1,0:T(8,128)(2,1)S(1)}, u32[]{:S(2)}, u32[]{:S(2)}) async-start(bf16[4,256,256]{2,1,0:T(8,128)(2,1)} %rotate_k.1), calls=%async_computation.1 | async-start | bytes 1048576 | tf_op jit(solution)/shard_map/all_to_all | solution.py:194
  15.5 0.0 collective-permute-done.v1_ref
  15.5 0.0 collective-permute-done.1.v2_ref
  15.5 0.0 collective-permute-done.2.v3_ref
  15.6 0.1 order_v.1.v_own
  15.6 5.0 %collective-permute-start.3 = (bf16[4,256,256]{2,1,0:T(8,128)(2,1)S(1)}, bf16[4,256,256]{2,1,0:T(8,128)(2,1)S(1)}, u32[]{:S(2)}, u32[]{:S(2)}) collective-permute-start(bf16[4,256,256]{2,1,0:T(8,128)(2,1)S(1)} %order_v.1.v_own), channel_id=1, source_target_pairs={{0,8},{1,9},{2,10},{3,11},{4,12},{5,13},{6,14},{7,15},{8,16},{9,17... | collective-permute-start | bytes 1572872 | tf_op jit(solution)/shard_map/ppermute | solution.py:197
  20.7 0.1 pad.2.clone
  20.8 0.0 collective-permute-start.8
  20.8 3.6 %all-to-all-done.1.k_own = bf16[4,256,256]{2,1,0:T(8,128)(2,1)S(1)} async-done(((bf16[4,256,256]{2,1,0:T(8,128)(2,1)}), bf16[4,256,256]{2,1,0:T(8,128)(2,1)S(1)}, u32[]{:S(2)}, u32[]{:S(2)}) %all-to-all-start.1) | async-done | bytes 524320 | tf_op jit(solution)/shard_map/all_to_all | solution.py:194
  24.4 5.0 %collective-permute-start.4 = (bf16[4,256,256]{2,1,0:T(8,128)(2,1)S(1)}, bf16[4,256,256]{2,1,0:T(8,128)(2,1)}, u32[]{:S(2)}, u32[]{:S(2)}) collective-permute-start(bf16[4,256,256]{2,1,0:T(8,128)(2,1)S(1)} %all-to-all-done.1.k_own), channel_id=1, source_target_pairs={{0,8},{1,9},{2,10},{3,11},{4,12},{5,13},{6,14},{7,15},{8,16},{9,17... | collective-permute-start | bytes 1572872 | tf_op jit(solution)/shard_map/ppermute | solution.py:197
  29.4 0.7 maximum_maximum_fusion.place_ref
  30.1 2.8 %rotate_q.1 = bf16[4,528,256]{2,1,0:T(8,128)(2,1)} custom-call(f32[256,128]{1,0:T(8,128)} %get-tuple-element.48.cos_ref, f32[256,128]{1,0:T(8,128)} %get-tuple-element.47.sin_ref, bf16[16,256]{1,0:T(8,128)(2,1)} %maximum_maximum_fusion.place_ref, bf16[256,2048]{1,0:T(8,128)(2,1)} %bitcast.7), custom_call_target="tpu_custom_call" | custom-call | tf_op jit(solution)/shard_map/rotate_q/pallas_call | solution.py:232
  32.9 0.1 collective-permute-done.3.v_own
  33.0 0.8 copy-done.1
  33.8 4.7 %all-to-all-start = ((bf16[4,528,256]{2,1,0:T(8,128)(2,1)}), bf16[4,528,256]{2,1,0:T(8,128)(2,1)S(1)}, u32[]{:S(2)}, u32[]{:S(2)}) async-start(bf16[4,528,256]{2,1,0:T(8,128)(2,1)} %rotate_q.1), calls=%async_computation | async-start | bytes 2162688 | tf_op jit(solution)/shard_map/all_to_all | solution.py:194
  38.6 0.0 collective-permute-start.7
  38.6 5.6 %collective-permute-start.9 = (bf16[4,256,256]{2,1,0:T(8,128)(2,1)}, bf16[4,256,256]{2,1,0:T(8,128)(2,1)}, u32[]{:S(2)}, u32[]{:S(2)}) collective-permute-start(bf16[4,256,256]{2,1,0:T(8,128)(2,1)} %copy-done.1), channel_id=1, source_target_pairs={{0,8},{1,9},{2,10},{3,11},{4,12},{5,13},{6,14},{7,15},{8,16},{9,17... | collective-permute-start | bytes 1572872 | tf_op jit(solution)/shard_map/ppermute | solution.py:197
  44.2 0.3 collective-permute-start.6
  44.5 0.3 collective-permute-start.5
  44.8 0.0 collective-permute-done.8.v_oth
  44.8 3.2 %collective-permute-start.10 = (bf16[4,256,256]{2,1,0:T(8,128)(2,1)}, bf16[4,256,256]{2,1,0:T(8,128)(2,1)}, u32[]{:S(2)}, u32[]{:S(2)}) collective-permute-start(bf16[4,256,256]{2,1,0:T(8,128)(2,1)} %collective-permute-done.4.k_own), channel_id=1, source_target_pairs={{0,8},{1,9},{2,10},{3,11},{4,12},{5,13},{6,14},{7,15},{8,16},{9,17... | collective-permute-start | bytes 1572872 | tf_op jit(solution)/shard_map/ppermute | solution.py:197
  48.0 1.6 %collective-permute-start.11 = (f32[1,2048]{1,0:T(1,128)S(1)}, f32[1,2048]{1,0:T(1,128)S(1)}, u32[]{:S(2)}, u32[]{:S(2)}) collective-permute-start(f32[1,2048]{1,0:T(1,128)S(1)} %copy-done.4), channel_id=1, source_target_pairs={{0,64},{64,128},{128,192},{192,0},{1,65},{65,129},{129,193},{193,1... | collective-permute-start | bytes 24584 | tf_op jit(solution)/shard_map/ppermute | solution.py:203
  49.6 1.0 all-to-all-done.q_ref
  50.6 6.2 %attend_0.1 = (f32[4,512,256]{2,1,0:T(8,128)S(1)}, f32[4,512,128]{2,1,0:T(8,128)S(1)}) custom-call(bf16[4,528,256]{2,1,0:T(8,128)(2,1)S(1)} %all-to-all-done.q_ref, bf16[4,256,256]{2,1,0:T(8,128)(2,1)S(1)} %all-to-all-done.1.k_own, bf16[4,256,256]{2,1,0:T(8,128)(2,1)} %collective-permute-done.7.k_oth, bf16[4,256,256]{2,1,0:T(8,128)(2,1)S(1)} %order_v.1.v_own, ...), custom_call_target="tpu_custom_call" | custom-call | flops 536870912 | bytes 65536 | tf_op jit(solution)/shard_map/attend_0/pallas_call | solution.py:153
  56.8 3.3 %collective-permute-start.12 = (f32[1,2048]{1,0:T(1,128)S(1)}, f32[1,2048]{1,0:T(1,128)S(1)}, u32[]{:S(2)}, u32[]{:S(2)}) collective-permute-start(f32[1,2048]{1,0:T(1,128)S(1)} %copy-done.4), channel_id=1, source_target_pairs={{0,128},{64,192},{128,0},{192,64},{1,129},{65,193},{129,1},{193,65... | collective-permute-start | bytes 24584 | tf_op jit(solution)/shard_map/ppermute | solution.py:203
  60.1 0.0 collective-permute-done.6.v_oth
  60.1 1.1 collective-permute-start.13
  61.2 0.0 collective-permute-done.5.k_oth
  61.2 7.7 %attend_1.1 = (f32[4,512,256]{2,1,0:T(8,128)S(1)}, f32[4,512,128]{2,1,0:T(8,128)S(1)}) custom-call(bf16[4,528,256]{2,1,0:T(8,128)(2,1)S(1)} %all-to-all-done.q_ref, bf16[4,256,256]{2,1,0:T(8,128)(2,1)} %collective-permute-done.4.k_own, bf16[4,256,256]{2,1,0:T(8,128)(2,1)} %collective-permute-done.5.k_oth, ...), custom_call_target="tpu_custom_call", output_to_operand_aliasing={{0}: (5, {}), {1}: (6, {})} | custom-call | flops 858993472 | bytes 65536 | tf_op jit(solution)/shard_map/attend_1/pallas_call | solution.py:153
  68.9 0.0 collective-permute-done.11.g1_ref
  68.9 0.0 collective-permute-done.13.g3_ref
  68.9 0.0 collective-permute-done.10.k_own
  68.9 0.1 collective-permute-start.14
  69.0 0.5 collective-permute-start.15
  69.5 1.6 %collective-permute-done.14.k_oth = bf16[4,256,256]{2,1,0:T(8,128)(2,1)S(1)} collective-permute-done((bf16[4,256,256]{2,1,0:T(8,128)(2,1)}, bf16[4,256,256]{2,1,0:T(8,128)(2,1)S(1)}, u32[]{:S(2)}, u32[]{:S(2)}) %collective-permute-start.14) | collective-permute-done | bytes 524320 | tf_op jit(solution)/shard_map/ppermute | solution.py:200
  71.1 0.7 collective-permute-done.15.v_oth
  71.9 5.6 %attend_2.1 = bf16[4,4,64,512]{3,2,1,0:T(8,128)(2,1)S(1)} custom-call(bf16[4,528,256]{2,1,0:T(8,128)(2,1)S(1)} %all-to-all-done.q_ref, bf16[4,256,256]{2,1,0:T(8,128)(2,1)} %collective-permute-done.10.k_own, bf16[4,256,256]{2,1,0:T(8,128)(2,1)S(1)} %collective-permute-done.14.k_oth, bf16[4,256,256]{2,1,0:T(8,128)(2,1)} %collective-permute-done.9.v_own, ...), custom_call_target="tpu_custom_call" | custom-call | flops 536870912 | bytes 65536 | tf_op jit(solution)/shard_map/attend_2/pallas_call | solution.py:153
  77.5 23.1 %all_to_all.20.got_ref = bf16[16,64,512]{2,1,0:T(8,128)(2,1)S(1)} all-to-all(bf16[16,64,512]{2,1,0:T(8,128)(2,1)S(1)} %bitcast.5), channel_id=1, replica_groups={{0,2,4,6,64,66,68,70,128,130,132,134,192,194,196,198},{1,3,5,7,65,67,69..., dimensions={0} | all-to-all | bytes 2097152 | tf_op jit(solution)/shard_map/all_to_all | solution.py:254
  100.6 0.5 combine.1
  101.1 16.4 %all_to_all.21 = bf16[4,64,2048]{2,1,0:T(8,128)(2,1)S(1)} all-to-all(bf16[4,64,2048]{2,1,0:T(8,128)(2,1)S(1)} %combine.1), channel_id=1, replica_groups=mesh['section'=4,'seq'=64] {'section'}, dimensions={0} | all-to-all | bytes 2097152 | tf_op jit(solution)/shard_map/all_to_all | solution.py:266
  117.5 1.0 copy.12
  (18 shorter events, 0.1 us)
Async XLA Ops:
  0.0 47.9 %copy-start = (bf16[256,2048]{1,0:T(8,128)(2,1)S(1)}, bf16[256,2048]{1,0:T(8,128)(2,1)}, u32[]{:S(2)}) copy-start(bf16[256,2048]{1,0:T(8,128)(2,1)} %param.11) | copy-start | bytes 3145732
  2.0 13.5 %copy-start.3 = (bf16[256,256]{1,0:T(8,128)(2,1)S(1)}, bf16[256,256]{1,0:T(8,128)(2,1)}, u32[]{:S(2)}) copy-start(bf16[256,256]{1,0:T(8,128)(2,1)} %get-tuple-element.26.v0_ref) | copy-start | bytes 393220
  2.0 13.5 %collective-permute-start = (bf16[256,256]{1,0:T(8,128)(2,1)}, bf16[256,256]{1,0:T(8,128)(2,1)S(1)}, u32[]{:S(2)}, u32[]{:S(2)}) collective-permute-start(bf16[256,256]{1,0:T(8,128)(2,1)} %get-tuple-element.27), channel_id=1, source_target_pairs={{0,2},{1,3},{2,4},{3,5},{4,6},{5,7},{6,0},{7,1},{8,10},{9,11},{10,... | collective-permute-start | bytes 393224 | tf_op jit(solution)/shard_map/ppermute | solution.py:214
  3.6 11.9 %collective-permute-start.1 = (bf16[256,256]{1,0:T(8,128)(2,1)}, bf16[256,256]{1,0:T(8,128)(2,1)S(1)}, u32[]{:S(2)}, u32[]{:S(2)}) collective-permute-start(bf16[256,256]{1,0:T(8,128)(2,1)} %get-tuple-element.28), channel_id=1, source_target_pairs={{0,4},{1,5},{2,6},{3,7},{4,0},{5,1},{6,2},{7,3},{8,12},{9,13},{10,... | collective-permute-start | bytes 393224 | tf_op jit(solution)/shard_map/ppermute | solution.py:214
  6.5 9.0 %collective-permute-start.2 = (bf16[256,256]{1,0:T(8,128)(2,1)}, bf16[256,256]{1,0:T(8,128)(2,1)S(1)}, u32[]{:S(2)}, u32[]{:S(2)}) collective-permute-start(bf16[256,256]{1,0:T(8,128)(2,1)} %get-tuple-element.29), channel_id=1, source_target_pairs={{0,6},{1,7},{2,0},{3,1},{4,2},{5,3},{6,4},{7,5},{8,14},{9,15},{10,... | collective-permute-start | bytes 393224 | tf_op jit(solution)/shard_map/ppermute | solution.py:214
  12.0 12.4 %all-to-all-start.1 = ((bf16[4,256,256]{2,1,0:T(8,128)(2,1)}), bf16[4,256,256]{2,1,0:T(8,128)(2,1)S(1)}, u32[]{:S(2)}, u32[]{:S(2)}) async-start(bf16[4,256,256]{2,1,0:T(8,128)(2,1)} %rotate_k.1), calls=%async_computation.1 | async-start | bytes 1048576 | tf_op jit(solution)/shard_map/all_to_all | solution.py:194
  15.6 17.4 %collective-permute-start.3 = (bf16[4,256,256]{2,1,0:T(8,128)(2,1)S(1)}, bf16[4,256,256]{2,1,0:T(8,128)(2,1)S(1)}, u32[]{:S(2)}, u32[]{:S(2)}) collective-permute-start(bf16[4,256,256]{2,1,0:T(8,128)(2,1)S(1)} %order_v.1.v_own), channel_id=1, source_target_pairs={{0,8},{1,9},{2,10},{3,11},{4,12},{5,13},{6,14},{7,15},{8,16},{9,17... | collective-permute-start | bytes 1572872 | tf_op jit(solution)/shard_map/ppermute | solution.py:197
  20.8 24.0 %collective-permute-start.8 = (bf16[4,256,256]{2,1,0:T(8,128)(2,1)S(1)}, bf16[4,256,256]{2,1,0:T(8,128)(2,1)}, u32[]{:S(2)}, u32[]{:S(2)}) collective-permute-start(bf16[4,256,256]{2,1,0:T(8,128)(2,1)S(1)} %order_v.1.v_own), channel_id=1, source_target_pairs={{0,1},{1,0},{2,3},{3,2},{4,5},{5,4},{6,7},{7,6},{8,9},{9,8},{10,11... | collective-permute-start | bytes 1572872 | tf_op jit(solution)/shard_map/ppermute | solution.py:200
  24.4 20.1 %collective-permute-start.4 = (bf16[4,256,256]{2,1,0:T(8,128)(2,1)S(1)}, bf16[4,256,256]{2,1,0:T(8,128)(2,1)}, u32[]{:S(2)}, u32[]{:S(2)}) collective-permute-start(bf16[4,256,256]{2,1,0:T(8,128)(2,1)S(1)} %all-to-all-done.1.k_own), channel_id=1, source_target_pairs={{0,8},{1,9},{2,10},{3,11},{4,12},{5,13},{6,14},{7,15},{8,16},{9,17... | collective-permute-start | bytes 1572872 | tf_op jit(solution)/shard_map/ppermute | solution.py:197
  30.1 17.9 %copy-start.4 = (f32[1,2048]{1,0:T(1,128)S(1)}, f32[1,2048]{1,0:T(1,128)}, u32[]{:S(2)}) copy-start(f32[1,2048]{1,0:T(1,128)} %g0_ref) | copy-start | bytes 24580
  33.0 0.8 copy-start.1
  33.8 16.8 %all-to-all-start = ((bf16[4,528,256]{2,1,0:T(8,128)(2,1)}), bf16[4,528,256]{2,1,0:T(8,128)(2,1)S(1)}, u32[]{:S(2)}, u32[]{:S(2)}) async-start(bf16[4,528,256]{2,1,0:T(8,128)(2,1)} %rotate_q.1), calls=%async_computation | async-start | bytes 2162688 | tf_op jit(solution)/shard_map/all_to_all | solution.py:194
  38.6 9.4 %collective-permute-start.7 = (bf16[4,256,256]{2,1,0:T(8,128)(2,1)S(1)}, bf16[4,256,256]{2,1,0:T(8,128)(2,1)}, u32[]{:S(2)}, u32[]{:S(2)}) collective-permute-start(bf16[4,256,256]{2,1,0:T(8,128)(2,1)S(1)} %all-to-all-done.1.k_own), channel_id=1, source_target_pairs={{0,1},{1,0},{2,3},{3,2},{4,5},{5,4},{6,7},{7,6},{8,9},{9,8},{10,11... | collective-permute-start | bytes 1572872 | tf_op jit(solution)/shard_map/ppermute | solution.py:200
  38.6 18.2 %collective-permute-start.9 = (bf16[4,256,256]{2,1,0:T(8,128)(2,1)}, bf16[4,256,256]{2,1,0:T(8,128)(2,1)}, u32[]{:S(2)}, u32[]{:S(2)}) collective-permute-start(bf16[4,256,256]{2,1,0:T(8,128)(2,1)} %copy-done.1), channel_id=1, source_target_pairs={{0,8},{1,9},{2,10},{3,11},{4,12},{5,13},{6,14},{7,15},{8,16},{9,17... | collective-permute-start | bytes 1572872 | tf_op jit(solution)/shard_map/ppermute | solution.py:197
  44.2 15.9 %collective-permute-start.6 = (bf16[4,256,256]{2,1,0:T(8,128)(2,1)}, bf16[4,256,256]{2,1,0:T(8,128)(2,1)}, u32[]{:S(2)}, u32[]{:S(2)}) collective-permute-start(bf16[4,256,256]{2,1,0:T(8,128)(2,1)} %copy-done.1), channel_id=1, source_target_pairs={{0,1},{1,0},{2,3},{3,2},{4,5},{5,4},{6,7},{7,6},{8,9},{9,8},{10,11... | collective-permute-start | bytes 1572872 | tf_op jit(solution)/shard_map/ppermute | solution.py:200
  44.5 16.7 %collective-permute-start.5 = (bf16[4,256,256]{2,1,0:T(8,128)(2,1)}, bf16[4,256,256]{2,1,0:T(8,128)(2,1)}, u32[]{:S(2)}, u32[]{:S(2)}) collective-permute-start(bf16[4,256,256]{2,1,0:T(8,128)(2,1)} %collective-permute-done.4.k_own), channel_id=1, source_target_pairs={{0,1},{1,0},{2,3},{3,2},{4,5},{5,4},{6,7},{7,6},{8,9},{9,8},{10,11... | collective-permute-start | bytes 1572872 | tf_op jit(solution)/shard_map/ppermute | solution.py:200
  44.8 24.1 %collective-permute-start.10 = (bf16[4,256,256]{2,1,0:T(8,128)(2,1)}, bf16[4,256,256]{2,1,0:T(8,128)(2,1)}, u32[]{:S(2)}, u32[]{:S(2)}) collective-permute-start(bf16[4,256,256]{2,1,0:T(8,128)(2,1)} %collective-permute-done.4.k_own), channel_id=1, source_target_pairs={{0,8},{1,9},{2,10},{3,11},{4,12},{5,13},{6,14},{7,15},{8,16},{9,17... | collective-permute-start | bytes 1572872 | tf_op jit(solution)/shard_map/ppermute | solution.py:197
  48.0 20.9 %collective-permute-start.11 = (f32[1,2048]{1,0:T(1,128)S(1)}, f32[1,2048]{1,0:T(1,128)S(1)}, u32[]{:S(2)}, u32[]{:S(2)}) collective-permute-start(f32[1,2048]{1,0:T(1,128)S(1)} %copy-done.4), channel_id=1, source_target_pairs={{0,64},{64,128},{128,192},{192,0},{1,65},{65,129},{129,193},{193,1... | collective-permute-start | bytes 24584 | tf_op jit(solution)/shard_map/ppermute | solution.py:203
  50.6 10.6 %copy-start.2 = (bf16[4,256,256]{2,1,0:T(8,128)(2,1)S(1)}, bf16[4,256,256]{2,1,0:T(8,128)(2,1)}, u32[]{:S(2)}) copy-start(bf16[4,256,256]{2,1,0:T(8,128)(2,1)} %copy-done.1) | copy-start | bytes 1572868
  56.8 12.1 %collective-permute-start.12 = (f32[1,2048]{1,0:T(1,128)S(1)}, f32[1,2048]{1,0:T(1,128)S(1)}, u32[]{:S(2)}, u32[]{:S(2)}) collective-permute-start(f32[1,2048]{1,0:T(1,128)S(1)} %copy-done.4), channel_id=1, source_target_pairs={{0,128},{64,192},{128,0},{192,64},{1,129},{65,193},{129,1},{193,65... | collective-permute-start | bytes 24584 | tf_op jit(solution)/shard_map/ppermute | solution.py:203
  60.1 8.8 %collective-permute-start.13 = (f32[1,2048]{1,0:T(1,128)S(1)}, f32[1,2048]{1,0:T(1,128)S(1)}, u32[]{:S(2)}, u32[]{:S(2)}) collective-permute-start(f32[1,2048]{1,0:T(1,128)S(1)} %copy-done.4), channel_id=1, source_target_pairs={{0,192},{64,0},{128,64},{192,128},{1,193},{65,1},{129,65},{193,129... | collective-permute-start | bytes 24584 | tf_op jit(solution)/shard_map/ppermute | solution.py:203
  68.9 2.2 %collective-permute-start.14 = (bf16[4,256,256]{2,1,0:T(8,128)(2,1)}, bf16[4,256,256]{2,1,0:T(8,128)(2,1)S(1)}, u32[]{:S(2)}, u32[]{:S(2)}) collective-permute-start(bf16[4,256,256]{2,1,0:T(8,128)(2,1)} %collective-permute-done.10.k_own), channel_id=1, source_target_pairs={{0,1},{1,0},{2,3},{3,2},{4,5},{5,4},{6,7},{7,6},{8,9},{9,8},{10,11... | collective-permute-start | bytes 1572872 | tf_op jit(solution)/shard_map/ppermute | solution.py:200
  69.0 2.9 %collective-permute-start.15 = (bf16[4,256,256]{2,1,0:T(8,128)(2,1)}, bf16[4,256,256]{2,1,0:T(8,128)(2,1)S(1)}, u32[]{:S(2)}, u32[]{:S(2)}) collective-permute-start(bf16[4,256,256]{2,1,0:T(8,128)(2,1)} %collective-permute-done.9.v_own), channel_id=1, source_target_pairs={{0,1},{1,0},{2,3},{3,2},{4,5},{5,4},{6,7},{7,6},{8,9},{9,8},{10,11... | collective-permute-start | bytes 1572872 | tf_op jit(solution)/shard_map/ppermute | solution.py:200

commit v6 on v5

--- a/solution.py
+++ b/solution.py
@@ -240,12 +240,12 @@
     residual = lax.dynamic_slice_in_dim(residual_in, lax.axis_index("section") * 64, 64, 0)
     v1 = onward(v0)
     k0 = over_y(k_msg)
+    k0, q_msg = lax.optimization_barrier((k0, q_msg))
     k1 = onward(k0)
     v1, q_msg = lax.optimization_barrier((v1, q_msg))
     query = over_y(q_msg)
     v2 = onward(v1)
     k2 = onward(k1)
-
     num, den = attend(0, query, k0, other(k0), v0, other(v0), None, None)
     num, den, v2 = lax.optimization_barrier((num, den, v2))
     num, den = attend(1, query, k1, other(k1), v1, other(v1), num, den)

time: 120 us -> 120 us (level)
    all_to_all x2, waiting for transfers between devices: 4.6 us -> 0.79 us  [over_y(): return lax.all_to_all(x, 'seq', 0, 0, axis_index_groups=SHARED_Y)]
    ppermute x4, waiting for transfers between devices: 0.12 us -> 3.81 us  [onward(): return lax.ppermute(x, 'seq', NEXT_PLANE)]
  transfers between devices with their start and end apart: 18 -> 18, of which waited for: 5 -> 6; matrix products, arithmetic and copies ran while one was open for 2% -> 2% of each run, Pallas kernels for 16% -> 16%
where the time goes in v6:
time: 120 us; the launch traced here: 118 us
  starting transfers between devices  39.9 us (33%)
  blocking collectives  39.8 us (33%)
  Pallas kernels  27 us (22%)
  waiting for transfers between devices  6.98 us (6%)
  other arithmetic  2.68 us (2%)
  local copies, waits for them, and re-layouts  1.89 us (2%)
    all_to_all x1, blocking collectives, per_device(): lax.all_to_all(sent.reshape(16, 64, 512), ('section', 'seq'), 0, 0, axis_...  23.4 us
    pallas_call x3, Pallas kernels, attend(): pl.pallas_call(functools.partial(attend_kernel, back), out_shape=outs, in...  19.4 us
    ppermute x4, starting transfers between devices, onward(): return lax.ppermute(x, 'seq', NEXT_PLANE)  18.8 us
    all_to_all x1, blocking collectives, per_device(): mine = lax.all_to_all(back, 'section', 0, 0)  16.4 us
    all_to_all x2, starting transfers between devices, over_y(): return lax.all_to_all(x, 'seq', 0, 0, axis_index_groups=SHARED_Y)  8.21 us
    ppermute x3, starting transfers between devices, per_device(): lax.ppermute(pieces[i], 'seq', [(d, d // 8 * 8 + (d + 2 * i) % 8) for d i...  5.83 us
    ppermute x3, starting transfers between devices, per_device(): lax.ppermute(post_gain, 'section', [(i, (i + r) % 4) for i in range(4)])  5.73 us
    ppermute x4, waiting for transfers between devices, onward(): return lax.ppermute(x, 'seq', NEXT_PLANE)  3.81 us
  transfers between devices with their start and end apart: 18, of which 6 were waited for; matrix products, arithmetic and copies ran while one was open for 2% of the time, Pallas kernels for 16%

profile of v6, /device:TPU:96, one launch (start us, length us, event | category | flops | bytes accessed | tf_op | source)
XLA Modules:
  0.0 118.5 jit_solution(1561751506867749292)
XLA Ops:
  0.0 2.0 %split_v.1 = (bf16[256,256]{1,0:T(8,128)(2,1)}, bf16[256,256]{1,0:T(8,128)(2,1)}, bf16[256,256]{1,0:T(8,128)(2,1)}, bf16[256,256]{1,0:T(8,128)(2,1)}) custom-call(bf16[256,1024]{1,0:T(8,128)(2,1)} %bitcast.8), custom_call_target="tpu_custom_call" | custom-call | tf_op jit(solution)/shard_map/split_v/pallas_call | solution.py:206
  2.0 1.6 %collective-permute-start = (bf16[256,256]{1,0:T(8,128)(2,1)}, bf16[256,256]{1,0:T(8,128)(2,1)S(1)}, u32[]{:S(2)}, u32[]{:S(2)}) collective-permute-start(bf16[256,256]{1,0:T(8,128)(2,1)} %get-tuple-element.29), channel_id=1, source_target_pairs={{0,2},{1,3},{2,4},{3,5},{4,6},{5,7},{6,0},{7,1},{8,10},{9,11},{10,... | collective-permute-start | bytes 393224 | tf_op jit(solution)/shard_map/ppermute | solution.py:214
  3.6 2.9 %collective-permute-start.1 = (bf16[256,256]{1,0:T(8,128)(2,1)}, bf16[256,256]{1,0:T(8,128)(2,1)S(1)}, u32[]{:S(2)}, u32[]{:S(2)}) collective-permute-start(bf16[256,256]{1,0:T(8,128)(2,1)} %get-tuple-element.30), channel_id=1, source_target_pairs={{0,4},{1,5},{2,6},{3,7},{4,0},{5,1},{6,2},{7,3},{8,12},{9,13},{10,... | collective-permute-start | bytes 393224 | tf_op jit(solution)/shard_map/ppermute | solution.py:214
  6.5 1.3 %collective-permute-start.2 = (bf16[256,256]{1,0:T(8,128)(2,1)}, bf16[256,256]{1,0:T(8,128)(2,1)S(1)}, u32[]{:S(2)}, u32[]{:S(2)}) collective-permute-start(bf16[256,256]{1,0:T(8,128)(2,1)} %get-tuple-element.31), channel_id=1, source_target_pairs={{0,6},{1,7},{2,0},{3,1},{4,2},{5,3},{6,4},{7,5},{8,14},{9,15},{10,... | collective-permute-start | bytes 393224 | tf_op jit(solution)/shard_map/ppermute | solution.py:214
  7.9 0.8 shift-right-logical_convert_fusion
  8.6 1.2 %multiply_sine_fusion = (f32[256,128]{1,0:T(8,128)}, f32[256,128]{1,0:T(8,128)}) fusion(f32[128]{0:T(128)S(1)} %multiply_exponential_fusion, f32[256]{0:T(256)S(1)} %get-tuple-element.54), kind=kLoop, calls=%fused_computation | loop fusion | flops 32768 | bytes 263680 | tf_op jit(solution)/shard_map/sin | solution.py:189
  9.9 2.2 %rotate_k.1 = bf16[4,256,256]{2,1,0:T(8,128)(2,1)} custom-call(f32[256,128]{1,0:T(8,128)} %get-tuple-element.52.cos_ref, f32[256,128]{1,0:T(8,128)} %get-tuple-element.51.sin_ref, bf16[256,1024]{1,0:T(8,128)(2,1)} %bitcast.9), custom_call_target="tpu_custom_call" | custom-call | tf_op jit(solution)/shard_map/rotate_k/pallas_call | solution.py:225
  12.0 3.5 %all-to-all-start = ((bf16[4,256,256]{2,1,0:T(8,128)(2,1)}), bf16[4,256,256]{2,1,0:T(8,128)(2,1)S(1)}, u32[]{:S(2)}, u32[]{:S(2)}) async-start(bf16[4,256,256]{2,1,0:T(8,128)(2,1)} %rotate_k.1), calls=%async_computation | async-start | bytes 1048576 | tf_op jit(solution)/shard_map/all_to_all | solution.py:194
  15.5 0.0 collective-permute-done.v1_ref
  15.5 0.0 collective-permute-done.1.v2_ref
  15.5 0.0 collective-permute-done.2.v3_ref
  15.6 0.1 order_v.1.v_own
  15.6 5.0 %collective-permute-start.3 = (bf16[4,256,256]{2,1,0:T(8,128)(2,1)S(1)}, bf16[4,256,256]{2,1,0:T(8,128)(2,1)S(1)}, u32[]{:S(2)}, u32[]{:S(2)}) collective-permute-start(bf16[4,256,256]{2,1,0:T(8,128)(2,1)S(1)} %order_v.1.v_own), channel_id=1, source_target_pairs={{0,8},{1,9},{2,10},{3,11},{4,12},{5,13},{6,14},{7,15},{8,16},{9,17... | collective-permute-start | bytes 1572872 | tf_op jit(solution)/shard_map/ppermute | solution.py:197
  20.7 0.1 pad.2.clone
  20.8 0.7 maximum_maximum_fusion.place_ref
  21.5 2.8 %rotate_q.1 = bf16[4,528,256]{2,1,0:T(8,128)(2,1)} custom-call(f32[256,128]{1,0:T(8,128)} %get-tuple-element.52.cos_ref, f32[256,128]{1,0:T(8,128)} %get-tuple-element.51.sin_ref, bf16[16,256]{1,0:T(8,128)(2,1)} %maximum_maximum_fusion.place_ref, bf16[256,2048]{1,0:T(8,128)(2,1)} %bitcast.7), custom_call_target="tpu_custom_call" | custom-call | tf_op jit(solution)/shard_map/rotate_q/pallas_call | solution.py:232
  24.3 0.1 all-to-all-done.k_own
  24.4 5.0 %collective-permute-start.4 = (bf16[4,256,256]{2,1,0:T(8,128)(2,1)S(1)}, bf16[4,256,256]{2,1,0:T(8,128)(2,1)}, u32[]{:S(2)}, u32[]{:S(2)}) collective-permute-start(bf16[4,256,256]{2,1,0:T(8,128)(2,1)S(1)} %all-to-all-done.k_own), channel_id=1, source_target_pairs={{0,8},{1,9},{2,10},{3,11},{4,12},{5,13},{6,14},{7,15},{8,16},{9,17... | collective-permute-start | bytes 1572872 | tf_op jit(solution)/shard_map/ppermute | solution.py:197
  29.4 0.1 collective-permute-start.8
  29.5 3.5 %collective-permute-done.3.v_own = bf16[4,256,256]{2,1,0:T(8,128)(2,1)S(1)} collective-permute-done((bf16[4,256,256]{2,1,0:T(8,128)(2,1)S(1)}, bf16[4,256,256]{2,1,0:T(8,128)(2,1)S(1)}, u32[]{:S(2)}, u32[]{:S(2)}) %collective-permute-start.3) | collective-permute-done | bytes 524320 | tf_op jit(solution)/shard_map/ppermute | solution.py:197
  33.0 0.8 copy-done.1
  33.8 4.7 %all-to-all-start.1 = ((bf16[4,528,256]{2,1,0:T(8,128)(2,1)}), bf16[4,528,256]{2,1,0:T(8,128)(2,1)S(1)}, u32[]{:S(2)}, u32[]{:S(2)}) async-start(bf16[4,528,256]{2,1,0:T(8,128)(2,1)} %rotate_q.1), calls=%async_computation.1 | async-start | bytes 2162688 | tf_op jit(solution)/shard_map/all_to_all | solution.py:194
  38.6 0.0 collective-permute-start.7
  38.6 5.6 %collective-permute-start.9 = (bf16[4,256,256]{2,1,0:T(8,128)(2,1)}, bf16[4,256,256]{2,1,0:T(8,128)(2,1)}, u32[]{:S(2)}, u32[]{:S(2)}) collective-permute-start(bf16[4,256,256]{2,1,0:T(8,128)(2,1)} %copy-done.1), channel_id=1, source_target_pairs={{0,8},{1,9},{2,10},{3,11},{4,12},{5,13},{6,14},{7,15},{8,16},{9,17... | collective-permute-start | bytes 1572872 | tf_op jit(solution)/shard_map/ppermute | solution.py:197
  44.2 0.3 collective-permute-start.6
  44.5 0.3 collective-permute-start.5
  44.8 0.0 collective-permute-done.8.v_oth
  44.8 3.2 %collective-permute-start.10 = (bf16[4,256,256]{2,1,0:T(8,128)(2,1)}, bf16[4,256,256]{2,1,0:T(8,128)(2,1)}, u32[]{:S(2)}, u32[]{:S(2)}) collective-permute-start(bf16[4,256,256]{2,1,0:T(8,128)(2,1)} %collective-permute-done.4.k_own), channel_id=1, source_target_pairs={{0,8},{1,9},{2,10},{3,11},{4,12},{5,13},{6,14},{7,15},{8,16},{9,17... | collective-permute-start | bytes 1572872 | tf_op jit(solution)/shard_map/ppermute | solution.py:197
  48.0 1.6 %collective-permute-start.11 = (f32[1,2048]{1,0:T(1,128)S(1)}, f32[1,2048]{1,0:T(1,128)S(1)}, u32[]{:S(2)}, u32[]{:S(2)}) collective-permute-start(f32[1,2048]{1,0:T(1,128)S(1)} %copy-done.4), channel_id=1, source_target_pairs={{0,64},{64,128},{128,192},{192,0},{1,65},{65,129},{129,193},{193,1... | collective-permute-start | bytes 24584 | tf_op jit(solution)/shard_map/ppermute | solution.py:203
  49.6 0.6 all-to-all-done.1.q_ref
  50.2 6.2 %attend_0.1 = (f32[4,512,256]{2,1,0:T(8,128)S(1)}, f32[4,512,128]{2,1,0:T(8,128)S(1)}) custom-call(bf16[4,528,256]{2,1,0:T(8,128)(2,1)S(1)} %all-to-all-done.1.q_ref, bf16[4,256,256]{2,1,0:T(8,128)(2,1)S(1)} %all-to-all-done.k_own, bf16[4,256,256]{2,1,0:T(8,128)(2,1)} %collective-permute-done.7.k_oth, bf16[4,256,256]{2,1,0:T(8,128)(2,1)S(1)} %order_v.1.v_own, ...), custom_call_target="tpu_custom_call" | custom-call | flops 536870912 | bytes 65536 | tf_op jit(solution)/shard_map/attend_0/pallas_call | solution.py:153
  56.4 0.3 collective-permute-done.9.v_own
  56.7 3.0 %collective-permute-start.12 = (f32[1,2048]{1,0:T(1,128)S(1)}, f32[1,2048]{1,0:T(1,128)S(1)}, u32[]{:S(2)}, u32[]{:S(2)}) collective-permute-start(f32[1,2048]{1,0:T(1,128)S(1)} %copy-done.4), channel_id=1, source_target_pairs={{0,128},{64,192},{128,0},{192,64},{1,129},{65,193},{129,1},{193,65... | collective-permute-start | bytes 24584 | tf_op jit(solution)/shard_map/ppermute | solution.py:203
  59.7 1.1 collective-permute-start.13
  60.9 0.0 collective-permute-done.5.k_oth
  60.9 7.7 %attend_1.1 = (f32[4,512,256]{2,1,0:T(8,128)S(1)}, f32[4,512,128]{2,1,0:T(8,128)S(1)}) custom-call(bf16[4,528,256]{2,1,0:T(8,128)(2,1)S(1)} %all-to-all-done.1.q_ref, bf16[4,256,256]{2,1,0:T(8,128)(2,1)} %collective-permute-done.4.k_own, bf16[4,256,256]{2,1,0:T(8,128)(2,1)} %collective-permute-done.5.k_oth, ...), custom_call_target="tpu_custom_call", output_to_operand_aliasing={{0}: (5, {}), {1}: (6, {})} | custom-call | flops 858993472 | bytes 65536 | tf_op jit(solution)/shard_map/attend_1/pallas_call | solution.py:153
  68.5 0.0 collective-permute-done.11.g1_ref
  68.6 0.0 collective-permute-done.12.g2_ref
  68.6 0.0 collective-permute-done.10.k_own
  68.6 0.1 collective-permute-start.14
  68.7 0.5 collective-permute-start.15
  69.2 1.6 %collective-permute-done.14.k_oth = bf16[4,256,256]{2,1,0:T(8,128)(2,1)S(1)} collective-permute-done((bf16[4,256,256]{2,1,0:T(8,128)(2,1)}, bf16[4,256,256]{2,1,0:T(8,128)(2,1)S(1)}, u32[]{:S(2)}, u32[]{:S(2)}) %collective-permute-start.14) | collective-permute-done | bytes 524320 | tf_op jit(solution)/shard_map/ppermute | solution.py:200
  70.8 0.7 collective-permute-done.15.v_oth
  71.5 5.6 %attend_2.1 = bf16[4,4,64,512]{3,2,1,0:T(8,128)(2,1)S(1)} custom-call(bf16[4,528,256]{2,1,0:T(8,128)(2,1)S(1)} %all-to-all-done.1.q_ref, bf16[4,256,256]{2,1,0:T(8,128)(2,1)} %collective-permute-done.10.k_own, bf16[4,256,256]{2,1,0:T(8,128)(2,1)S(1)} %collective-permute-done.14.k_oth, bf16[4,256,256]{2,1,0:T(8,128)(2,1)} %collective-permute-done.9.v_own, ...), custom_call_target="tpu_custom_call" | custom-call | flops 536870912 | bytes 65536 | tf_op jit(solution)/shard_map/attend_2/pallas_call | solution.py:153
  77.2 23.4 %all_to_all.20.got_ref = bf16[16,64,512]{2,1,0:T(8,128)(2,1)S(1)} all-to-all(bf16[16,64,512]{2,1,0:T(8,128)(2,1)S(1)} %bitcast.5), channel_id=1, replica_groups={{0,2,4,6,64,66,68,70,128,130,132,134,192,194,196,198},{1,3,5,7,65,67,69..., dimensions={0} | all-to-all | bytes 2097152 | tf_op jit(solution)/shard_map/all_to_all | solution.py:254
  100.6 0.5 combine.1
  101.1 16.4 %all_to_all.21 = bf16[4,64,2048]{2,1,0:T(8,128)(2,1)S(1)} all-to-all(bf16[4,64,2048]{2,1,0:T(8,128)(2,1)S(1)} %combine.1), channel_id=1, replica_groups=mesh['section'=4,'seq'=64] {'section'}, dimensions={0} | all-to-all | bytes 2097152 | tf_op jit(solution)/shard_map/all_to_all | solution.py:266
  117.5 1.0 copy.12
  (18 shorter events, 0.1 us)
Async XLA Ops:
  0.0 47.9 %copy-start = (bf16[256,2048]{1,0:T(8,128)(2,1)S(1)}, bf16[256,2048]{1,0:T(8,128)(2,1)}, u32[]{:S(2)}) copy-start(bf16[256,2048]{1,0:T(8,128)(2,1)} %param.11) | copy-start | bytes 3145732
  2.0 13.5 %copy-start.3 = (bf16[256,256]{1,0:T(8,128)(2,1)S(1)}, bf16[256,256]{1,0:T(8,128)(2,1)}, u32[]{:S(2)}) copy-start(bf16[256,256]{1,0:T(8,128)(2,1)} %get-tuple-element.28.v0_ref) | copy-start | bytes 393220
  2.0 13.5 %collective-permute-start = (bf16[256,256]{1,0:T(8,128)(2,1)}, bf16[256,256]{1,0:T(8,128)(2,1)S(1)}, u32[]{:S(2)}, u32[]{:S(2)}) collective-permute-start(bf16[256,256]{1,0:T(8,128)(2,1)} %get-tuple-element.29), channel_id=1, source_target_pairs={{0,2},{1,3},{2,4},{3,5},{4,6},{5,7},{6,0},{7,1},{8,10},{9,11},{10,... | collective-permute-start | bytes 393224 | tf_op jit(solution)/shard_map/ppermute | solution.py:214
  3.6 11.9 %collective-permute-start.1 = (bf16[256,256]{1,0:T(8,128)(2,1)}, bf16[256,256]{1,0:T(8,128)(2,1)S(1)}, u32[]{:S(2)}, u32[]{:S(2)}) collective-permute-start(bf16[256,256]{1,0:T(8,128)(2,1)} %get-tuple-element.30), channel_id=1, source_target_pairs={{0,4},{1,5},{2,6},{3,7},{4,0},{5,1},{6,2},{7,3},{8,12},{9,13},{10,... | collective-permute-start | bytes 393224 | tf_op jit(solution)/shard_map/ppermute | solution.py:214
  6.5 9.0 %collective-permute-start.2 = (bf16[256,256]{1,0:T(8,128)(2,1)}, bf16[256,256]{1,0:T(8,128)(2,1)S(1)}, u32[]{:S(2)}, u32[]{:S(2)}) collective-permute-start(bf16[256,256]{1,0:T(8,128)(2,1)} %get-tuple-element.31), channel_id=1, source_target_pairs={{0,6},{1,7},{2,0},{3,1},{4,2},{5,3},{6,4},{7,5},{8,14},{9,15},{10,... | collective-permute-start | bytes 393224 | tf_op jit(solution)/shard_map/ppermute | solution.py:214
  12.0 12.4 %all-to-all-start = ((bf16[4,256,256]{2,1,0:T(8,128)(2,1)}), bf16[4,256,256]{2,1,0:T(8,128)(2,1)S(1)}, u32[]{:S(2)}, u32[]{:S(2)}) async-start(bf16[4,256,256]{2,1,0:T(8,128)(2,1)} %rotate_k.1), calls=%async_computation | async-start | bytes 1048576 | tf_op jit(solution)/shard_map/all_to_all | solution.py:194
  15.6 17.4 %collective-permute-start.3 = (bf16[4,256,256]{2,1,0:T(8,128)(2,1)S(1)}, bf16[4,256,256]{2,1,0:T(8,128)(2,1)S(1)}, u32[]{:S(2)}, u32[]{:S(2)}) collective-permute-start(bf16[4,256,256]{2,1,0:T(8,128)(2,1)S(1)} %order_v.1.v_own), channel_id=1, source_target_pairs={{0,8},{1,9},{2,10},{3,11},{4,12},{5,13},{6,14},{7,15},{8,16},{9,17... | collective-permute-start | bytes 1572872 | tf_op jit(solution)/shard_map/ppermute | solution.py:197
  21.4 26.5 %copy-start.4 = (f32[1,2048]{1,0:T(1,128)S(1)}, f32[1,2048]{1,0:T(1,128)}, u32[]{:S(2)}) copy-start(f32[1,2048]{1,0:T(1,128)} %g0_ref) | copy-start | bytes 24580
  24.4 20.1 %collective-permute-start.4 = (bf16[4,256,256]{2,1,0:T(8,128)(2,1)S(1)}, bf16[4,256,256]{2,1,0:T(8,128)(2,1)}, u32[]{:S(2)}, u32[]{:S(2)}) collective-permute-start(bf16[4,256,256]{2,1,0:T(8,128)(2,1)S(1)} %all-to-all-done.k_own), channel_id=1, source_target_pairs={{0,8},{1,9},{2,10},{3,11},{4,12},{5,13},{6,14},{7,15},{8,16},{9,17... | collective-permute-start | bytes 1572872 | tf_op jit(solution)/shard_map/ppermute | solution.py:197
  29.4 15.3 %collective-permute-start.8 = (bf16[4,256,256]{2,1,0:T(8,128)(2,1)S(1)}, bf16[4,256,256]{2,1,0:T(8,128)(2,1)}, u32[]{:S(2)}, u32[]{:S(2)}) collective-permute-start(bf16[4,256,256]{2,1,0:T(8,128)(2,1)S(1)} %order_v.1.v_own), channel_id=1, source_target_pairs={{0,1},{1,0},{2,3},{3,2},{4,5},{5,4},{6,7},{7,6},{8,9},{9,8},{10,11... | collective-permute-start | bytes 1572872 | tf_op jit(solution)/shard_map/ppermute | solution.py:200
  33.0 0.8 copy-start.1
  33.8 16.4 %all-to-all-start.1 = ((bf16[4,528,256]{2,1,0:T(8,128)(2,1)}), bf16[4,528,256]{2,1,0:T(8,128)(2,1)S(1)}, u32[]{:S(2)}, u32[]{:S(2)}) async-start(bf16[4,528,256]{2,1,0:T(8,128)(2,1)} %rotate_q.1), calls=%async_computation.1 | async-start | bytes 2162688 | tf_op jit(solution)/shard_map/all_to_all | solution.py:194
  38.6 9.4 %collective-permute-start.7 = (bf16[4,256,256]{2,1,0:T(8,128)(2,1)S(1)}, bf16[4,256,256]{2,1,0:T(8,128)(2,1)}, u32[]{:S(2)}, u32[]{:S(2)}) collective-permute-start(bf16[4,256,256]{2,1,0:T(8,128)(2,1)S(1)} %all-to-all-done.k_own), channel_id=1, source_target_pairs={{0,1},{1,0},{2,3},{3,2},{4,5},{5,4},{6,7},{7,6},{8,9},{9,8},{10,11... | collective-permute-start | bytes 1572872 | tf_op jit(solution)/shard_map/ppermute | solution.py:200
  38.6 18.1 %collective-permute-start.9 = (bf16[4,256,256]{2,1,0:T(8,128)(2,1)}, bf16[4,256,256]{2,1,0:T(8,128)(2,1)}, u32[]{:S(2)}, u32[]{:S(2)}) collective-permute-start(bf16[4,256,256]{2,1,0:T(8,128)(2,1)} %copy-done.1), channel_id=1, source_target_pairs={{0,8},{1,9},{2,10},{3,11},{4,12},{5,13},{6,14},{7,15},{8,16},{9,17... | collective-permute-start | bytes 1572872 | tf_op jit(solution)/shard_map/ppermute | solution.py:197
  44.2 15.6 %collective-permute-start.6 = (bf16[4,256,256]{2,1,0:T(8,128)(2,1)}, bf16[4,256,256]{2,1,0:T(8,128)(2,1)}, u32[]{:S(2)}, u32[]{:S(2)}) collective-permute-start(bf16[4,256,256]{2,1,0:T(8,128)(2,1)} %copy-done.1), channel_id=1, source_target_pairs={{0,1},{1,0},{2,3},{3,2},{4,5},{5,4},{6,7},{7,6},{8,9},{9,8},{10,11... | collective-permute-start | bytes 1572872 | tf_op jit(solution)/shard_map/ppermute | solution.py:200
  44.5 16.4 %collective-permute-start.5 = (bf16[4,256,256]{2,1,0:T(8,128)(2,1)}, bf16[4,256,256]{2,1,0:T(8,128)(2,1)}, u32[]{:S(2)}, u32[]{:S(2)}) collective-permute-start(bf16[4,256,256]{2,1,0:T(8,128)(2,1)} %collective-permute-done.4.k_own), channel_id=1, source_target_pairs={{0,1},{1,0},{2,3},{3,2},{4,5},{5,4},{6,7},{7,6},{8,9},{9,8},{10,11... | collective-permute-start | bytes 1572872 | tf_op jit(solution)/shard_map/ppermute | solution.py:200
  44.8 23.8 %collective-permute-start.10 = (bf16[4,256,256]{2,1,0:T(8,128)(2,1)}, bf16[4,256,256]{2,1,0:T(8,128)(2,1)}, u32[]{:S(2)}, u32[]{:S(2)}) collective-permute-start(bf16[4,256,256]{2,1,0:T(8,128)(2,1)} %collective-permute-done.4.k_own), channel_id=1, source_target_pairs={{0,8},{1,9},{2,10},{3,11},{4,12},{5,13},{6,14},{7,15},{8,16},{9,17... | collective-permute-start | bytes 1572872 | tf_op jit(solution)/shard_map/ppermute | solution.py:197
  48.0 20.5 %collective-permute-start.11 = (f32[1,2048]{1,0:T(1,128)S(1)}, f32[1,2048]{1,0:T(1,128)S(1)}, u32[]{:S(2)}, u32[]{:S(2)}) collective-permute-start(f32[1,2048]{1,0:T(1,128)S(1)} %copy-done.4), channel_id=1, source_target_pairs={{0,64},{64,128},{128,192},{192,0},{1,65},{65,129},{129,193},{193,1... | collective-permute-start | bytes 24584 | tf_op jit(solution)/shard_map/ppermute | solution.py:203
  50.2 10.7 %copy-start.2 = (bf16[4,256,256]{2,1,0:T(8,128)(2,1)S(1)}, bf16[4,256,256]{2,1,0:T(8,128)(2,1)}, u32[]{:S(2)}) copy-start(bf16[4,256,256]{2,1,0:T(8,128)(2,1)} %copy-done.1) | copy-start | bytes 1572868
  56.7 11.9 %collective-permute-start.12 = (f32[1,2048]{1,0:T(1,128)S(1)}, f32[1,2048]{1,0:T(1,128)S(1)}, u32[]{:S(2)}, u32[]{:S(2)}) collective-permute-start(f32[1,2048]{1,0:T(1,128)S(1)} %copy-done.4), channel_id=1, source_target_pairs={{0,128},{64,192},{128,0},{192,64},{1,129},{65,193},{129,1},{193,65... | collective-permute-start | bytes 24584 | tf_op jit(solution)/shard_map/ppermute | solution.py:203
  59.7 8.8 %collective-permute-start.13 = (f32[1,2048]{1,0:T(1,128)S(1)}, f32[1,2048]{1,0:T(1,128)S(1)}, u32[]{:S(2)}, u32[]{:S(2)}) collective-permute-start(f32[1,2048]{1,0:T(1,128)S(1)} %copy-done.4), channel_id=1, source_target_pairs={{0,192},{64,0},{128,64},{192,128},{1,193},{65,1},{129,65},{193,129... | collective-permute-start | bytes 24584 | tf_op jit(solution)/shard_map/ppermute | solution.py:203
  68.6 2.2 %collective-permute-start.14 = (bf16[4,256,256]{2,1,0:T(8,128)(2,1)}, bf16[4,256,256]{2,1,0:T(8,128)(2,1)S(1)}, u32[]{:S(2)}, u32[]{:S(2)}) collective-permute-start(bf16[4,256,256]{2,1,0:T(8,128)(2,1)} %collective-permute-done.10.k_own), channel_id=1, source_target_pairs={{0,1},{1,0},{2,3},{3,2},{4,5},{5,4},{6,7},{7,6},{8,9},{9,8},{10,11... | collective-permute-start | bytes 1572872 | tf_op jit(solution)/shard_map/ppermute | solution.py:200
  68.7 2.9 %collective-permute-start.15 = (bf16[4,256,256]{2,1,0:T(8,128)(2,1)}, bf16[4,256,256]{2,1,0:T(8,128)(2,1)S(1)}, u32[]{:S(2)}, u32[]{:S(2)}) collective-permute-start(bf16[4,256,256]{2,1,0:T(8,128)(2,1)} %collective-permute-done.9.v_own), channel_id=1, source_target_pairs={{0,1},{1,0},{2,3},{3,2},{4,5},{5,4},{6,7},{7,6},{8,9},{9,8},{10,11... | collective-permute-start | bytes 1572872 | tf_op jit(solution)/shard_map/ppermute | solution.py:200

commit v7 on v6

--- a/solution.py
+++ b/solution.py
@@ -72,98 +72,86 @@
         qm_ref[h, 2 * ROWS :] = place_ref[...]
 
 
-def attend_kernel(back, q_ref, k_own, k_oth, v_own, v_oth, *refs):
-    if back == 0:
-        num, den = refs
-    elif back == 1:
-        num_in, den_in, num, den = refs
+def attend_kernel(last, q_ref, *refs):
+    if last:
+        planes = ((2, refs[:4]),)
+        num_in, den_in, out_ref = refs[4:]
     else:
-        num_in, den_in, out_ref = refs
+        planes = ((1, refs[4:8]), (0, refs[:4]))
+        num, den = refs[8:]
     device = lax.axis_index("seq")
     plane0 = device // 8 * PLANE
     core = lax.rem(device, 2)
-    keys0 = plane0 - back * PLANE
     for r in range(4):
-        begin, end = {0: (0, r + 1), 1: (0, 4), 2: (r, 4)}[back]
-        count = (end - begin) * ROWS
         query = q_ref[r, : 2 * ROWS]
         split = q_ref[r, 2 * ROWS :].astype(jnp.float32)
         place = (split[0:1] * 128.0 + split[1:2]).astype(jnp.int32)
         token = plane0 + r * 512 + core * ROWS + lax.broadcasted_iota(jnp.int32, (1, ROWS), 1)
-        low = token - jnp.minimum(place, WINDOW - 1)
-        low = jnp.transpose(jnp.broadcast_to(low, (HALF, ROWS)))
-        low = jnp.concatenate([low, low], axis=0)
-        low = jnp.concatenate([low] * (count // HALF), axis=1)
-        col = lax.broadcasted_iota(jnp.int32, (1, count), 1)
-        spread = col + lax.shift_right_logical(col, 8) * ROWS + begin * 512 + keys0
+        first = token - jnp.minimum(place, WINDOW - 1)
+        first = jnp.transpose(jnp.broadcast_to(first, (HALF, ROWS)))
+        first = jnp.concatenate([first, first], axis=0)
         total, added = None, None
-        for k_ref, v_ref, side in ((k_own, v_own, core), (k_oth, v_oth, 1 - core)):
-            score = lax.dot_general(
-                query,
-                k_ref[begin:end].reshape(count, HD),
-                (((1,), (1,)), ((), ())),
-                preferred_element_type=jnp.float32,
-            )
-            weight = jnp.exp2(jnp.tanh(score * (1.0 / 800.0)) * CAP)
-            key = spread + side * ROWS
-            ok = key >= low
-            if back == 0:
-                row = lax.broadcasted_iota(jnp.int32, (2 * ROWS, 1), 0) & (ROWS - 1)
-                ok = ok & (key <= plane0 + r * 512 + core * ROWS + row)
-            weight = jnp.where(ok, weight, 0.0)
-            lanes = sum(weight[:, i * HALF : (i + 1) * HALF] for i in range(count // HALF))
-            part = jnp.dot(
-                weight.astype(jnp.bfloat16),
-                v_ref[begin:end].reshape(count, HD),
-                preferred_element_type=jnp.float32,
-            )
-            total = lanes if total is None else total + lanes
-            added = part if added is None else added + part
-        if back == 0:
-            num[r] = added
-            den[r] = total
-        elif back == 1:
-            num[r] = num_in[r] + added
-            den[r] = den_in[r] + total
-        else:
+        for back, (k_own, k_oth, v_own, v_oth) in planes:
+            begin, end = {0: (0, r + 1), 1: (0, 4), 2: (r, 4)}[back]
+            count = (end - begin) * ROWS
+            low = jnp.concatenate([first] * (count // HALF), axis=1)
+            col = lax.broadcasted_iota(jnp.int32, (1, count), 1)
+            spread = col + lax.shift_right_logical(col, 8) * ROWS + begin * 512
+            spread = spread + plane0 - back * PLANE
+            for k_ref, v_ref, side in ((k_own, v_own, core), (k_oth, v_oth, 1 - core)):
+                score = lax.dot_general(
+                    query,
+                    k_ref[begin:end].reshape(count, HD),
+                    (((1,), (1,)), ((), ())),
+                    preferred_element_type=jnp.float32,
+                )
+                weight = jnp.exp2(jnp.tanh(score * (1.0 / 800.0)) * CAP)
+                key = spread + side * ROWS
+                ok = key >= low
+                if back == 0:
+                    row = lax.broadcasted_iota(jnp.int32, (2 * ROWS, 1), 0) & (ROWS - 1)
+                    ok = ok & (key <= plane0 + r * 512 + core * ROWS + row)
+                weight = jnp.where(ok, weight, 0.0)
+                lanes = sum(weight[:, i * HALF : (i + 1) * HALF] for i in range(count // HALF))
+                part = jnp.dot(
+                    weight.astype(jnp.bfloat16),
+                    v_ref[begin:end].reshape(count, HD),
+                    preferred_element_type=jnp.float32,
+                )
+                total = lanes if total is None else total + lanes
+                added = part if added is None else added + part
+        if last:
             scale = 1.0 / jnp.sum(den_in[r] + total, axis=-1, keepdims=True)
             whole = ((num_in[r] + added) * scale).astype(jnp.bfloat16)
             for q in range(4):
                 for h in range(2):
-                    first = h * ROWS + q * 64
-                    out_ref[q, r, :, h * HD : (h + 1) * HD] = whole[first : first + 64]
-
-
-def attend(back, query, k_own, k_oth, v_own, v_oth, num, den):
-    args = [query, k_own, k_oth, v_own, v_oth]
-    aliases = {}
+                    top = h * ROWS + q * 64
+                    out_ref[q, r, :, h * HD : (h + 1) * HD] = whole[top : top + 64]
+        else:
+            num[r] = added
+            den[r] = total
+
+
+def attend(last, query, *args):
     outs = [
         jax.ShapeDtypeStruct((4, 512, HD), jnp.float32),
         jax.ShapeDtypeStruct((4, 512, HALF), jnp.float32),
     ]
     out_specs = [vspec(), vspec()]
-    if back:
-        args += [num, den]
-    if back == 1:
-        aliases = {5: 0, 6: 1}
-    if back == 2:
+    if last:
         outs = jax.ShapeDtypeStruct((4, 4, 64, 512), jnp.bfloat16)
         out_specs = vspec()
-    pairs = {0: 20, 1: 32, 2: 20}[back]
     return pl.pallas_call(
-        functools.partial(attend_kernel, back),
+        functools.partial(attend_kernel, last),
         out_shape=outs,
-        in_specs=[vspec()] * len(args),
+        in_specs=[vspec()] * (1 + len(args)),
         out_specs=out_specs,
-        input_output_aliases=aliases,
         compiler_params=pltpu.CompilerParams(vmem_limit_bytes=24 << 20),
         cost_estimate=pl.CostEstimate(
-            flops=int(pairs * 512 * 256 * 256 * 4 * 0.2),
-            bytes_accessed=1 << 16,
-            transcendentals=1,
+            flops=20 * 512 * 256 * 256, bytes_accessed=1 << 16, transcendentals=1
         ),
-        name="attend_%d" % back,
-    )(*args)
+        name="attend_last" if last else "attend_near",
+    )(query, *args)
 
 
 def combine_kernel(got_ref, res_ref, g0_ref, g1_ref, g2_ref, g3_ref, out_ref, gain_ref):
@@ -187,7 +175,8 @@
     angle = positions.astype(jnp.float32)[:, None] * inverse[None, :]
     cosine = jnp.cos(angle)
     sine = jnp.sin(angle)
-    split = jnp.stack([lax.shift_right_logical(positions, 7), positions & 127])
+    later, values = lax.optimization_barrier((positions, values))
+    split = jnp.stack([lax.shift_right_logical(later, 7), later & 127])
     places = jnp.concatenate([split, jnp.zeros((14, ROWS), jnp.int32)]).astype(jnp.bfloat16)
 
     def over_y(x):
@@ -246,11 +235,11 @@
     query = over_y(q_msg)
     v2 = onward(v1)
     k2 = onward(k1)
-    num, den = attend(0, query, k0, other(k0), v0, other(v0), None, None)
-    num, den, v2 = lax.optimization_barrier((num, den, v2))
-    num, den = attend(1, query, k1, other(k1), v1, other(v1), num, den)
+    num, den = attend(
+        False, query, k0, other(k0), v0, other(v0), k1, other(k1), v1, other(v1)
+    )
     num, den, k2, residual, *gains = lax.optimization_barrier((num, den, k2, residual, *gains))
-    sent = attend(2, query, k2, other(k2), v2, other(v2), num, den)
+    sent = attend(True, query, k2, other(k2), v2, other(v2), num, den)
     got = lax.all_to_all(
         sent.reshape(16, 64, 512), ("section", "seq"), 0, 0, axis_index_groups=SHARED_XY
     )

time: 120 us -> 123 us (1.025)
  waiting for transfers between devices: 6.98 us -> 10.4 us
  Pallas kernels: 27 us -> 25.1 us
  starting transfers between devices: 39.9 us -> 41.5 us
    ppermute x4, waiting for transfers between devices: 3.81 us -> 8.47 us  [onward(): return lax.ppermute(x, 'seq', NEXT_PLANE)]
    pallas_call x3 -> x2, Pallas kernels: 19.4 us -> 17.5 us  [attend(): pl.pallas_call(functools.partial(attend_kernel, last), out_shape=outs, in...]
    ppermute x3, starting transfers between devices: 5.73 us -> 7.06 us  [per_device(): lax.ppermute(post_gain, 'section', [(i, (i + r) % 4) for i in range(4)])]
    unnamed x11 -> x13, local copies, waits for them, and re-layouts: 1.78 us -> 2.81 us
  transfers between devices with their start and end apart: 18 -> 18, of which waited for: 6 -> 4; matrix products, arithmetic and copies ran while one was open for 2% -> 2% of each run, Pallas kernels for 16% -> 14%
where the time goes in v7:
time: 123 us; the launch traced here: 122 us
  starting transfers between devices  41.5 us (34%)
  blocking collectives  39 us (32%)
  Pallas kernels  25.1 us (20%)
  waiting for transfers between devices  10.4 us (8%)
  local copies, waits for them, and re-layouts  2.93 us (2%)
  other arithmetic  2.61 us (2%)
    all_to_all x1, blocking collectives, per_device(): lax.all_to_all(sent.reshape(16, 64, 512), ('section', 'seq'), 0, 0, axis_...  22.6 us
    ppermute x4, starting transfers between devices, onward(): return lax.ppermute(x, 'seq', NEXT_PLANE)  18.8 us
    pallas_call x2, Pallas kernels, attend(): pl.pallas_call(functools.partial(attend_kernel, last), out_shape=outs, in...  17.5 us
    all_to_all x1, blocking collectives, per_device(): mine = lax.all_to_all(back, 'section', 0, 0)  16.4 us
    ppermute x4, waiting for transfers between devices, onward(): return lax.ppermute(x, 'seq', NEXT_PLANE)  8.47 us
    all_to_all x2, starting transfers between devices, over_y(): return lax.all_to_all(x, 'seq', 0, 0, axis_index_groups=SHARED_Y)  8.34 us
    ppermute x3, starting transfers between devices, per_device(): lax.ppermute(post_gain, 'section', [(i, (i + r) % 4) for i in range(4)])  7.06 us
    ppermute x3, starting transfers between devices, per_device(): lax.ppermute(pieces[i], 'seq', [(d, d // 8 * 8 + (d + 2 * i) % 8) for d i...  5.83 us
  transfers between devices with their start and end apart: 18, of which 4 were waited for; matrix products, arithmetic and copies ran while one was open for 2% of the time, Pallas kernels for 14%

profile of v7, /device:TPU:96, one launch (start us, length us, event | category | flops | bytes accessed | tf_op | source)
XLA Modules:
  0.0 121.8 jit_solution(638768087229449492)
XLA Ops:
  0.0 2.0 %split_v.1 = (bf16[256,256]{1,0:T(8,128)(2,1)}, bf16[256,256]{1,0:T(8,128)(2,1)}, bf16[256,256]{1,0:T(8,128)(2,1)}, bf16[256,256]{1,0:T(8,128)(2,1)}) custom-call(bf16[256,1024]{1,0:T(8,128)(2,1)} %bitcast.8), custom_call_target="tpu_custom_call" | custom-call | tf_op jit(solution)/shard_map/split_v/pallas_call | solution.py:195
  2.0 1.6 %collective-permute-start = (bf16[256,256]{1,0:T(8,128)(2,1)}, bf16[256,256]{1,0:T(8,128)(2,1)S(1)}, u32[]{:S(2)}, u32[]{:S(2)}) collective-permute-start(bf16[256,256]{1,0:T(8,128)(2,1)} %get-tuple-element.27), channel_id=1, source_target_pairs={{0,2},{1,3},{2,4},{3,5},{4,6},{5,7},{6,0},{7,1},{8,10},{9,11},{10,... | collective-permute-start | bytes 393224 | tf_op jit(solution)/shard_map/ppermute | solution.py:203
  3.6 2.9 %collective-permute-start.1 = (bf16[256,256]{1,0:T(8,128)(2,1)}, bf16[256,256]{1,0:T(8,128)(2,1)S(1)}, u32[]{:S(2)}, u32[]{:S(2)}) collective-permute-start(bf16[256,256]{1,0:T(8,128)(2,1)} %get-tuple-element.28), channel_id=1, source_target_pairs={{0,4},{1,5},{2,6},{3,7},{4,0},{5,1},{6,2},{7,3},{8,12},{9,13},{10,... | collective-permute-start | bytes 393224 | tf_op jit(solution)/shard_map/ppermute | solution.py:203
  6.5 1.3 %collective-permute-start.2 = (bf16[256,256]{1,0:T(8,128)(2,1)}, bf16[256,256]{1,0:T(8,128)(2,1)S(1)}, u32[]{:S(2)}, u32[]{:S(2)}) collective-permute-start(bf16[256,256]{1,0:T(8,128)(2,1)} %get-tuple-element.29), channel_id=1, source_target_pairs={{0,6},{1,7},{2,0},{3,1},{4,2},{5,3},{6,4},{7,5},{8,14},{9,15},{10,... | collective-permute-start | bytes 393224 | tf_op jit(solution)/shard_map/ppermute | solution.py:203
  7.8 0.7 convert_element_type.11
  8.5 1.2 %multiply_sine_fusion = (f32[256,128]{1,0:T(8,128)}, f32[256,128]{1,0:T(8,128)}) fusion(f32[128]{0:T(128)S(1)} %multiply_exponential_fusion, f32[256]{0:T(256)S(1)} %convert_element_type.11), kind=kLoop, calls=%fused_computation | loop fusion | flops 32768 | bytes 263680 | tf_op jit(solution)/shard_map/sin | solution.py:177
  9.8 2.2 %rotate_k.1 = bf16[4,256,256]{2,1,0:T(8,128)(2,1)} custom-call(f32[256,128]{1,0:T(8,128)} %get-tuple-element.46.cos_ref, f32[256,128]{1,0:T(8,128)} %get-tuple-element.45.sin_ref, bf16[256,1024]{1,0:T(8,128)(2,1)} %bitcast.9), custom_call_target="tpu_custom_call" | custom-call | tf_op jit(solution)/shard_map/rotate_k/pallas_call | solution.py:214
  12.0 3.6 %all-to-all-start = ((bf16[4,256,256]{2,1,0:T(8,128)(2,1)}), bf16[4,256,256]{2,1,0:T(8,128)(2,1)S(1)}, u32[]{:S(2)}, u32[]{:S(2)}) async-start(bf16[4,256,256]{2,1,0:T(8,128)(2,1)} %rotate_k.1), calls=%async_computation | async-start | bytes 1048576 | tf_op jit(solution)/shard_map/all_to_all | solution.py:183
  15.6 0.0 collective-permute-done.v1_ref
  15.6 0.0 collective-permute-done.1.v2_ref
  15.6 0.0 collective-permute-done.2.v3_ref
  15.6 0.1 order_v.1.refs_2_
  15.7 5.0 %collective-permute-start.3 = (bf16[4,256,256]{2,1,0:T(8,128)(2,1)S(1)}, bf16[4,256,256]{2,1,0:T(8,128)(2,1)S(1)}, u32[]{:S(2)}, u32[]{:S(2)}) collective-permute-start(bf16[4,256,256]{2,1,0:T(8,128)(2,1)S(1)} %order_v.1.refs_2_), channel_id=1, source_target_pairs={{0,8},{1,9},{2,10},{3,11},{4,12},{5,13},{6,14},{7,15},{8,16},{9,17... | collective-permute-start | bytes 1572872 | tf_op jit(solution)/shard_map/ppermute | solution.py:186
  20.8 0.1 pad.2.clone
  20.9 0.7 maximum_maximum_fusion.place_ref
  21.6 2.8 %rotate_q.1 = bf16[4,528,256]{2,1,0:T(8,128)(2,1)} custom-call(f32[256,128]{1,0:T(8,128)} %get-tuple-element.46.cos_ref, f32[256,128]{1,0:T(8,128)} %get-tuple-element.45.sin_ref, bf16[16,256]{1,0:T(8,128)(2,1)} %maximum_maximum_fusion.place_ref, bf16[256,2048]{1,0:T(8,128)(2,1)} %bitcast.7), custom_call_target="tpu_custom_call" | custom-call | tf_op jit(solution)/shard_map/rotate_q/pallas_call | solution.py:221
  24.4 0.1 all-to-all-done.refs_0_
  24.5 5.0 %collective-permute-start.6 = (bf16[4,256,256]{2,1,0:T(8,128)(2,1)S(1)}, bf16[4,256,256]{2,1,0:T(8,128)(2,1)}, u32[]{:S(2)}, u32[]{:S(2)}) collective-permute-start(bf16[4,256,256]{2,1,0:T(8,128)(2,1)S(1)} %all-to-all-done.refs_0_), channel_id=1, source_target_pairs={{0,8},{1,9},{2,10},{3,11},{4,12},{5,13},{6,14},{7,15},{8,16},{9,17... | collective-permute-start | bytes 1572872 | tf_op jit(solution)/shard_map/ppermute | solution.py:186
  29.5 0.1 collective-permute-start.5
  29.6 3.5 %collective-permute-done.3.refs_6_ = bf16[4,256,256]{2,1,0:T(8,128)(2,1)S(1)} collective-permute-done((bf16[4,256,256]{2,1,0:T(8,128)(2,1)S(1)}, bf16[4,256,256]{2,1,0:T(8,128)(2,1)S(1)}, u32[]{:S(2)}, u32[]{:S(2)}) %collective-permute-start.3) | collective-permute-done | bytes 524320 | tf_op jit(solution)/shard_map/ppermute | solution.py:186
  33.1 0.8 copy-done.1
  33.9 4.7 %all-to-all-start.1 = ((bf16[4,528,256]{2,1,0:T(8,128)(2,1)}), bf16[4,528,256]{2,1,0:T(8,128)(2,1)S(1)}, u32[]{:S(2)}, u32[]{:S(2)}) async-start(bf16[4,528,256]{2,1,0:T(8,128)(2,1)} %rotate_q.1), calls=%async_computation.1 | async-start | bytes 2162688 | tf_op jit(solution)/shard_map/all_to_all | solution.py:183
  38.6 0.0 collective-permute-start.4
  38.7 0.5 collective-permute-start.8
  39.2 5.6 %collective-permute-start.14 = (bf16[4,256,256]{2,1,0:T(8,128)(2,1)}, bf16[4,256,256]{2,1,0:T(8,128)(2,1)}, u32[]{:S(2)}, u32[]{:S(2)}) collective-permute-start(bf16[4,256,256]{2,1,0:T(8,128)(2,1)} %copy-done.1), channel_id=1, source_target_pairs={{0,8},{1,9},{2,10},{3,11},{4,12},{5,13},{6,14},{7,15},{8,16},{9,17... | collective-permute-start | bytes 1572872 | tf_op jit(solution)/shard_map/ppermute | solution.py:186
  44.8 0.1 collective-permute-start.7
  44.9 3.1 %collective-permute-start.9 = (bf16[4,256,256]{2,1,0:T(8,128)(2,1)}, bf16[4,256,256]{2,1,0:T(8,128)(2,1)}, u32[]{:S(2)}, u32[]{:S(2)}) collective-permute-start(bf16[4,256,256]{2,1,0:T(8,128)(2,1)} %collective-permute-done.6.refs_4_), channel_id=1, source_target_pairs={{0,8},{1,9},{2,10},{3,11},{4,12},{5,13},{6,14},{7,15},{8,16},{9,17... | collective-permute-start | bytes 1572872 | tf_op jit(solution)/shard_map/ppermute | solution.py:186
  48.1 0.0 collective-permute-done.4.refs_1_
  48.1 1.6 %collective-permute-start.10 = (f32[1,2048]{1,0:T(1,128)S(1)}, f32[1,2048]{1,0:T(1,128)S(1)}, u32[]{:S(2)}, u32[]{:S(2)}) collective-permute-start(f32[1,2048]{1,0:T(1,128)S(1)} %copy-done.4), channel_id=1, source_target_pairs={{0,64},{64,128},{128,192},{192,0},{1,65},{65,129},{129,193},{193,1... | collective-permute-start | bytes 24584 | tf_op jit(solution)/shard_map/ppermute | solution.py:192
  49.7 2.7 %collective-permute-start.11 = (f32[1,2048]{1,0:T(1,128)S(1)}, f32[1,2048]{1,0:T(1,128)S(1)}, u32[]{:S(2)}, u32[]{:S(2)}) collective-permute-start(f32[1,2048]{1,0:T(1,128)S(1)} %copy-done.4), channel_id=1, source_target_pairs={{0,128},{64,192},{128,0},{192,64},{1,129},{65,193},{129,1},{193,65... | collective-permute-start | bytes 24584 | tf_op jit(solution)/shard_map/ppermute | solution.py:192
  52.4 5.0 %collective-permute-done.14.refs_2_ = bf16[4,256,256]{2,1,0:T(8,128)(2,1)} collective-permute-done((bf16[4,256,256]{2,1,0:T(8,128)(2,1)}, bf16[4,256,256]{2,1,0:T(8,128)(2,1)}, u32[]{:S(2)}, u32[]{:S(2)}) %collective-permute-start.14) | collective-permute-done | bytes 524320 | tf_op jit(solution)/shard_map/ppermute | solution.py:186
  57.4 2.8 %collective-permute-start.12 = (f32[1,2048]{1,0:T(1,128)S(1)}, f32[1,2048]{1,0:T(1,128)S(1)}, u32[]{:S(2)}, u32[]{:S(2)}) collective-permute-start(f32[1,2048]{1,0:T(1,128)S(1)} %copy-done.4), channel_id=1, source_target_pairs={{0,192},{64,0},{128,64},{192,128},{1,193},{65,1},{129,65},{193,129... | collective-permute-start | bytes 24584 | tf_op jit(solution)/shard_map/ppermute | solution.py:192
  60.1 0.0 collective-permute-done.7.refs_5_
  60.1 0.0 collective-permute-start.15
  60.1 0.0 all-to-all-done.1.q_ref
  60.1 0.0 copy-start.2
  60.1 1.0 copy-done.2
  61.2 11.8 %attend_near.1 = (f32[4,512,256]{2,1,0:T(8,128)S(1)}, f32[4,512,128]{2,1,0:T(8,128)S(1)}) custom-call(bf16[4,528,256]{2,1,0:T(8,128)(2,1)S(1)} %all-to-all-done.1.q_ref, bf16[4,256,256]{2,1,0:T(8,128)(2,1)S(1)} %all-to-all-done.refs_0_, bf16[4,256,256]{2,1,0:T(8,128)(2,1)} %collective-permute-done.4.refs_1_, bf16[4,256,256]{2,1,0:T(8,128)(2,1)S(1)} %order_v.1.refs_2_, ...), custom_call_target="tpu_custom_call" | custom-call | flops 671088640 | bytes 65536 | tf_op jit(solution)/shard_map/attend_near/pallas_call | solution.py:144
  73.0 0.0 collective-permute-done.10.g1_ref
  73.0 0.0 collective-permute-done.11.g2_ref
  73.0 0.0 collective-permute-done.9.refs_0_
  73.0 0.8 collective-permute-start.13
  73.9 1.7 %collective-permute-done.13.refs_1_ = bf16[4,256,256]{2,1,0:T(8,128)(2,1)S(1)} collective-permute-done((bf16[4,256,256]{2,1,0:T(8,128)(2,1)}, bf16[4,256,256]{2,1,0:T(8,128)(2,1)S(1)}, u32[]{:S(2)}, u32[]{:S(2)}) %collective-permute-start.13) | collective-permute-done | bytes 524320 | tf_op jit(solution)/shard_map/ppermute | solution.py:189
  75.6 5.7 %attend_last.1 = bf16[4,4,64,512]{3,2,1,0:T(8,128)(2,1)S(1)} custom-call(bf16[4,528,256]{2,1,0:T(8,128)(2,1)S(1)} %all-to-all-done.1.q_ref, bf16[4,256,256]{2,1,0:T(8,128)(2,1)} %collective-permute-done.9.refs_0_, bf16[4,256,256]{2,1,0:T(8,128)(2,1)S(1)} %collective-permute-done.13.refs_1_, bf16[4,256,256]{2,1,0:T(8,128)(2,1)} %collective-permute-done.14.refs_2_, ...), custom_call_target="tpu_custom_call" | custom-call | flops 671088640 | bytes 65536 | tf_op jit(solution)/shard_map/attend_last/pallas_call | solution.py:144
  81.3 22.6 %all_to_all.20.got_ref = bf16[16,64,512]{2,1,0:T(8,128)(2,1)S(1)} all-to-all(bf16[16,64,512]{2,1,0:T(8,128)(2,1)S(1)} %bitcast.5), channel_id=1, replica_groups={{0,2,4,6,64,66,68,70,128,130,132,134,192,194,196,198},{1,3,5,7,65,67,69..., dimensions={0} | all-to-all | bytes 2097152 | tf_op jit(solution)/shard_map/all_to_all | solution.py:243
  103.9 0.5 combine.1
  104.5 16.4 %all_to_all.21 = bf16[4,64,2048]{2,1,0:T(8,128)(2,1)S(1)} all-to-all(bf16[4,64,2048]{2,1,0:T(8,128)(2,1)S(1)} %combine.1), channel_id=1, replica_groups=mesh['section'=4,'seq'=64] {'section'}, dimensions={0} | all-to-all | bytes 2097152 | tf_op jit(solution)/shard_map/all_to_all | solution.py:255
  120.8 1.0 copy.8
  (20 shorter events, 0.1 us)
Async XLA Ops:
  0.0 48.0 %copy-start = (bf16[256,2048]{1,0:T(8,128)(2,1)S(1)}, bf16[256,2048]{1,0:T(8,128)(2,1)}, u32[]{:S(2)}) copy-start(bf16[256,2048]{1,0:T(8,128)(2,1)} %param.11) | copy-start | bytes 3145732
  2.0 13.6 %collective-permute-start = (bf16[256,256]{1,0:T(8,128)(2,1)}, bf16[256,256]{1,0:T(8,128)(2,1)S(1)}, u32[]{:S(2)}, u32[]{:S(2)}) collective-permute-start(bf16[256,256]{1,0:T(8,128)(2,1)} %get-tuple-element.27), channel_id=1, source_target_pairs={{0,2},{1,3},{2,4},{3,5},{4,6},{5,7},{6,0},{7,1},{8,10},{9,11},{10,... | collective-permute-start | bytes 393224 | tf_op jit(solution)/shard_map/ppermute | solution.py:203
  3.6 12.0 %collective-permute-start.1 = (bf16[256,256]{1,0:T(8,128)(2,1)}, bf16[256,256]{1,0:T(8,128)(2,1)S(1)}, u32[]{:S(2)}, u32[]{:S(2)}) collective-permute-start(bf16[256,256]{1,0:T(8,128)(2,1)} %get-tuple-element.28), channel_id=1, source_target_pairs={{0,4},{1,5},{2,6},{3,7},{4,0},{5,1},{6,2},{7,3},{8,12},{9,13},{10,... | collective-permute-start | bytes 393224 | tf_op jit(solution)/shard_map/ppermute | solution.py:203
  6.5 9.1 %collective-permute-start.2 = (bf16[256,256]{1,0:T(8,128)(2,1)}, bf16[256,256]{1,0:T(8,128)(2,1)S(1)}, u32[]{:S(2)}, u32[]{:S(2)}) collective-permute-start(bf16[256,256]{1,0:T(8,128)(2,1)} %get-tuple-element.29), channel_id=1, source_target_pairs={{0,6},{1,7},{2,0},{3,1},{4,2},{5,3},{6,4},{7,5},{8,14},{9,15},{10,... | collective-permute-start | bytes 393224 | tf_op jit(solution)/shard_map/ppermute | solution.py:203
  9.8 5.9 %copy-start.3 = (bf16[256,256]{1,0:T(8,128)(2,1)S(1)}, bf16[256,256]{1,0:T(8,128)(2,1)}, u32[]{:S(2)}) copy-start(bf16[256,256]{1,0:T(8,128)(2,1)} %get-tuple-element.26.v0_ref) | copy-start | bytes 393220
  12.0 8.8 %copy-start.5 = (s32[256]{0:T(256)S(1)}, s32[256]{0:T(256)}, u32[]{:S(2)}) copy-start(s32[256]{0:T(256)} %param.10) | copy-start | bytes 3076
  12.0 12.5 %all-to-all-start = ((bf16[4,256,256]{2,1,0:T(8,128)(2,1)}), bf16[4,256,256]{2,1,0:T(8,128)(2,1)S(1)}, u32[]{:S(2)}, u32[]{:S(2)}) async-start(bf16[4,256,256]{2,1,0:T(8,128)(2,1)} %rotate_k.1), calls=%async_computation | async-start | bytes 1048576 | tf_op jit(solution)/shard_map/all_to_all | solution.py:183
  15.7 17.4 %collective-permute-start.3 = (bf16[4,256,256]{2,1,0:T(8,128)(2,1)S(1)}, bf16[4,256,256]{2,1,0:T(8,128)(2,1)S(1)}, u32[]{:S(2)}, u32[]{:S(2)}) collective-permute-start(bf16[4,256,256]{2,1,0:T(8,128)(2,1)S(1)} %order_v.1.refs_2_), channel_id=1, source_target_pairs={{0,8},{1,9},{2,10},{3,11},{4,12},{5,13},{6,14},{7,15},{8,16},{9,17... | collective-permute-start | bytes 1572872 | tf_op jit(solution)/shard_map/ppermute | solution.py:186
  24.4 23.7 %copy-start.4 = (f32[1,2048]{1,0:T(1,128)S(1)}, f32[1,2048]{1,0:T(1,128)}, u32[]{:S(2)}) copy-start(f32[1,2048]{1,0:T(1,128)} %g0_ref) | copy-start | bytes 24580
  24.5 20.3 %collective-permute-start.6 = (bf16[4,256,256]{2,1,0:T(8,128)(2,1)S(1)}, bf16[4,256,256]{2,1,0:T(8,128)(2,1)}, u32[]{:S(2)}, u32[]{:S(2)}) collective-permute-start(bf16[4,256,256]{2,1,0:T(8,128)(2,1)S(1)} %all-to-all-done.refs_0_), channel_id=1, source_target_pairs={{0,8},{1,9},{2,10},{3,11},{4,12},{5,13},{6,14},{7,15},{8,16},{9,17... | collective-permute-start | bytes 1572872 | tf_op jit(solution)/shard_map/ppermute | solution.py:186
  29.5 15.4 %collective-permute-start.5 = (bf16[4,256,256]{2,1,0:T(8,128)(2,1)S(1)}, bf16[4,256,256]{2,1,0:T(8,128)(2,1)}, u32[]{:S(2)}, u32[]{:S(2)}) collective-permute-start(bf16[4,256,256]{2,1,0:T(8,128)(2,1)S(1)} %order_v.1.refs_2_), channel_id=1, source_target_pairs={{0,1},{1,0},{2,3},{3,2},{4,5},{5,4},{6,7},{7,6},{8,9},{9,8},{10,11... | collective-permute-start | bytes 1572872 | tf_op jit(solution)/shard_map/ppermute | solution.py:189
  33.1 0.8 copy-start.1
  33.9 26.2 %all-to-all-start.1 = ((bf16[4,528,256]{2,1,0:T(8,128)(2,1)}), bf16[4,528,256]{2,1,0:T(8,128)(2,1)S(1)}, u32[]{:S(2)}, u32[]{:S(2)}) async-start(bf16[4,528,256]{2,1,0:T(8,128)(2,1)} %rotate_q.1), calls=%async_computation.1 | async-start | bytes 2162688 | tf_op jit(solution)/shard_map/all_to_all | solution.py:183
  38.6 9.4 %collective-permute-start.4 = (bf16[4,256,256]{2,1,0:T(8,128)(2,1)S(1)}, bf16[4,256,256]{2,1,0:T(8,128)(2,1)}, u32[]{:S(2)}, u32[]{:S(2)}) collective-permute-start(bf16[4,256,256]{2,1,0:T(8,128)(2,1)S(1)} %all-to-all-done.refs_0_), channel_id=1, source_target_pairs={{0,1},{1,0},{2,3},{3,2},{4,5},{5,4},{6,7},{7,6},{8,9},{9,8},{10,11... | collective-permute-start | bytes 1572872 | tf_op jit(solution)/shard_map/ppermute | solution.py:189
  38.7 11.0 %collective-permute-start.8 = (bf16[4,256,256]{2,1,0:T(8,128)(2,1)}, bf16[4,256,256]{2,1,0:T(8,128)(2,1)}, u32[]{:S(2)}, u32[]{:S(2)}) collective-permute-start(bf16[4,256,256]{2,1,0:T(8,128)(2,1)} %copy-done.1), channel_id=1, source_target_pairs={{0,1},{1,0},{2,3},{3,2},{4,5},{5,4},{6,7},{7,6},{8,9},{9,8},{10,11... | collective-permute-start | bytes 1572872 | tf_op jit(solution)/shard_map/ppermute | solution.py:189
  39.2 18.2 %collective-permute-start.14 = (bf16[4,256,256]{2,1,0:T(8,128)(2,1)}, bf16[4,256,256]{2,1,0:T(8,128)(2,1)}, u32[]{:S(2)}, u32[]{:S(2)}) collective-permute-start(bf16[4,256,256]{2,1,0:T(8,128)(2,1)} %copy-done.1), channel_id=1, source_target_pairs={{0,8},{1,9},{2,10},{3,11},{4,12},{5,13},{6,14},{7,15},{8,16},{9,17... | collective-permute-start | bytes 1572872 | tf_op jit(solution)/shard_map/ppermute | solution.py:186
  44.8 15.4 %collective-permute-start.7 = (bf16[4,256,256]{2,1,0:T(8,128)(2,1)}, bf16[4,256,256]{2,1,0:T(8,128)(2,1)}, u32[]{:S(2)}, u32[]{:S(2)}) collective-permute-start(bf16[4,256,256]{2,1,0:T(8,128)(2,1)} %collective-permute-done.6.refs_4_), channel_id=1, source_target_pairs={{0,1},{1,0},{2,3},{3,2},{4,5},{5,4},{6,7},{7,6},{8,9},{9,8},{10,11... | collective-permute-start | bytes 1572872 | tf_op jit(solution)/shard_map/ppermute | solution.py:189
  44.9 28.2 %collective-permute-start.9 = (bf16[4,256,256]{2,1,0:T(8,128)(2,1)}, bf16[4,256,256]{2,1,0:T(8,128)(2,1)}, u32[]{:S(2)}, u32[]{:S(2)}) collective-permute-start(bf16[4,256,256]{2,1,0:T(8,128)(2,1)} %collective-permute-done.6.refs_4_), channel_id=1, source_target_pairs={{0,8},{1,9},{2,10},{3,11},{4,12},{5,13},{6,14},{7,15},{8,16},{9,17... | collective-permute-start | bytes 1572872 | tf_op jit(solution)/shard_map/ppermute | solution.py:186
  48.1 24.9 %collective-permute-start.10 = (f32[1,2048]{1,0:T(1,128)S(1)}, f32[1,2048]{1,0:T(1,128)S(1)}, u32[]{:S(2)}, u32[]{:S(2)}) collective-permute-start(f32[1,2048]{1,0:T(1,128)S(1)} %copy-done.4), channel_id=1, source_target_pairs={{0,64},{64,128},{128,192},{192,0},{1,65},{65,129},{129,193},{193,1... | collective-permute-start | bytes 24584 | tf_op jit(solution)/shard_map/ppermute | solution.py:192
  49.7 23.4 %collective-permute-start.11 = (f32[1,2048]{1,0:T(1,128)S(1)}, f32[1,2048]{1,0:T(1,128)S(1)}, u32[]{:S(2)}, u32[]{:S(2)}) collective-permute-start(f32[1,2048]{1,0:T(1,128)S(1)} %copy-done.4), channel_id=1, source_target_pairs={{0,128},{64,192},{128,0},{192,64},{1,129},{65,193},{129,1},{193,65... | collective-permute-start | bytes 24584 | tf_op jit(solution)/shard_map/ppermute | solution.py:192
  57.4 15.7 %collective-permute-start.12 = (f32[1,2048]{1,0:T(1,128)S(1)}, f32[1,2048]{1,0:T(1,128)S(1)}, u32[]{:S(2)}, u32[]{:S(2)}) collective-permute-start(f32[1,2048]{1,0:T(1,128)S(1)} %copy-done.4), channel_id=1, source_target_pairs={{0,192},{64,0},{128,64},{192,128},{1,193},{65,1},{129,65},{193,129... | collective-permute-start | bytes 24584 | tf_op jit(solution)/shard_map/ppermute | solution.py:192
  60.1 13.7 %collective-permute-start.15 = (bf16[4,256,256]{2,1,0:T(8,128)(2,1)}, bf16[4,256,256]{2,1,0:T(8,128)(2,1)}, u32[]{:S(2)}, u32[]{:S(2)}) collective-permute-start(bf16[4,256,256]{2,1,0:T(8,128)(2,1)} %collective-permute-done.14.refs_2_), channel_id=1, source_target_pairs={{0,1},{1,0},{2,3},{3,2},{4,5},{5,4},{6,7},{7,6},{8,9},{9,8},{10,11... | collective-permute-start | bytes 1572872 | tf_op jit(solution)/shard_map/ppermute | solution.py:189
  60.1 1.0 copy-start.2
  73.0 2.6 %collective-permute-start.13 = (bf16[4,256,256]{2,1,0:T(8,128)(2,1)}, bf16[4,256,256]{2,1,0:T(8,128)(2,1)S(1)}, u32[]{:S(2)}, u32[]{:S(2)}) collective-permute-start(bf16[4,256,256]{2,1,0:T(8,128)(2,1)} %collective-permute-done.9.refs_0_), channel_id=1, source_target_pairs={{0,1},{1,0},{2,3},{3,2},{4,5},{5,4},{6,7},{7,6},{8,9},{9,8},{10,11... | collective-permute-start | bytes 1572872 | tf_op jit(solution)/shard_map/ppermute | solution.py:189

commit v8 on v6

--- a/solution.py
+++ b/solution.py
@@ -72,16 +72,23 @@
         qm_ref[h, 2 * ROWS :] = place_ref[...]
 
 
-def attend_kernel(back, q_ref, k_own, k_oth, v_own, v_oth, *refs):
-    if back == 0:
-        num, den = refs
-    elif back == 1:
-        num_in, den_in, num, den = refs
-    else:
-        num_in, den_in, out_ref = refs
+def attend_kernel(back, part, q_ref, *refs):
     device = lax.axis_index("seq")
     plane0 = device // 8 * PLANE
     core = lax.rem(device, 2)
+    if part == "both":
+        pairs = ((refs[0], refs[2], core), (refs[1], refs[3], 1 - core))
+        refs = refs[4:]
+    else:
+        pairs = ((refs[0], refs[1], core if part == "own" else 1 - core),)
+        refs = refs[2:]
+    last = part == "other"
+    if back == 0:
+        num, den = refs
+    elif last:
+        num_in, den_in, out_ref = refs
+    else:
+        num_in, den_in, num, den = refs
     keys0 = plane0 - back * PLANE
     for r in range(4):
         begin, end = {0: (0, r + 1), 1: (0, 4), 2: (r, 4)}[back]
@@ -97,7 +104,7 @@
         col = lax.broadcasted_iota(jnp.int32, (1, count), 1)
         spread = col + lax.shift_right_logical(col, 8) * ROWS + begin * 512 + keys0
         total, added = None, None
-        for k_ref, v_ref, side in ((k_own, v_own, core), (k_oth, v_oth, 1 - core)):
+        for k_ref, v_ref, side in pairs:
             score = lax.dot_general(
                 query,
                 k_ref[begin:end].reshape(count, HD),
@@ -122,7 +129,7 @@
         if back == 0:
             num[r] = added
             den[r] = total
-        elif back == 1:
+        elif not last:
             num[r] = num_in[r] + added
             den[r] = den_in[r] + total
         else:
@@ -134,26 +141,24 @@
                     out_ref[q, r, :, h * HD : (h + 1) * HD] = whole[first : first + 64]
 
 
-def attend(back, query, k_own, k_oth, v_own, v_oth, num, den):
-    args = [query, k_own, k_oth, v_own, v_oth]
+def attend(back, part, query, *args):
+    last = part == "other"
     aliases = {}
     outs = [
         jax.ShapeDtypeStruct((4, 512, HD), jnp.float32),
         jax.ShapeDtypeStruct((4, 512, HALF), jnp.float32),
     ]
     out_specs = [vspec(), vspec()]
-    if back:
-        args += [num, den]
-    if back == 1:
-        aliases = {5: 0, 6: 1}
-    if back == 2:
+    if back and not last:
+        aliases = {len(args) - 1: 0, len(args): 1}
+    if last:
         outs = jax.ShapeDtypeStruct((4, 4, 64, 512), jnp.bfloat16)
         out_specs = vspec()
-    pairs = {0: 20, 1: 32, 2: 20}[back]
+    pairs = {0: 20, 1: 32, 2: 10}[back]
     return pl.pallas_call(
-        functools.partial(attend_kernel, back),
+        functools.partial(attend_kernel, back, part),
         out_shape=outs,
-        in_specs=[vspec()] * len(args),
+        in_specs=[vspec()] * (1 + len(args)),
         out_specs=out_specs,
         input_output_aliases=aliases,
         compiler_params=pltpu.CompilerParams(vmem_limit_bytes=24 << 20),
@@ -162,8 +167,8 @@
             bytes_accessed=1 << 16,
             transcendentals=1,
         ),
-        name="attend_%d" % back,
-    )(*args)
+        name="attend_%d_%s" % (back, part),
+    )(query, *args)
 
 
 def combine_kernel(got_ref, res_ref, g0_ref, g1_ref, g2_ref, g3_ref, out_ref, gain_ref):
@@ -246,11 +251,12 @@
     query = over_y(q_msg)
     v2 = onward(v1)
     k2 = onward(k1)
-    num, den = attend(0, query, k0, other(k0), v0, other(v0), None, None)
+    num, den = attend(0, "both", query, k0, other(k0), v0, other(v0))
     num, den, v2 = lax.optimization_barrier((num, den, v2))
-    num, den = attend(1, query, k1, other(k1), v1, other(v1), num, den)
+    num, den = attend(1, "both", query, k1, other(k1), v1, other(v1), num, den)
     num, den, k2, residual, *gains = lax.optimization_barrier((num, den, k2, residual, *gains))
-    sent = attend(2, query, k2, other(k2), v2, other(v2), num, den)
+    num, den = attend(2, "own", query, k2, v2, num, den)
+    sent = attend(2, "other", query, other(k2), other(v2), num, den)
     got = lax.all_to_all(
         sent.reshape(16, 64, 512), ("section", "seq"), 0, 0, axis_index_groups=SHARED_XY
     )

time: 120 us -> 117 us (0.975)
  waiting for transfers between devices: 6.98 us -> 4.62 us
    ppermute x6, waiting for transfers between devices: 2.37 us -> 0.02 us  [other(): return lax.ppermute(x, 'seq', OTHER_CORE)]
    pallas_call x3 -> x4, Pallas kernels: 19.4 us -> 19.9 us  [attend(): pl.pallas_call(functools.partial(attend_kernel, back, part), out_shape=ou...]
  transfers between devices with their start and end apart: 18 -> 18, of which waited for: 6 -> 4; matrix products, arithmetic and copies ran while one was open for 2% -> 2% of each run, Pallas kernels for 16% -> 19%
where the time goes in v8:
time: 117 us; the launch traced here: 116 us
  starting transfers between devices  39.9 us (34%)
  blocking collectives  39.6 us (34%)
  Pallas kernels  27.5 us (24%)
  waiting for transfers between devices  4.62 us (4%)
  other arithmetic  2.68 us (2%)
  local copies, waits for them, and re-layouts  1.89 us (2%)
    all_to_all x1, blocking collectives, per_device(): lax.all_to_all(sent.reshape(16, 64, 512), ('section', 'seq'), 0, 0, axis_...  23 us
    pallas_call x4, Pallas kernels, attend(): pl.pallas_call(functools.partial(attend_kernel, back, part), out_shape=ou...  19.9 us
    ppermute x4, starting transfers between devices, onward(): return lax.ppermute(x, 'seq', NEXT_PLANE)  18.8 us
    all_to_all x1, blocking collectives, per_device(): mine = lax.all_to_all(back, 'section', 0, 0)  16.6 us
    all_to_all x2, starting transfers between devices, over_y(): return lax.all_to_all(x, 'seq', 0, 0, axis_index_groups=SHARED_Y)  8.21 us
    ppermute x3, starting transfers between devices, per_device(): lax.ppermute(pieces[i], 'seq', [(d, d // 8 * 8 + (d + 2 * i) % 8) for d i...  5.83 us
    ppermute x3, starting transfers between devices, per_device(): lax.ppermute(post_gain, 'section', [(i, (i + r) % 4) for i in range(4)])  5.73 us
    ppermute x4, waiting for transfers between devices, onward(): return lax.ppermute(x, 'seq', NEXT_PLANE)  3.81 us
  transfers between devices with their start and end apart: 18, of which 4 were waited for; matrix products, arithmetic and copies ran while one was open for 2% of the time, Pallas kernels for 19%

profile of v8, /device:TPU:96, one launch (start us, length us, event | category | flops | bytes accessed | tf_op | source)
XLA Modules:
  0.0 116.3 jit_solution(2899823335452653495)
XLA Ops:
  0.0 2.0 %split_v.1 = (bf16[256,256]{1,0:T(8,128)(2,1)}, bf16[256,256]{1,0:T(8,128)(2,1)}, bf16[256,256]{1,0:T(8,128)(2,1)}, bf16[256,256]{1,0:T(8,128)(2,1)}) custom-call(bf16[256,1024]{1,0:T(8,128)(2,1)} %bitcast.8), custom_call_target="tpu_custom_call" | custom-call | tf_op jit(solution)/shard_map/split_v/pallas_call | solution.py:211
  2.0 1.6 %collective-permute-start = (bf16[256,256]{1,0:T(8,128)(2,1)}, bf16[256,256]{1,0:T(8,128)(2,1)S(1)}, u32[]{:S(2)}, u32[]{:S(2)}) collective-permute-start(bf16[256,256]{1,0:T(8,128)(2,1)} %get-tuple-element.31), channel_id=1, source_target_pairs={{0,2},{1,3},{2,4},{3,5},{4,6},{5,7},{6,0},{7,1},{8,10},{9,11},{10,... | collective-permute-start | bytes 393224 | tf_op jit(solution)/shard_map/ppermute | solution.py:219
  3.6 2.9 %collective-permute-start.1 = (bf16[256,256]{1,0:T(8,128)(2,1)}, bf16[256,256]{1,0:T(8,128)(2,1)S(1)}, u32[]{:S(2)}, u32[]{:S(2)}) collective-permute-start(bf16[256,256]{1,0:T(8,128)(2,1)} %get-tuple-element.32), channel_id=1, source_target_pairs={{0,4},{1,5},{2,6},{3,7},{4,0},{5,1},{6,2},{7,3},{8,12},{9,13},{10,... | collective-permute-start | bytes 393224 | tf_op jit(solution)/shard_map/ppermute | solution.py:219
  6.5 1.3 %collective-permute-start.2 = (bf16[256,256]{1,0:T(8,128)(2,1)}, bf16[256,256]{1,0:T(8,128)(2,1)S(1)}, u32[]{:S(2)}, u32[]{:S(2)}) collective-permute-start(bf16[256,256]{1,0:T(8,128)(2,1)} %get-tuple-element.33), channel_id=1, source_target_pairs={{0,6},{1,7},{2,0},{3,1},{4,2},{5,3},{6,4},{7,5},{8,14},{9,15},{10,... | collective-permute-start | bytes 393224 | tf_op jit(solution)/shard_map/ppermute | solution.py:219
  7.9 0.8 shift-right-logical_convert_fusion
  8.6 1.2 %multiply_sine_fusion = (f32[256,128]{1,0:T(8,128)}, f32[256,128]{1,0:T(8,128)}) fusion(f32[128]{0:T(128)S(1)} %multiply_exponential_fusion, f32[256]{0:T(256)S(1)} %get-tuple-element.58), kind=kLoop, calls=%fused_computation | loop fusion | flops 32768 | bytes 263680 | tf_op jit(solution)/shard_map/sin | solution.py:194
  9.9 2.2 %rotate_k.1 = bf16[4,256,256]{2,1,0:T(8,128)(2,1)} custom-call(f32[256,128]{1,0:T(8,128)} %get-tuple-element.56.cos_ref, f32[256,128]{1,0:T(8,128)} %get-tuple-element.55.sin_ref, bf16[256,1024]{1,0:T(8,128)(2,1)} %bitcast.9), custom_call_target="tpu_custom_call" | custom-call | tf_op jit(solution)/shard_map/rotate_k/pallas_call | solution.py:230
  12.1 3.5 %all-to-all-start = ((bf16[4,256,256]{2,1,0:T(8,128)(2,1)}), bf16[4,256,256]{2,1,0:T(8,128)(2,1)S(1)}, u32[]{:S(2)}, u32[]{:S(2)}) async-start(bf16[4,256,256]{2,1,0:T(8,128)(2,1)} %rotate_k.1), calls=%async_computation | async-start | bytes 1048576 | tf_op jit(solution)/shard_map/all_to_all | solution.py:199
  15.5 0.0 collective-permute-done.v1_ref
  15.5 0.0 collective-permute-done.1.v2_ref
  15.6 0.0 collective-permute-done.2.v3_ref
  15.6 0.1 order_v.1.refs_2_
  15.6 5.0 %collective-permute-start.3 = (bf16[4,256,256]{2,1,0:T(8,128)(2,1)S(1)}, bf16[4,256,256]{2,1,0:T(8,128)(2,1)S(1)}, u32[]{:S(2)}, u32[]{:S(2)}) collective-permute-start(bf16[4,256,256]{2,1,0:T(8,128)(2,1)S(1)} %order_v.1.refs_2_), channel_id=1, source_target_pairs={{0,8},{1,9},{2,10},{3,11},{4,12},{5,13},{6,14},{7,15},{8,16},{9,17... | collective-permute-start | bytes 1572872 | tf_op jit(solution)/shard_map/ppermute | solution.py:202
  20.7 0.1 pad.2.clone
  20.8 0.7 maximum_maximum_fusion.place_ref
  21.5 2.8 %rotate_q.1 = bf16[4,528,256]{2,1,0:T(8,128)(2,1)} custom-call(f32[256,128]{1,0:T(8,128)} %get-tuple-element.56.cos_ref, f32[256,128]{1,0:T(8,128)} %get-tuple-element.55.sin_ref, bf16[16,256]{1,0:T(8,128)(2,1)} %maximum_maximum_fusion.place_ref, bf16[256,2048]{1,0:T(8,128)(2,1)} %bitcast.7), custom_call_target="tpu_custom_call" | custom-call | tf_op jit(solution)/shard_map/rotate_q/pallas_call | solution.py:237
  24.3 0.1 all-to-all-done.refs_0_
  24.4 5.0 %collective-permute-start.4 = (bf16[4,256,256]{2,1,0:T(8,128)(2,1)S(1)}, bf16[4,256,256]{2,1,0:T(8,128)(2,1)}, u32[]{:S(2)}, u32[]{:S(2)}) collective-permute-start(bf16[4,256,256]{2,1,0:T(8,128)(2,1)S(1)} %all-to-all-done.refs_0_), channel_id=1, source_target_pairs={{0,8},{1,9},{2,10},{3,11},{4,12},{5,13},{6,14},{7,15},{8,16},{9,17... | collective-permute-start | bytes 1572872 | tf_op jit(solution)/shard_map/ppermute | solution.py:202
  29.5 0.1 collective-permute-start.8
  29.6 3.5 %collective-permute-done.3.refs_2_ = bf16[4,256,256]{2,1,0:T(8,128)(2,1)S(1)} collective-permute-done((bf16[4,256,256]{2,1,0:T(8,128)(2,1)S(1)}, bf16[4,256,256]{2,1,0:T(8,128)(2,1)S(1)}, u32[]{:S(2)}, u32[]{:S(2)}) %collective-permute-start.3) | collective-permute-done | bytes 524320 | tf_op jit(solution)/shard_map/ppermute | solution.py:202
  33.0 0.8 copy-done.1
  33.8 4.7 %all-to-all-start.1 = ((bf16[4,528,256]{2,1,0:T(8,128)(2,1)}), bf16[4,528,256]{2,1,0:T(8,128)(2,1)S(1)}, u32[]{:S(2)}, u32[]{:S(2)}) async-start(bf16[4,528,256]{2,1,0:T(8,128)(2,1)} %rotate_q.1), calls=%async_computation.1 | async-start | bytes 2162688 | tf_op jit(solution)/shard_map/all_to_all | solution.py:199
  38.6 0.0 collective-permute-start.7
  38.6 5.6 %collective-permute-start.9 = (bf16[4,256,256]{2,1,0:T(8,128)(2,1)}, bf16[4,256,256]{2,1,0:T(8,128)(2,1)}, u32[]{:S(2)}, u32[]{:S(2)}) collective-permute-start(bf16[4,256,256]{2,1,0:T(8,128)(2,1)} %copy-done.1), channel_id=1, source_target_pairs={{0,8},{1,9},{2,10},{3,11},{4,12},{5,13},{6,14},{7,15},{8,16},{9,17... | collective-permute-start | bytes 1572872 | tf_op jit(solution)/shard_map/ppermute | solution.py:202
  44.2 0.3 collective-permute-start.6
  44.5 0.0 collective-permute-done.4.refs_0_
  44.5 0.3 collective-permute-start.5
  44.8 3.2 %collective-permute-start.10 = (bf16[4,256,256]{2,1,0:T(8,128)(2,1)}, bf16[4,256,256]{2,1,0:T(8,128)(2,1)}, u32[]{:S(2)}, u32[]{:S(2)}) collective-permute-start(bf16[4,256,256]{2,1,0:T(8,128)(2,1)} %collective-permute-done.4.refs_0_), channel_id=1, source_target_pairs={{0,8},{1,9},{2,10},{3,11},{4,12},{5,13},{6,14},{7,15},{8,16},{9,17... | collective-permute-start | bytes 1572872 | tf_op jit(solution)/shard_map/ppermute | solution.py:202
  48.0 0.0 collective-permute-done.7.refs_1_
  48.0 1.6 %collective-permute-start.11 = (f32[1,2048]{1,0:T(1,128)S(1)}, f32[1,2048]{1,0:T(1,128)S(1)}, u32[]{:S(2)}, u32[]{:S(2)}) collective-permute-start(f32[1,2048]{1,0:T(1,128)S(1)} %copy-done.4), channel_id=1, source_target_pairs={{0,64},{64,128},{128,192},{192,0},{1,65},{65,129},{129,193},{193,1... | collective-permute-start | bytes 24584 | tf_op jit(solution)/shard_map/ppermute | solution.py:208
  49.6 0.6 all-to-all-done.1.q_ref
  50.2 6.2 %attend_0_both.1 = (f32[4,512,256]{2,1,0:T(8,128)S(1)}, f32[4,512,128]{2,1,0:T(8,128)S(1)}) custom-call(bf16[4,528,256]{2,1,0:T(8,128)(2,1)S(1)} %all-to-all-done.1.q_ref, bf16[4,256,256]{2,1,0:T(8,128)(2,1)S(1)} %all-to-all-done.refs_0_, bf16[4,256,256]{2,1,0:T(8,128)(2,1)} %collective-permute-done.7.refs_1_, bf16[4,256,256]{2,1,0:T(8,128)(2,1)S(1)} %order_v.1.refs_2_, ...), custom_call_target="tpu_custom_call" | custom-call | flops 536870912 | bytes 65536 | tf_op jit(solution)/shard_map/attend_0_both/pallas_call | solution.py:158
  56.4 0.3 collective-permute-done.9.refs_1_
  56.7 3.0 %collective-permute-start.12 = (f32[1,2048]{1,0:T(1,128)S(1)}, f32[1,2048]{1,0:T(1,128)S(1)}, u32[]{:S(2)}, u32[]{:S(2)}) collective-permute-start(f32[1,2048]{1,0:T(1,128)S(1)} %copy-done.4), channel_id=1, source_target_pairs={{0,128},{64,192},{128,0},{192,64},{1,129},{65,193},{129,1},{193,65... | collective-permute-start | bytes 24584 | tf_op jit(solution)/shard_map/ppermute | solution.py:208
  59.7 0.0 collective-permute-done.6.refs_3_
  59.7 1.1 collective-permute-start.13
  60.9 7.7 %attend_1_both.1 = (f32[4,512,256]{2,1,0:T(8,128)S(1)}, f32[4,512,128]{2,1,0:T(8,128)S(1)}) custom-call(bf16[4,528,256]{2,1,0:T(8,128)(2,1)S(1)} %all-to-all-done.1.q_ref, bf16[4,256,256]{2,1,0:T(8,128)(2,1)} %collective-permute-done.4.refs_0_, bf16[4,256,256]{2,1,0:T(8,128)(2,1)} %collective-permute-done.5.refs_1_, ...), custom_call_target="tpu_custom_call", output_to_operand_aliasing={{0}: (5, {}), {1}: (6, {})} | custom-call | flops 858993472 | bytes 65536 | tf_op jit(solution)/shard_map/attend_1_both/pallas_call | solution.py:158
  68.7 0.0 collective-permute-done.12.g2_ref
  68.7 0.0 collective-permute-done.13.g3_ref
  68.7 0.1 collective-permute-start.14
  68.8 0.5 collective-permute-start.15
  69.3 3.6 %attend_2_own.1 = (f32[4,512,256]{2,1,0:T(8,128)S(1)}, f32[4,512,128]{2,1,0:T(8,128)S(1)}) custom-call(bf16[4,528,256]{2,1,0:T(8,128)(2,1)S(1)} %all-to-all-done.1.q_ref, bf16[4,256,256]{2,1,0:T(8,128)(2,1)} %collective-permute-done.10.refs_0_, bf16[4,256,256]{2,1,0:T(8,128)(2,1)} %collective-permute-done.9.refs_1_, ...), custom_call_target="tpu_custom_call", output_to_operand_aliasing={{0}: (3, {}), {1}: (4, {})} | custom-call | flops 268435456 | bytes 65536 | tf_op jit(solution)/shard_map/attend_2_own/pallas_call | solution.py:158
  72.9 0.0 collective-permute-done.14.refs_0_
  72.9 2.3 %attend_2_other.1 = bf16[4,4,64,512]{3,2,1,0:T(8,128)(2,1)S(1)} custom-call(bf16[4,528,256]{2,1,0:T(8,128)(2,1)S(1)} %all-to-all-done.1.q_ref, bf16[4,256,256]{2,1,0:T(8,128)(2,1)S(1)} %collective-permute-done.14.refs_0_, bf16[4,256,256]{2,1,0:T(8,128)(2,1)S(1)} %collective-permute-done.15.refs_1_, f32[4,512,256]{2,1,0:T(8,128)S(1)} %get-tuple-element.48.refs_2_, ...), custom_call_target="tpu_custom_call" | custom-call | flops 268435456 | bytes 65536 | tf_op jit(solution)/shard_map/attend_2_other/pallas_call | solution.py:158
  75.3 23.0 %all_to_all.20.got_ref = bf16[16,64,512]{2,1,0:T(8,128)(2,1)S(1)} all-to-all(bf16[16,64,512]{2,1,0:T(8,128)(2,1)S(1)} %bitcast.5), channel_id=1, replica_groups={{0,2,4,6,64,66,68,70,128,130,132,134,192,194,196,198},{1,3,5,7,65,67,69..., dimensions={0} | all-to-all | bytes 2097152 | tf_op jit(solution)/shard_map/all_to_all | solution.py:260
  98.3 0.5 combine.1
  98.8 16.6 %all_to_all.21 = bf16[4,64,2048]{2,1,0:T(8,128)(2,1)S(1)} all-to-all(bf16[4,64,2048]{2,1,0:T(8,128)(2,1)S(1)} %combine.1), channel_id=1, replica_groups=mesh['section'=4,'seq'=64] {'section'}, dimensions={0} | all-to-all | bytes 2097152 | tf_op jit(solution)/shard_map/all_to_all | solution.py:272
  115.4 1.0 copy.16
  (19 shorter events, 0.1 us)
Async XLA Ops:
  0.0 48.0 %copy-start = (bf16[256,2048]{1,0:T(8,128)(2,1)S(1)}, bf16[256,2048]{1,0:T(8,128)(2,1)}, u32[]{:S(2)}) copy-start(bf16[256,2048]{1,0:T(8,128)(2,1)} %param.11) | copy-start | bytes 3145732
  2.0 13.5 %copy-start.3 = (bf16[256,256]{1,0:T(8,128)(2,1)S(1)}, bf16[256,256]{1,0:T(8,128)(2,1)}, u32[]{:S(2)}) copy-start(bf16[256,256]{1,0:T(8,128)(2,1)} %get-tuple-element.30.v0_ref) | copy-start | bytes 393220
  2.0 13.5 %collective-permute-start = (bf16[256,256]{1,0:T(8,128)(2,1)}, bf16[256,256]{1,0:T(8,128)(2,1)S(1)}, u32[]{:S(2)}, u32[]{:S(2)}) collective-permute-start(bf16[256,256]{1,0:T(8,128)(2,1)} %get-tuple-element.31), channel_id=1, source_target_pairs={{0,2},{1,3},{2,4},{3,5},{4,6},{5,7},{6,0},{7,1},{8,10},{9,11},{10,... | collective-permute-start | bytes 393224 | tf_op jit(solution)/shard_map/ppermute | solution.py:219
  3.6 11.9 %collective-permute-start.1 = (bf16[256,256]{1,0:T(8,128)(2,1)}, bf16[256,256]{1,0:T(8,128)(2,1)S(1)}, u32[]{:S(2)}, u32[]{:S(2)}) collective-permute-start(bf16[256,256]{1,0:T(8,128)(2,1)} %get-tuple-element.32), channel_id=1, source_target_pairs={{0,4},{1,5},{2,6},{3,7},{4,0},{5,1},{6,2},{7,3},{8,12},{9,13},{10,... | collective-permute-start | bytes 393224 | tf_op jit(solution)/shard_map/ppermute | solution.py:219
  6.5 9.0 %collective-permute-start.2 = (bf16[256,256]{1,0:T(8,128)(2,1)}, bf16[256,256]{1,0:T(8,128)(2,1)S(1)}, u32[]{:S(2)}, u32[]{:S(2)}) collective-permute-start(bf16[256,256]{1,0:T(8,128)(2,1)} %get-tuple-element.33), channel_id=1, source_target_pairs={{0,6},{1,7},{2,0},{3,1},{4,2},{5,3},{6,4},{7,5},{8,14},{9,15},{10,... | collective-permute-start | bytes 393224 | tf_op jit(solution)/shard_map/ppermute | solution.py:219
  12.1 12.4 %all-to-all-start = ((bf16[4,256,256]{2,1,0:T(8,128)(2,1)}), bf16[4,256,256]{2,1,0:T(8,128)(2,1)S(1)}, u32[]{:S(2)}, u32[]{:S(2)}) async-start(bf16[4,256,256]{2,1,0:T(8,128)(2,1)} %rotate_k.1), calls=%async_computation | async-start | bytes 1048576 | tf_op jit(solution)/shard_map/all_to_all | solution.py:199
  15.6 17.4 %collective-permute-start.3 = (bf16[4,256,256]{2,1,0:T(8,128)(2,1)S(1)}, bf16[4,256,256]{2,1,0:T(8,128)(2,1)S(1)}, u32[]{:S(2)}, u32[]{:S(2)}) collective-permute-start(bf16[4,256,256]{2,1,0:T(8,128)(2,1)S(1)} %order_v.1.refs_2_), channel_id=1, source_target_pairs={{0,8},{1,9},{2,10},{3,11},{4,12},{5,13},{6,14},{7,15},{8,16},{9,17... | collective-permute-start | bytes 1572872 | tf_op jit(solution)/shard_map/ppermute | solution.py:202
  21.5 26.5 %copy-start.4 = (f32[1,2048]{1,0:T(1,128)S(1)}, f32[1,2048]{1,0:T(1,128)}, u32[]{:S(2)}) copy-start(f32[1,2048]{1,0:T(1,128)} %g0_ref) | copy-start | bytes 24580
  24.4 20.1 %collective-permute-start.4 = (bf16[4,256,256]{2,1,0:T(8,128)(2,1)S(1)}, bf16[4,256,256]{2,1,0:T(8,128)(2,1)}, u32[]{:S(2)}, u32[]{:S(2)}) collective-permute-start(bf16[4,256,256]{2,1,0:T(8,128)(2,1)S(1)} %all-to-all-done.refs_0_), channel_id=1, source_target_pairs={{0,8},{1,9},{2,10},{3,11},{4,12},{5,13},{6,14},{7,15},{8,16},{9,17... | collective-permute-start | bytes 1572872 | tf_op jit(solution)/shard_map/ppermute | solution.py:202
  29.5 15.3 %collective-permute-start.8 = (bf16[4,256,256]{2,1,0:T(8,128)(2,1)S(1)}, bf16[4,256,256]{2,1,0:T(8,128)(2,1)}, u32[]{:S(2)}, u32[]{:S(2)}) collective-permute-start(bf16[4,256,256]{2,1,0:T(8,128)(2,1)S(1)} %order_v.1.refs_2_), channel_id=1, source_target_pairs={{0,1},{1,0},{2,3},{3,2},{4,5},{5,4},{6,7},{7,6},{8,9},{9,8},{10,11... | collective-permute-start | bytes 1572872 | tf_op jit(solution)/shard_map/ppermute | solution.py:205
  33.0 0.8 copy-start.1
  33.8 16.4 %all-to-all-start.1 = ((bf16[4,528,256]{2,1,0:T(8,128)(2,1)}), bf16[4,528,256]{2,1,0:T(8,128)(2,1)S(1)}, u32[]{:S(2)}, u32[]{:S(2)}) async-start(bf16[4,528,256]{2,1,0:T(8,128)(2,1)} %rotate_q.1), calls=%async_computation.1 | async-start | bytes 2162688 | tf_op jit(solution)/shard_map/all_to_all | solution.py:199
  38.6 9.4 %collective-permute-start.7 = (bf16[4,256,256]{2,1,0:T(8,128)(2,1)S(1)}, bf16[4,256,256]{2,1,0:T(8,128)(2,1)}, u32[]{:S(2)}, u32[]{:S(2)}) collective-permute-start(bf16[4,256,256]{2,1,0:T(8,128)(2,1)S(1)} %all-to-all-done.refs_0_), channel_id=1, source_target_pairs={{0,1},{1,0},{2,3},{3,2},{4,5},{5,4},{6,7},{7,6},{8,9},{9,8},{10,11... | collective-permute-start | bytes 1572872 | tf_op jit(solution)/shard_map/ppermute | solution.py:205
  38.6 18.1 %collective-permute-start.9 = (bf16[4,256,256]{2,1,0:T(8,128)(2,1)}, bf16[4,256,256]{2,1,0:T(8,128)(2,1)}, u32[]{:S(2)}, u32[]{:S(2)}) collective-permute-start(bf16[4,256,256]{2,1,0:T(8,128)(2,1)} %copy-done.1), channel_id=1, source_target_pairs={{0,8},{1,9},{2,10},{3,11},{4,12},{5,13},{6,14},{7,15},{8,16},{9,17... | collective-permute-start | bytes 1572872 | tf_op jit(solution)/shard_map/ppermute | solution.py:202
  44.2 15.6 %collective-permute-start.6 = (bf16[4,256,256]{2,1,0:T(8,128)(2,1)}, bf16[4,256,256]{2,1,0:T(8,128)(2,1)}, u32[]{:S(2)}, u32[]{:S(2)}) collective-permute-start(bf16[4,256,256]{2,1,0:T(8,128)(2,1)} %copy-done.1), channel_id=1, source_target_pairs={{0,1},{1,0},{2,3},{3,2},{4,5},{5,4},{6,7},{7,6},{8,9},{9,8},{10,11... | collective-permute-start | bytes 1572872 | tf_op jit(solution)/shard_map/ppermute | solution.py:205
  44.5 16.4 %collective-permute-start.5 = (bf16[4,256,256]{2,1,0:T(8,128)(2,1)}, bf16[4,256,256]{2,1,0:T(8,128)(2,1)}, u32[]{:S(2)}, u32[]{:S(2)}) collective-permute-start(bf16[4,256,256]{2,1,0:T(8,128)(2,1)} %collective-permute-done.4.refs_0_), channel_id=1, source_target_pairs={{0,1},{1,0},{2,3},{3,2},{4,5},{5,4},{6,7},{7,6},{8,9},{9,8},{10,11... | collective-permute-start | bytes 1572872 | tf_op jit(solution)/shard_map/ppermute | solution.py:205
  44.8 23.9 %collective-permute-start.10 = (bf16[4,256,256]{2,1,0:T(8,128)(2,1)}, bf16[4,256,256]{2,1,0:T(8,128)(2,1)}, u32[]{:S(2)}, u32[]{:S(2)}) collective-permute-start(bf16[4,256,256]{2,1,0:T(8,128)(2,1)} %collective-permute-done.4.refs_0_), channel_id=1, source_target_pairs={{0,8},{1,9},{2,10},{3,11},{4,12},{5,13},{6,14},{7,15},{8,16},{9,17... | collective-permute-start | bytes 1572872 | tf_op jit(solution)/shard_map/ppermute | solution.py:202
  48.0 20.6 %collective-permute-start.11 = (f32[1,2048]{1,0:T(1,128)S(1)}, f32[1,2048]{1,0:T(1,128)S(1)}, u32[]{:S(2)}, u32[]{:S(2)}) collective-permute-start(f32[1,2048]{1,0:T(1,128)S(1)} %copy-done.4), channel_id=1, source_target_pairs={{0,64},{64,128},{128,192},{192,0},{1,65},{65,129},{129,193},{193,1... | collective-permute-start | bytes 24584 | tf_op jit(solution)/shard_map/ppermute | solution.py:208
  50.2 10.7 %copy-start.2 = (bf16[4,256,256]{2,1,0:T(8,128)(2,1)S(1)}, bf16[4,256,256]{2,1,0:T(8,128)(2,1)}, u32[]{:S(2)}) copy-start(bf16[4,256,256]{2,1,0:T(8,128)(2,1)} %copy-done.1) | copy-start | bytes 1572868
  56.7 11.9 %collective-permute-start.12 = (f32[1,2048]{1,0:T(1,128)S(1)}, f32[1,2048]{1,0:T(1,128)S(1)}, u32[]{:S(2)}, u32[]{:S(2)}) collective-permute-start(f32[1,2048]{1,0:T(1,128)S(1)} %copy-done.4), channel_id=1, source_target_pairs={{0,128},{64,192},{128,0},{192,64},{1,129},{65,193},{129,1},{193,65... | collective-permute-start | bytes 24584 | tf_op jit(solution)/shard_map/ppermute | solution.py:208
  59.7 8.9 %collective-permute-start.13 = (f32[1,2048]{1,0:T(1,128)S(1)}, f32[1,2048]{1,0:T(1,128)S(1)}, u32[]{:S(2)}, u32[]{:S(2)}) collective-permute-start(f32[1,2048]{1,0:T(1,128)S(1)} %copy-done.4), channel_id=1, source_target_pairs={{0,192},{64,0},{128,64},{192,128},{1,193},{65,1},{129,65},{193,129... | collective-permute-start | bytes 24584 | tf_op jit(solution)/shard_map/ppermute | solution.py:208
  68.7 4.2 %collective-permute-start.14 = (bf16[4,256,256]{2,1,0:T(8,128)(2,1)}, bf16[4,256,256]{2,1,0:T(8,128)(2,1)S(1)}, u32[]{:S(2)}, u32[]{:S(2)}) collective-permute-start(bf16[4,256,256]{2,1,0:T(8,128)(2,1)} %collective-permute-done.10.refs_0_), channel_id=1, source_target_pairs={{0,1},{1,0},{2,3},{3,2},{4,5},{5,4},{6,7},{7,6},{8,9},{9,8},{10,11... | collective-permute-start | bytes 1572872 | tf_op jit(solution)/shard_map/ppermute | solution.py:205
  68.8 4.2 %collective-permute-start.15 = (bf16[4,256,256]{2,1,0:T(8,128)(2,1)}, bf16[4,256,256]{2,1,0:T(8,128)(2,1)S(1)}, u32[]{:S(2)}, u32[]{:S(2)}) collective-permute-start(bf16[4,256,256]{2,1,0:T(8,128)(2,1)} %collective-permute-done.9.refs_1_), channel_id=1, source_target_pairs={{0,1},{1,0},{2,3},{3,2},{4,5},{5,4},{6,7},{7,6},{8,9},{9,8},{10,11... | collective-permute-start | bytes 1572872 | tf_op jit(solution)/shard_map/ppermute | solution.py:205

commit v9 on v8

--- a/solution.py
+++ b/solution.py
@@ -254,7 +254,7 @@
     num, den = attend(0, "both", query, k0, other(k0), v0, other(v0))
     num, den, v2 = lax.optimization_barrier((num, den, v2))
     num, den = attend(1, "both", query, k1, other(k1), v1, other(v1), num, den)
-    num, den, k2, residual, *gains = lax.optimization_barrier((num, den, k2, residual, *gains))
+    num, den, k2, residual = lax.optimization_barrier((num, den, k2, residual))
     num, den = attend(2, "own", query, k2, v2, num, den)
     sent = attend(2, "other", query, other(k2), other(v2), num, den)
     got = lax.all_to_all(

time: 117 us -> 118 us (level)
  blocking collectives: 39.6 us -> 15.3 us
  waiting for transfers between devices: 4.62 us -> 21.6 us
  starting transfers between devices: 39.9 us -> 47.9 us
    all_to_all x1 -> x0, blocking collectives: 23 us -> none  [per_device(): lax.all_to_all(sent.reshape(16, 64, 512), ('section', 'seq'), 0, 0, axis_...]
    ppermute x3, waiting for transfers between devices: 0.01 us -> 9.37 us  [per_device(): lax.ppermute(post_gain, 'section', [(i, (i + r) % 4) for i in range(4)])]
    all_to_all x0 -> x1, starting transfers between devices: none -> 7.49 us  [per_device(): lax.all_to_all(sent.reshape(16, 64, 512), ('section', 'seq'), 0, 0, axis_...]
    ppermute x4, waiting for transfers between devices: 3.81 us -> 7.58 us  [onward(): return lax.ppermute(x, 'seq', NEXT_PLANE)]
    all_to_all x0 -> x1, waiting for transfers between devices: none -> 2.46 us  [per_device(): lax.all_to_all(sent.reshape(16, 64, 512), ('section', 'seq'), 0, 0, axis_...]
    all_to_all x2, waiting for transfers between devices: 0.79 us -> 2.18 us  [over_y(): return lax.all_to_all(x, 'seq', 0, 0, axis_index_groups=SHARED_Y)]
    all_to_all x1, blocking collectives: 16.6 us -> 15.3 us  [per_device(): mine = lax.all_to_all(back, 'section', 0, 0)]
  transfers between devices with their start and end apart: 18 -> 19, of which waited for: 4 -> 8; matrix products, arithmetic and copies ran while one was open for 2% -> 2% of each run, Pallas kernels for 19% -> 19%
where the time goes in v9:
time: 118 us; the launch traced here: 117 us
  starting transfers between devices  47.9 us (41%)
  Pallas kernels  27.5 us (23%)
  waiting for transfers between devices  21.6 us (18%)
  blocking collectives  15.3 us (13%)
  other arithmetic  2.68 us (2%)
  local copies, waits for them, and re-layouts  1.89 us (2%)
    pallas_call x4, Pallas kernels, attend(): pl.pallas_call(functools.partial(attend_kernel, back, part), out_shape=ou...  19.9 us
    ppermute x4, starting transfers between devices, onward(): return lax.ppermute(x, 'seq', NEXT_PLANE)  19 us
    all_to_all x1, blocking collectives, per_device(): mine = lax.all_to_all(back, 'section', 0, 0)  15.3 us
    ppermute x3, waiting for transfers between devices, per_device(): lax.ppermute(post_gain, 'section', [(i, (i + r) % 4) for i in range(4)])  9.37 us
    all_to_all x2, starting transfers between devices, over_y(): return lax.all_to_all(x, 'seq', 0, 0, axis_index_groups=SHARED_Y)  8.21 us
    ppermute x4, waiting for transfers between devices, onward(): return lax.ppermute(x, 'seq', NEXT_PLANE)  7.58 us
    all_to_all x1, starting transfers between devices, per_device(): lax.all_to_all(sent.reshape(16, 64, 512), ('section', 'seq'), 0, 0, axis_...  7.49 us
    ppermute x3, starting transfers between devices, per_device(): lax.ppermute(post_gain, 'section', [(i, (i + r) % 4) for i in range(4)])  6.14 us
  transfers between devices with their start and end apart: 19, of which 8 were waited for; matrix products, arithmetic and copies ran while one was open for 2% of the time, Pallas kernels for 19%

profile of v9, /device:TPU:96, one launch (start us, length us, event | category | flops | bytes accessed | tf_op | source)
XLA Modules:
  0.0 117.0 jit_solution(14261185659890070180)
XLA Ops:
  0.0 2.0 %split_v.1 = (bf16[256,256]{1,0:T(8,128)(2,1)}, bf16[256,256]{1,0:T(8,128)(2,1)}, bf16[256,256]{1,0:T(8,128)(2,1)}, bf16[256,256]{1,0:T(8,128)(2,1)}) custom-call(bf16[256,1024]{1,0:T(8,128)(2,1)} %bitcast.7), custom_call_target="tpu_custom_call" | custom-call | tf_op jit(solution)/shard_map/split_v/pallas_call | solution.py:211
  2.0 1.6 %collective-permute-start = (bf16[256,256]{1,0:T(8,128)(2,1)}, bf16[256,256]{1,0:T(8,128)(2,1)S(1)}, u32[]{:S(2)}, u32[]{:S(2)}) collective-permute-start(bf16[256,256]{1,0:T(8,128)(2,1)} %get-tuple-element.27), channel_id=1, source_target_pairs={{0,2},{1,3},{2,4},{3,5},{4,6},{5,7},{6,0},{7,1},{8,10},{9,11},{10,... | collective-permute-start | bytes 393224 | tf_op jit(solution)/shard_map/ppermute | solution.py:219
  3.6 2.9 %collective-permute-start.1 = (bf16[256,256]{1,0:T(8,128)(2,1)}, bf16[256,256]{1,0:T(8,128)(2,1)S(1)}, u32[]{:S(2)}, u32[]{:S(2)}) collective-permute-start(bf16[256,256]{1,0:T(8,128)(2,1)} %get-tuple-element.28), channel_id=1, source_target_pairs={{0,4},{1,5},{2,6},{3,7},{4,0},{5,1},{6,2},{7,3},{8,12},{9,13},{10,... | collective-permute-start | bytes 393224 | tf_op jit(solution)/shard_map/ppermute | solution.py:219
  6.5 1.3 %collective-permute-start.2 = (bf16[256,256]{1,0:T(8,128)(2,1)}, bf16[256,256]{1,0:T(8,128)(2,1)S(1)}, u32[]{:S(2)}, u32[]{:S(2)}) collective-permute-start(bf16[256,256]{1,0:T(8,128)(2,1)} %get-tuple-element.29), channel_id=1, source_target_pairs={{0,6},{1,7},{2,0},{3,1},{4,2},{5,3},{6,4},{7,5},{8,14},{9,15},{10,... | collective-permute-start | bytes 393224 | tf_op jit(solution)/shard_map/ppermute | solution.py:219
  7.8 0.8 shift-right-logical_convert_fusion
  8.6 1.2 %multiply_sine_fusion = (f32[256,128]{1,0:T(8,128)}, f32[256,128]{1,0:T(8,128)}) fusion(f32[128]{0:T(128)S(1)} %multiply_exponential_fusion, f32[256]{0:T(256)S(1)} %get-tuple-element.50), kind=kLoop, calls=%fused_computation | loop fusion | flops 32768 | bytes 263680 | tf_op jit(solution)/shard_map/sin | solution.py:194
  9.8 2.2 %rotate_k.1 = bf16[4,256,256]{2,1,0:T(8,128)(2,1)} custom-call(f32[256,128]{1,0:T(8,128)} %get-tuple-element.48.cos_ref, f32[256,128]{1,0:T(8,128)} %get-tuple-element.47.sin_ref, bf16[256,1024]{1,0:T(8,128)(2,1)} %bitcast.8), custom_call_target="tpu_custom_call" | custom-call | tf_op jit(solution)/shard_map/rotate_k/pallas_call | solution.py:230
  12.0 3.5 %all-to-all-start = ((bf16[4,256,256]{2,1,0:T(8,128)(2,1)}), bf16[4,256,256]{2,1,0:T(8,128)(2,1)S(1)}, u32[]{:S(2)}, u32[]{:S(2)}) async-start(bf16[4,256,256]{2,1,0:T(8,128)(2,1)} %rotate_k.1), calls=%async_computation | async-start | bytes 1048576 | tf_op jit(solution)/shard_map/all_to_all | solution.py:199
  15.5 0.0 collective-permute-done.v1_ref
  15.5 0.1 order_v.1.refs_2_
  15.6 5.0 %collective-permute-start.3 = (bf16[4,256,256]{2,1,0:T(8,128)(2,1)S(1)}, bf16[4,256,256]{2,1,0:T(8,128)(2,1)S(1)}, u32[]{:S(2)}, u32[]{:S(2)}) collective-permute-start(bf16[4,256,256]{2,1,0:T(8,128)(2,1)S(1)} %order_v.1.refs_2_), channel_id=1, source_target_pairs={{0,8},{1,9},{2,10},{3,11},{4,12},{5,13},{6,14},{7,15},{8,16},{9,17... | collective-permute-start | bytes 1572872 | tf_op jit(solution)/shard_map/ppermute | solution.py:202
  20.7 0.1 pad.2.clone
  20.8 0.7 maximum_maximum_fusion.place_ref
  21.4 2.8 %rotate_q.1 = bf16[4,528,256]{2,1,0:T(8,128)(2,1)} custom-call(f32[256,128]{1,0:T(8,128)} %get-tuple-element.48.cos_ref, f32[256,128]{1,0:T(8,128)} %get-tuple-element.47.sin_ref, bf16[16,256]{1,0:T(8,128)(2,1)} %maximum_maximum_fusion.place_ref, bf16[256,2048]{1,0:T(8,128)(2,1)} %bitcast.6), custom_call_target="tpu_custom_call" | custom-call | tf_op jit(solution)/shard_map/rotate_q/pallas_call | solution.py:237
  24.2 0.1 all-to-all-done.refs_0_
  24.4 5.0 %collective-permute-start.4 = (bf16[4,256,256]{2,1,0:T(8,128)(2,1)S(1)}, bf16[4,256,256]{2,1,0:T(8,128)(2,1)}, u32[]{:S(2)}, u32[]{:S(2)}) collective-permute-start(bf16[4,256,256]{2,1,0:T(8,128)(2,1)S(1)} %all-to-all-done.refs_0_), channel_id=1, source_target_pairs={{0,8},{1,9},{2,10},{3,11},{4,12},{5,13},{6,14},{7,15},{8,16},{9,17... | collective-permute-start | bytes 1572872 | tf_op jit(solution)/shard_map/ppermute | solution.py:202
  29.4 0.1 collective-permute-start.8
  29.5 3.5 %collective-permute-done.3.refs_2_ = bf16[4,256,256]{2,1,0:T(8,128)(2,1)S(1)} collective-permute-done((bf16[4,256,256]{2,1,0:T(8,128)(2,1)S(1)}, bf16[4,256,256]{2,1,0:T(8,128)(2,1)S(1)}, u32[]{:S(2)}, u32[]{:S(2)}) %collective-permute-start.3) | collective-permute-done | bytes 524320 | tf_op jit(solution)/shard_map/ppermute | solution.py:202
  33.0 0.8 copy-done.1
  33.8 4.7 %all-to-all-start.1 = ((bf16[4,528,256]{2,1,0:T(8,128)(2,1)}), bf16[4,528,256]{2,1,0:T(8,128)(2,1)S(1)}, u32[]{:S(2)}, u32[]{:S(2)}) async-start(bf16[4,528,256]{2,1,0:T(8,128)(2,1)} %rotate_q.1), calls=%async_computation.1 | async-start | bytes 2162688 | tf_op jit(solution)/shard_map/all_to_all | solution.py:199
  38.5 0.0 collective-permute-start.7
  38.6 5.6 %collective-permute-start.9 = (bf16[4,256,256]{2,1,0:T(8,128)(2,1)}, bf16[4,256,256]{2,1,0:T(8,128)(2,1)}, u32[]{:S(2)}, u32[]{:S(2)}) collective-permute-start(bf16[4,256,256]{2,1,0:T(8,128)(2,1)} %copy-done.1), channel_id=1, source_target_pairs={{0,8},{1,9},{2,10},{3,11},{4,12},{5,13},{6,14},{7,15},{8,16},{9,17... | collective-permute-start | bytes 1572872 | tf_op jit(solution)/shard_map/ppermute | solution.py:202
  44.1 0.3 collective-permute-start.6
  44.5 0.0 collective-permute-done.4.refs_0_
  44.5 0.3 collective-permute-start.5
  44.8 3.3 %collective-permute-start.10 = (bf16[4,256,256]{2,1,0:T(8,128)(2,1)}, bf16[4,256,256]{2,1,0:T(8,128)(2,1)}, u32[]{:S(2)}, u32[]{:S(2)}) collective-permute-start(bf16[4,256,256]{2,1,0:T(8,128)(2,1)} %collective-permute-done.4.refs_0_), channel_id=1, source_target_pairs={{0,8},{1,9},{2,10},{3,11},{4,12},{5,13},{6,14},{7,15},{8,16},{9,17... | collective-permute-start | bytes 1572872 | tf_op jit(solution)/shard_map/ppermute | solution.py:202
  48.1 0.0 collective-permute-done.7.refs_1_
  48.2 2.0 %all-to-all-done.1.q_ref = bf16[4,528,256]{2,1,0:T(8,128)(2,1)S(1)} async-done(((bf16[4,528,256]{2,1,0:T(8,128)(2,1)}), bf16[4,528,256]{2,1,0:T(8,128)(2,1)S(1)}, u32[]{:S(2)}, u32[]{:S(2)}) %all-to-all-start.1) | async-done | bytes 1081376 | tf_op jit(solution)/shard_map/all_to_all | solution.py:199
  50.2 5.9 %attend_0_both.1 = (f32[4,512,256]{2,1,0:T(8,128)S(1)}, f32[4,512,128]{2,1,0:T(8,128)S(1)}) custom-call(bf16[4,528,256]{2,1,0:T(8,128)(2,1)S(1)} %all-to-all-done.1.q_ref, bf16[4,256,256]{2,1,0:T(8,128)(2,1)S(1)} %all-to-all-done.refs_0_, bf16[4,256,256]{2,1,0:T(8,128)(2,1)} %collective-permute-done.7.refs_1_, bf16[4,256,256]{2,1,0:T(8,128)(2,1)S(1)} %order_v.1.refs_2_, ...), custom_call_target="tpu_custom_call" | custom-call | flops 536870912 | bytes 65536 | tf_op jit(solution)/shard_map/attend_0_both/pallas_call | solution.py:158
  56.1 0.6 collective-permute-done.9.refs_1_
  56.7 0.0 collective-permute-done.6.refs_3_
  56.7 0.0 collective-permute-done.5.refs_1_
  56.7 7.3 %attend_1_both.1 = (f32[4,512,256]{2,1,0:T(8,128)S(1)}, f32[4,512,128]{2,1,0:T(8,128)S(1)}) custom-call(bf16[4,528,256]{2,1,0:T(8,128)(2,1)S(1)} %all-to-all-done.1.q_ref, bf16[4,256,256]{2,1,0:T(8,128)(2,1)} %collective-permute-done.4.refs_0_, bf16[4,256,256]{2,1,0:T(8,128)(2,1)} %collective-permute-done.5.refs_1_, ...), custom_call_target="tpu_custom_call", output_to_operand_aliasing={{0}: (5, {}), {1}: (6, {})} | custom-call | flops 858993472 | bytes 65536 | tf_op jit(solution)/shard_map/attend_1_both/pallas_call | solution.py:158
  64.0 3.5 %collective-permute-done.10.refs_0_ = bf16[4,256,256]{2,1,0:T(8,128)(2,1)} collective-permute-done((bf16[4,256,256]{2,1,0:T(8,128)(2,1)}, bf16[4,256,256]{2,1,0:T(8,128)(2,1)}, u32[]{:S(2)}, u32[]{:S(2)}) %collective-permute-start.10) | collective-permute-done | bytes 524320 | tf_op jit(solution)/shard_map/ppermute | solution.py:202
  67.5 0.0 collective-permute-start.11
  67.5 0.5 collective-permute-start.12
  68.0 3.5 %attend_2_own.1 = (f32[4,512,256]{2,1,0:T(8,128)S(1)}, f32[4,512,128]{2,1,0:T(8,128)S(1)}) custom-call(bf16[4,528,256]{2,1,0:T(8,128)(2,1)S(1)} %all-to-all-done.1.q_ref, bf16[4,256,256]{2,1,0:T(8,128)(2,1)} %collective-permute-done.10.refs_0_, bf16[4,256,256]{2,1,0:T(8,128)(2,1)} %collective-permute-done.9.refs_1_, ...), custom_call_target="tpu_custom_call", output_to_operand_aliasing={{0}: (3, {}), {1}: (4, {})} | custom-call | flops 268435456 | bytes 65536 | tf_op jit(solution)/shard_map/attend_2_own/pallas_call | solution.py:158
  71.6 3.1 %attend_2_other.1 = bf16[4,4,64,512]{3,2,1,0:T(8,128)(2,1)} custom-call(bf16[4,528,256]{2,1,0:T(8,128)(2,1)S(1)} %all-to-all-done.1.q_ref, bf16[4,256,256]{2,1,0:T(8,128)(2,1)S(1)} %collective-permute-done.11.refs_0_, bf16[4,256,256]{2,1,0:T(8,128)(2,1)S(1)} %collective-permute-done.12.refs_1_, f32[4,512,256]{2,1,0:T(8,128)S(1)} %get-tuple-element.44.refs_2_, ...), custom_call_target="tpu_custom_call" | custom-call | flops 268435456 | bytes 65536 | tf_op jit(solution)/shard_map/attend_2_other/pallas_call | solution.py:158
  74.7 7.5 %all-to-all-start.2 = ((bf16[16,64,512]{2,1,0:T(8,128)(2,1)}), bf16[16,64,512]{2,1,0:T(8,128)(2,1)S(1)}, u32[]{:S(2)}, u32[]{:S(2)}) async-start(bf16[16,64,512]{2,1,0:T(8,128)(2,1)} %bitcast.3), calls=%async_computation.2 | async-start | bytes 2097152 | tf_op jit(solution)/shard_map/all_to_all | solution.py:260
  82.3 2.0 %collective-permute-start.13 = (f32[1,2048]{1,0:T(1,128)S(1)}, f32[1,2048]{1,0:T(1,128)S(1)}, u32[]{:S(2)}, u32[]{:S(2)}) collective-permute-start(f32[1,2048]{1,0:T(1,128)S(1)} %copy-done.4), channel_id=1, source_target_pairs={{0,64},{64,128},{128,192},{192,0},{1,65},{65,129},{129,193},{193,1... | collective-permute-start | bytes 24584 | tf_op jit(solution)/shard_map/ppermute | solution.py:208
  84.3 2.7 %collective-permute-start.14 = (f32[1,2048]{1,0:T(1,128)S(1)}, f32[1,2048]{1,0:T(1,128)S(1)}, u32[]{:S(2)}, u32[]{:S(2)}) collective-permute-start(f32[1,2048]{1,0:T(1,128)S(1)} %copy-done.4), channel_id=1, source_target_pairs={{0,128},{64,192},{128,0},{192,64},{1,129},{65,193},{129,1},{193,65... | collective-permute-start | bytes 24584 | tf_op jit(solution)/shard_map/ppermute | solution.py:208
  86.9 1.5 %collective-permute-start.15 = (f32[1,2048]{1,0:T(1,128)S(1)}, f32[1,2048]{1,0:T(1,128)S(1)}, u32[]{:S(2)}, u32[]{:S(2)}) collective-permute-start(f32[1,2048]{1,0:T(1,128)S(1)} %copy-done.4), channel_id=1, source_target_pairs={{0,192},{64,0},{128,64},{192,128},{1,193},{65,1},{129,65},{193,129... | collective-permute-start | bytes 24584 | tf_op jit(solution)/shard_map/ppermute | solution.py:208
  88.4 7.2 %collective-permute-done.13.g1_ref = f32[1,2048]{1,0:T(1,128)S(1)} collective-permute-done((f32[1,2048]{1,0:T(1,128)S(1)}, f32[1,2048]{1,0:T(1,128)S(1)}, u32[]{:S(2)}, u32[]{:S(2)}) %collective-permute-start.13) | collective-permute-done | bytes 8224 | tf_op jit(solution)/shard_map/ppermute | solution.py:208
  95.6 2.1 %collective-permute-done.14.g2_ref = f32[1,2048]{1,0:T(1,128)S(1)} collective-permute-done((f32[1,2048]{1,0:T(1,128)S(1)}, f32[1,2048]{1,0:T(1,128)S(1)}, u32[]{:S(2)}, u32[]{:S(2)}) %collective-permute-start.14) | collective-permute-done | bytes 8224 | tf_op jit(solution)/shard_map/ppermute | solution.py:208
  97.8 2.5 %all-to-all-done.2.got_ref = bf16[16,64,512]{2,1,0:T(8,128)(2,1)S(1)} async-done(((bf16[16,64,512]{2,1,0:T(8,128)(2,1)}), bf16[16,64,512]{2,1,0:T(8,128)(2,1)S(1)}, u32[]{:S(2)}, u32[]{:S(2)}) %all-to-all-start.2) | async-done | bytes 1048608 | tf_op jit(solution)/shard_map/all_to_all | solution.py:260
  100.2 0.5 combine.1
  100.7 15.3 %all_to_all.20 = bf16[4,64,2048]{2,1,0:T(8,128)(2,1)S(1)} all-to-all(bf16[4,64,2048]{2,1,0:T(8,128)(2,1)S(1)} %combine.1), channel_id=1, replica_groups=mesh['section'=4,'seq'=64] {'section'}, dimensions={0} | all-to-all | bytes 2097152 | tf_op jit(solution)/shard_map/all_to_all | solution.py:272
  116.1 1.0 copy.16
  (20 shorter events, 0.1 us)
Async XLA Ops:
  0.0 48.1 %copy-start = (bf16[256,2048]{1,0:T(8,128)(2,1)S(1)}, bf16[256,2048]{1,0:T(8,128)(2,1)}, u32[]{:S(2)}) copy-start(bf16[256,2048]{1,0:T(8,128)(2,1)} %param.11) | copy-start | bytes 3145732
  2.0 13.5 %copy-start.3 = (bf16[256,256]{1,0:T(8,128)(2,1)S(1)}, bf16[256,256]{1,0:T(8,128)(2,1)}, u32[]{:S(2)}) copy-start(bf16[256,256]{1,0:T(8,128)(2,1)} %get-tuple-element.26.v0_ref) | copy-start | bytes 393220
  2.0 13.5 %collective-permute-start = (bf16[256,256]{1,0:T(8,128)(2,1)}, bf16[256,256]{1,0:T(8,128)(2,1)S(1)}, u32[]{:S(2)}, u32[]{:S(2)}) collective-permute-start(bf16[256,256]{1,0:T(8,128)(2,1)} %get-tuple-element.27), channel_id=1, source_target_pairs={{0,2},{1,3},{2,4},{3,5},{4,6},{5,7},{6,0},{7,1},{8,10},{9,11},{10,... | collective-permute-start | bytes 393224 | tf_op jit(solution)/shard_map/ppermute | solution.py:219
  3.6 11.9 %collective-permute-start.1 = (bf16[256,256]{1,0:T(8,128)(2,1)}, bf16[256,256]{1,0:T(8,128)(2,1)S(1)}, u32[]{:S(2)}, u32[]{:S(2)}) collective-permute-start(bf16[256,256]{1,0:T(8,128)(2,1)} %get-tuple-element.28), channel_id=1, source_target_pairs={{0,4},{1,5},{2,6},{3,7},{4,0},{5,1},{6,2},{7,3},{8,12},{9,13},{10,... | collective-permute-start | bytes 393224 | tf_op jit(solution)/shard_map/ppermute | solution.py:219
  6.5 9.0 %collective-permute-start.2 = (bf16[256,256]{1,0:T(8,128)(2,1)}, bf16[256,256]{1,0:T(8,128)(2,1)S(1)}, u32[]{:S(2)}, u32[]{:S(2)}) collective-permute-start(bf16[256,256]{1,0:T(8,128)(2,1)} %get-tuple-element.29), channel_id=1, source_target_pairs={{0,6},{1,7},{2,0},{3,1},{4,2},{5,3},{6,4},{7,5},{8,14},{9,15},{10,... | collective-permute-start | bytes 393224 | tf_op jit(solution)/shard_map/ppermute | solution.py:219
  12.0 12.4 %all-to-all-start = ((bf16[4,256,256]{2,1,0:T(8,128)(2,1)}), bf16[4,256,256]{2,1,0:T(8,128)(2,1)S(1)}, u32[]{:S(2)}, u32[]{:S(2)}) async-start(bf16[4,256,256]{2,1,0:T(8,128)(2,1)} %rotate_k.1), calls=%async_computation | async-start | bytes 1048576 | tf_op jit(solution)/shard_map/all_to_all | solution.py:199
  15.6 17.4 %collective-permute-start.3 = (bf16[4,256,256]{2,1,0:T(8,128)(2,1)S(1)}, bf16[4,256,256]{2,1,0:T(8,128)(2,1)S(1)}, u32[]{:S(2)}, u32[]{:S(2)}) collective-permute-start(bf16[4,256,256]{2,1,0:T(8,128)(2,1)S(1)} %order_v.1.refs_2_), channel_id=1, source_target_pairs={{0,8},{1,9},{2,10},{3,11},{4,12},{5,13},{6,14},{7,15},{8,16},{9,17... | collective-permute-start | bytes 1572872 | tf_op jit(solution)/shard_map/ppermute | solution.py:202
  24.4 20.1 %collective-permute-start.4 = (bf16[4,256,256]{2,1,0:T(8,128)(2,1)S(1)}, bf16[4,256,256]{2,1,0:T(8,128)(2,1)}, u32[]{:S(2)}, u32[]{:S(2)}) collective-permute-start(bf16[4,256,256]{2,1,0:T(8,128)(2,1)S(1)} %all-to-all-done.refs_0_), channel_id=1, source_target_pairs={{0,8},{1,9},{2,10},{3,11},{4,12},{5,13},{6,14},{7,15},{8,16},{9,17... | collective-permute-start | bytes 1572872 | tf_op jit(solution)/shard_map/ppermute | solution.py:202
  29.4 15.3 %collective-permute-start.8 = (bf16[4,256,256]{2,1,0:T(8,128)(2,1)S(1)}, bf16[4,256,256]{2,1,0:T(8,128)(2,1)}, u32[]{:S(2)}, u32[]{:S(2)}) collective-permute-start(bf16[4,256,256]{2,1,0:T(8,128)(2,1)S(1)} %order_v.1.refs_2_), channel_id=1, source_target_pairs={{0,1},{1,0},{2,3},{3,2},{4,5},{5,4},{6,7},{7,6},{8,9},{9,8},{10,11... | collective-permute-start | bytes 1572872 | tf_op jit(solution)/shard_map/ppermute | solution.py:205
  33.0 0.8 copy-start.1
  33.8 16.4 %all-to-all-start.1 = ((bf16[4,528,256]{2,1,0:T(8,128)(2,1)}), bf16[4,528,256]{2,1,0:T(8,128)(2,1)S(1)}, u32[]{:S(2)}, u32[]{:S(2)}) async-start(bf16[4,528,256]{2,1,0:T(8,128)(2,1)} %rotate_q.1), calls=%async_computation.1 | async-start | bytes 2162688 | tf_op jit(solution)/shard_map/all_to_all | solution.py:199
  38.5 9.6 %collective-permute-start.7 = (bf16[4,256,256]{2,1,0:T(8,128)(2,1)S(1)}, bf16[4,256,256]{2,1,0:T(8,128)(2,1)}, u32[]{:S(2)}, u32[]{:S(2)}) collective-permute-start(bf16[4,256,256]{2,1,0:T(8,128)(2,1)S(1)} %all-to-all-done.refs_0_), channel_id=1, source_target_pairs={{0,1},{1,0},{2,3},{3,2},{4,5},{5,4},{6,7},{7,6},{8,9},{9,8},{10,11... | collective-permute-start | bytes 1572872 | tf_op jit(solution)/shard_map/ppermute | solution.py:205
  38.6 18.1 %collective-permute-start.9 = (bf16[4,256,256]{2,1,0:T(8,128)(2,1)}, bf16[4,256,256]{2,1,0:T(8,128)(2,1)}, u32[]{:S(2)}, u32[]{:S(2)}) collective-permute-start(bf16[4,256,256]{2,1,0:T(8,128)(2,1)} %copy-done.1), channel_id=1, source_target_pairs={{0,8},{1,9},{2,10},{3,11},{4,12},{5,13},{6,14},{7,15},{8,16},{9,17... | collective-permute-start | bytes 1572872 | tf_op jit(solution)/shard_map/ppermute | solution.py:202
  44.1 12.5 %collective-permute-start.6 = (bf16[4,256,256]{2,1,0:T(8,128)(2,1)}, bf16[4,256,256]{2,1,0:T(8,128)(2,1)}, u32[]{:S(2)}, u32[]{:S(2)}) collective-permute-start(bf16[4,256,256]{2,1,0:T(8,128)(2,1)} %copy-done.1), channel_id=1, source_target_pairs={{0,1},{1,0},{2,3},{3,2},{4,5},{5,4},{6,7},{7,6},{8,9},{9,8},{10,11... | collective-permute-start | bytes 1572872 | tf_op jit(solution)/shard_map/ppermute | solution.py:205
  44.5 12.2 %collective-permute-start.5 = (bf16[4,256,256]{2,1,0:T(8,128)(2,1)}, bf16[4,256,256]{2,1,0:T(8,128)(2,1)}, u32[]{:S(2)}, u32[]{:S(2)}) collective-permute-start(bf16[4,256,256]{2,1,0:T(8,128)(2,1)} %collective-permute-done.4.refs_0_), channel_id=1, source_target_pairs={{0,1},{1,0},{2,3},{3,2},{4,5},{5,4},{6,7},{7,6},{8,9},{9,8},{10,11... | collective-permute-start | bytes 1572872 | tf_op jit(solution)/shard_map/ppermute | solution.py:205
  44.8 22.8 %collective-permute-start.10 = (bf16[4,256,256]{2,1,0:T(8,128)(2,1)}, bf16[4,256,256]{2,1,0:T(8,128)(2,1)}, u32[]{:S(2)}, u32[]{:S(2)}) collective-permute-start(bf16[4,256,256]{2,1,0:T(8,128)(2,1)} %collective-permute-done.4.refs_0_), channel_id=1, source_target_pairs={{0,8},{1,9},{2,10},{3,11},{4,12},{5,13},{6,14},{7,15},{8,16},{9,17... | collective-permute-start | bytes 1572872 | tf_op jit(solution)/shard_map/ppermute | solution.py:202
  50.2 6.5 %copy-start.2 = (bf16[4,256,256]{2,1,0:T(8,128)(2,1)S(1)}, bf16[4,256,256]{2,1,0:T(8,128)(2,1)}, u32[]{:S(2)}) copy-start(bf16[4,256,256]{2,1,0:T(8,128)(2,1)} %copy-done.1) | copy-start | bytes 1572868
  67.5 4.0 %collective-permute-start.11 = (bf16[4,256,256]{2,1,0:T(8,128)(2,1)}, bf16[4,256,256]{2,1,0:T(8,128)(2,1)S(1)}, u32[]{:S(2)}, u32[]{:S(2)}) collective-permute-start(bf16[4,256,256]{2,1,0:T(8,128)(2,1)} %collective-permute-done.10.refs_0_), channel_id=1, source_target_pairs={{0,1},{1,0},{2,3},{3,2},{4,5},{5,4},{6,7},{7,6},{8,9},{9,8},{10,11... | collective-permute-start | bytes 1572872 | tf_op jit(solution)/shard_map/ppermute | solution.py:205
  67.5 4.1 %collective-permute-start.12 = (bf16[4,256,256]{2,1,0:T(8,128)(2,1)}, bf16[4,256,256]{2,1,0:T(8,128)(2,1)S(1)}, u32[]{:S(2)}, u32[]{:S(2)}) collective-permute-start(bf16[4,256,256]{2,1,0:T(8,128)(2,1)} %collective-permute-done.9.refs_1_), channel_id=1, source_target_pairs={{0,1},{1,0},{2,3},{3,2},{4,5},{5,4},{6,7},{7,6},{8,9},{9,8},{10,11... | collective-permute-start | bytes 1572872 | tf_op jit(solution)/shard_map/ppermute | solution.py:205
  74.7 7.5 %copy-start.4 = (f32[1,2048]{1,0:T(1,128)S(1)}, f32[1,2048]{1,0:T(1,128)}, u32[]{:S(2)}) copy-start(f32[1,2048]{1,0:T(1,128)} %g0_ref.1) | copy-start | bytes 24580
  74.7 25.5 %all-to-all-start.2 = ((bf16[16,64,512]{2,1,0:T(8,128)(2,1)}), bf16[16,64,512]{2,1,0:T(8,128)(2,1)S(1)}, u32[]{:S(2)}, u32[]{:S(2)}) async-start(bf16[16,64,512]{2,1,0:T(8,128)(2,1)} %bitcast.3), calls=%async_computation.2 | async-start | bytes 2097152 | tf_op jit(solution)/shard_map/all_to_all | solution.py:260
  82.3 13.4 %collective-permute-start.13 = (f32[1,2048]{1,0:T(1,128)S(1)}, f32[1,2048]{1,0:T(1,128)S(1)}, u32[]{:S(2)}, u32[]{:S(2)}) collective-permute-start(f32[1,2048]{1,0:T(1,128)S(1)} %copy-done.4), channel_id=1, source_target_pairs={{0,64},{64,128},{128,192},{192,0},{1,65},{65,129},{129,193},{193,1... | collective-permute-start | bytes 24584 | tf_op jit(solution)/shard_map/ppermute | solution.py:208
  84.3 13.5 %collective-permute-start.14 = (f32[1,2048]{1,0:T(1,128)S(1)}, f32[1,2048]{1,0:T(1,128)S(1)}, u32[]{:S(2)}, u32[]{:S(2)}) collective-permute-start(f32[1,2048]{1,0:T(1,128)S(1)} %copy-done.4), channel_id=1, source_target_pairs={{0,128},{64,192},{128,0},{192,64},{1,129},{65,193},{129,1},{193,65... | collective-permute-start | bytes 24584 | tf_op jit(solution)/shard_map/ppermute | solution.py:208
  86.9 10.8 %collective-permute-start.15 = (f32[1,2048]{1,0:T(1,128)S(1)}, f32[1,2048]{1,0:T(1,128)S(1)}, u32[]{:S(2)}, u32[]{:S(2)}) collective-permute-start(f32[1,2048]{1,0:T(1,128)S(1)} %copy-done.4), channel_id=1, source_target_pairs={{0,192},{64,0},{128,64},{192,128},{1,193},{65,1},{129,65},{193,129... | collective-permute-start | bytes 24584 | tf_op jit(solution)/shard_map/ppermute | solution.py:208
